TPU v7x, 32 devices: a whole 2x2x4 slice. The times are simulated.
32 devices in a mesh: gx: 4 (over z), gy: 8 (over y, x, core).
Axes of the slice: x: 2, y: 2, z: 4, core: 2. Of those that a mesh axis runs over, the one named last changes fastest.
Arguments:
- enthalpy: float32 [32, 256, 128], P('gx', 'gy'), may hold values from 0 to 2.5
- porosity: float32 [32, 256, 128], P('gx', 'gy'), may hold values from 0.05 to 0.85
- active: int32 [8, 16], P('gx', 'gy'), may hold values from 0 to 1, as said below
- move_count: int32 [4, 8, 2], P('gx', 'gy'), may hold values from 0 to 2, as said below
- move_slot: int32 [4, 8, 2, 2], P('gx', 'gy'), may hold values from 0 to 3, as said below
Outputs:
- enthalpy_out: float32 [4, 8, 4, 4, 16, 128], P('gx', 'gy')
- porosity_out: float32 [4, 8, 4, 4, 16, 128], P('gx', 'gy')
Inputs may be any that keep to these rules, and one draw needn't show every extreme that they name: Before balancing some devices hold several active tiles; after both rounds each device holds at most 2 active tiles, and some device holds exactly 2. `move_count`: A device and its partner in a round carry the same count; some pair in each round trades 2 tiles. `move_slot`: the 2 entries of a device and round are distinct slots; only the first move_count of them are used.
All inputs are finite; a program needn't handle non-finite values.
Results may differ from a plain program's by a relative error of at most 0.0003.
Values may be sent and summed in bfloat16 or wider, within the bound.
No kernel may reach another device: no remote copies, remote signals or barrier semaphores. Data moves between devices by JAX's collectives and lax.ppermute only.
A program may use at most 64 MiB of HBM per device.

v0:
```python
import jax
import jax.numpy as jnp
from jax import lax
from jax.sharding import PartitionSpec as P

PAIRS = 4


melt_point = 1.0
melt_width = 0.25
latent_heat = 0.4
conduct_base = 0.4
conduct_melt = 0.6
heat_step = 0.15
sinter_point = 0.8
sinter_width = 0.1
shrink_rate = 0.3
merge_step = 0.15


def with_halo(cells, sides, width):
    for axis, dim in sides:
        count = lax.axis_size(axis)
        ends = count - 1
        head = lax.slice_in_dim(cells, 0, width, axis=dim)
        tail = lax.slice_in_dim(cells, cells.shape[dim] - width, cells.shape[dim], axis=dim)
        cells = jnp.concatenate(
            [
                lax.ppermute(tail, axis, [(i, (i + 1) % count) for i in range(ends)]),
                cells,
                lax.ppermute(head, axis, [((i + 1) % count, i) for i in range(ends)]),
            ],
            axis=dim,
        )
    return cells


def swapped(shard, axis, distance):
    return lax.ppermute(shard, axis, [(i, i ^ 1 << distance) for i in range(lax.axis_size(axis))])


def liquid(values):
    return jax.nn.sigmoid((values - melt_point) / melt_width)


def neighbour_sum(values, weights):
    centre = values[:, 1:-1, 1:-1]
    weight = weights[:, 1:-1, 1:-1]
    summed = jnp.zeros_like(centre)
    pairs_list = (
        (values[:, 2:, 1:-1], weights[:, 2:, 1:-1]),
        (values[:, :-2, 1:-1], weights[:, :-2, 1:-1]),
        (values[:, 1:-1, 2:], weights[:, 1:-1, 2:]),
        (values[:, 1:-1, :-2], weights[:, 1:-1, :-2]),
    )
    for beside, beside_weight in pairs_list:
        summed = summed + 0.5 * (weight + beside_weight) * (beside - centre)
    vertical = 0.5 * (weight[..., 1:] + weight[..., :-1]) * (centre[..., 1:] - centre[..., :-1])
    zeros_col = jnp.zeros_like(centre[..., :1])
    return (
        summed
        + jnp.concatenate([vertical, zeros_col], axis=-1)
        - jnp.concatenate([zeros_col, vertical], axis=-1)
    )


def spread(near_flags, span_x, span_y):
    widened = jnp.concatenate(
        [
            jnp.repeat(near_flags[:, :1], 2, axis=1),
            jnp.repeat(near_flags[:, 1:2], span_x, axis=1),
            jnp.repeat(near_flags[:, 2:], 2, axis=1),
        ],
        axis=1,
    )
    return jnp.concatenate(
        [
            jnp.repeat(widened[:, :, :1], 2, axis=2),
            jnp.repeat(widened[:, :, 1:2], span_y, axis=2),
            jnp.repeat(widened[:, :, 2:], 2, axis=2),
        ],
        axis=2,
    )


def advance(own_heat, own_pore, win_heat, win_pore, region):
    warm_copy = win_heat.astype(jnp.float32).at[:, 2:-2, 2:-2].set(own_heat)
    pore_copy = win_pore.astype(jnp.float32).at[:, 2:-2, 2:-2].set(own_pore)
    melted = liquid(warm_copy)
    temper = warm_copy - latent_heat * melted
    conduct = (1.0 - pore_copy) ** 2 * (conduct_base + conduct_melt * melted)
    raised = warm_copy[:, 1:-1, 1:-1] + heat_step * neighbour_sum(temper, conduct)
    heated = jnp.where(region[:, 1:-1, 1:-1, None] > 0, raised, warm_copy[:, 1:-1, 1:-1])
    melt_again = liquid(heated)
    sinter = jax.nn.sigmoid((heated - latent_heat * melt_again - sinter_point) / sinter_width)
    inner_pore = pore_copy[:, 1:-1, 1:-1]
    new_pore = (
        own_pore
        - shrink_rate * sinter[:, 1:-1, 1:-1] * own_pore
        + merge_step * neighbour_sum(inner_pore, sinter)
    )
    return (heated[:, 1:-1, 1:-1], new_pore)


def to_tiles(home_block):
    fields = home_block.shape[0]
    span_x = home_block.shape[1] // 2
    span_y = home_block.shape[2] // 2
    depth = home_block.shape[3]
    parted = home_block.reshape(fields, 2, span_x, 2, span_y, depth).transpose(1, 3, 0, 2, 4, 5)
    return parted.reshape(4, fields, span_x, span_y, depth)


def to_block(tile_state):
    fields = tile_state.shape[1]
    span_x = tile_state.shape[2]
    span_y = tile_state.shape[3]
    depth = tile_state.shape[4]
    parted = tile_state.reshape(2, 2, fields, span_x, span_y, depth).transpose(2, 0, 3, 1, 4, 5)
    return parted.reshape(fields, 2 * span_x, 2 * span_y, depth)


def windows_of(shelled, span_x, span_y):
    return jnp.stack(
        [
            shelled[
                :,
                row_index * span_x : row_index * span_x + span_x + 4,
                col_index * span_y : col_index * span_y + span_y + 4,
            ]
            for row_index in range(2)
            for col_index in range(2)
        ]
    )


def place_moved(arrays, received, count, slot_list):
    result = []
    for member, incoming in zip(arrays, received):
        for position in range(incoming.shape[0]):
            updated = member.at[slot_list[position]].set(incoming[position])
            member = jnp.where(position < count, updated, member)
        result.append(member)
    return tuple(result)


def per_device(enthalpy, porosity, active, move_count, move_slot):
    span_x = enthalpy.shape[0] // 2
    span_y = enthalpy.shape[1] // 2
    swap_bit_x = lax.axis_size("gx").bit_length() - 2
    swap_bit_y = lax.axis_size("gy").bit_length() - 2
    padded_flags = with_halo(active, (("gx", 0), ("gy", 1)), 1)
    near_flags = jnp.stack(
        [
            padded_flags[row_index : row_index + 3, col_index : col_index + 3]
            for row_index in range(2)
            for col_index in range(2)
        ]
    ).astype(jnp.float32)
    count_x = move_count[0, 0, 0]
    count_y = move_count[0, 0, 1]
    slots_x = move_slot[0, 0, 0]
    slots_y = move_slot[0, 0, 1]
    tile_state = to_tiles(jnp.stack([enthalpy, porosity]))
    live_flags = active.reshape(4).astype(jnp.float32)
    region = spread(near_flags, span_x, span_y)
    for pair_index in range(PAIRS):
        rounded = to_block(tile_state).astype(jnp.bfloat16)
        shelled = with_halo(rounded, (("gx", 1), ("gy", 2)), 2)
        windows = windows_of(shelled, span_x, span_y)
        new_heat, new_pore = advance(
            tile_state[:, 0], tile_state[:, 1], windows[:, 0], windows[:, 1], region
        )
        tile_state = jnp.where(
            live_flags[:, None, None, None, None] > 0,
            jnp.stack([new_heat, new_pore], axis=1),
            tile_state,
        )
    received = swapped(tile_state[slots_x], "gx", swap_bit_x)
    tile_state = place_moved((tile_state,), (received,), count_x, slots_x)[0]
    received = swapped(tile_state[slots_y], "gy", swap_bit_y)
    tile_state = place_moved((tile_state,), (received,), count_y, slots_y)[0]
    return (tile_state[None, None, :, 0], tile_state[None, None, :, 1])


def solution(mesh):
    placed = (
        P("gx", "gy", None),
        P("gx", "gy", None),
        P("gx", "gy"),
        P("gx", "gy", None),
        P("gx", "gy", None, None),
    )
    return jax.shard_map(
        per_device,
        mesh=mesh,
        in_specs=placed,
        out_specs=(P("gx", "gy", None, None, None, None), P("gx", "gy", None, None, None, None)),
        check_vma=False,
    )
```

profile of v0, /device:TPU:0, one launch (start us, length us, event | category | flops | bytes accessed | tf_op | source)
XLA Modules:
  0.0 114.4 jit_solution(8214403932657087628)
XLA Ops:
  0.6 0.8 fusion.164
  1.4 4.9 %collective-permute-start = (s32[1,2]{1,0:T(1,128)S(1)}, s32[1,2]{1,0:T(1,128)S(1)}, u32[]{:S(2)}, u32[]{:S(2)}) collective-permute-start(s32[1,2]{1,0:T(1,128)S(1)} %get-tuple-element.242), channel_id=1, source_target_pairs={{0,8},{8,16},{16,24},{1,9},{9,17},{17,25},{2,10},{10,18},{18,26},{... | collective-permute-start | bytes 32 | tf_op jit(solution)/shard_map/ppermute | solution.py:29
  6.3 1.3 %collective-permute-start.1 = (s32[1,2]{1,0:T(1,128)S(1)}, s32[1,2]{1,0:T(1,128)S(1)}, u32[]{:S(2)}, u32[]{:S(2)}) collective-permute-start(s32[1,2]{1,0:T(1,128)S(1)} %get-tuple-element.243), channel_id=1, source_target_pairs={{8,0},{16,8},{24,16},{9,1},{17,9},{25,17},{10,2},{18,10},{26,18},{... | collective-permute-start | bytes 32 | tf_op jit(solution)/shard_map/ppermute | solution.py:31
  7.7 1.0 convert_bitcast_fusion.2
  8.7 4.7 %collective-permute-start.4 = (bf16[2,2,32,128]{3,2,1,0:T(8,128)(2,1)S(1)}, bf16[2,2,32,128]{3,2,1,0:T(8,128)(2,1)S(1)}, u32[]{:S(2)}, u32[]{:S(2)}) collective-permute-start(bf16[2,2,32,128]{3,2,1,0:T(8,128)(2,1)S(1)} %get-tuple-element.220), channel_id=1, source_target_pairs={{0,8},{8,16},{16,24},{1,9},{9,17},{17,25},{2,10},{10,18},{18,26},{... | collective-permute-start | bytes 98312 | tf_op jit(solution)/shard_map/ppermute | solution.py:29
  13.4 1.3 %collective-permute-start.5 = (bf16[2,2,32,128]{3,2,1,0:T(8,128)(2,1)S(1)}, bf16[2,2,32,128]{3,2,1,0:T(8,128)(2,1)S(1)}, u32[]{:S(2)}, u32[]{:S(2)}) collective-permute-start(bf16[2,2,32,128]{3,2,1,0:T(8,128)(2,1)S(1)} %get-tuple-element.221), channel_id=1, source_target_pairs={{8,0},{16,8},{24,16},{9,1},{17,9},{25,17},{10,2},{18,10},{26,18},{... | collective-permute-start | bytes 98312 | tf_op jit(solution)/shard_map/ppermute | solution.py:31
  14.8 0.6 fusion.163
  15.5 0.6 copy-done.4
  16.2 0.6 fusion.165
  16.9 1.3 %collective-permute-start.2 = (s32[4,1]{1,0:T(4,128)S(1)}, s32[4,1]{1,0:T(4,128)S(1)}, u32[]{:S(2)}, u32[]{:S(2)}) collective-permute-start(s32[4,1]{1,0:T(4,128)S(1)} %get-tuple-element.234), channel_id=1, source_target_pairs={{0,1},{1,2},{2,3},{3,4},{4,5},{5,6},{6,7},{8,9},{9,10},{10,11},{11... | collective-permute-start | bytes 56 | tf_op jit(solution)/shard_map/ppermute | solution.py:29
  18.2 1.3 %collective-permute-start.3 = (s32[4,1]{1,0:T(4,128)S(1)}, s32[4,1]{1,0:T(4,128)S(1)}, u32[]{:S(2)}, u32[]{:S(2)}) collective-permute-start(s32[4,1]{1,0:T(4,128)S(1)} %get-tuple-element.235), channel_id=1, source_target_pairs={{1,0},{2,1},{3,2},{4,3},{5,4},{6,5},{7,6},{9,8},{10,9},{11,10},{12... | collective-permute-start | bytes 56 | tf_op jit(solution)/shard_map/ppermute | solution.py:31
  19.5 3.5 %collective-permute-done.3 = s32[4,1]{1,0:T(4,128)S(1)} collective-permute-done((s32[4,1]{1,0:T(4,128)S(1)}, s32[4,1]{1,0:T(4,128)S(1)}, u32[]{:S(2)}, u32[]{:S(2)}) %collective-permute-start.3) | collective-permute-done | bytes 48 | tf_op jit(solution)/shard_map/ppermute | solution.py:31
  23.7 4.2 %collective-permute-start.6 = (bf16[2,12,2,128]{3,2,1,0:T(2,128)(2,1)S(1)}, bf16[2,12,2,128]{3,2,1,0:T(2,128)(2,1)S(1)}, u32[]{:S(2)}, u32[]{:S(2)}) collective-permute-start(bf16[2,12,2,128]{3,2,1,0:T(2,128)(2,1)S(1)} %get-tuple-element.212), channel_id=1, source_target_pairs={{0,1},{1,2},{2,3},{3,4},{4,5},{5,6},{6,7},{8,9},{9,10},{10,11},{11... | collective-permute-start | bytes 36872 | tf_op jit(solution)/shard_map/ppermute | solution.py:29
  28.3 1.3 %collective-permute-start.7 = (bf16[2,12,2,128]{3,2,1,0:T(2,128)(2,1)S(1)}, bf16[2,12,2,128]{3,2,1,0:T(2,128)(2,1)S(1)}, u32[]{:S(2)}, u32[]{:S(2)}) collective-permute-start(bf16[2,12,2,128]{3,2,1,0:T(2,128)(2,1)S(1)} %get-tuple-element.213), channel_id=1, source_target_pairs={{1,0},{2,1},{3,2},{4,3},{5,4},{6,5},{7,6},{9,8},{10,9},{11,10},{12... | collective-permute-start | bytes 36872 | tf_op jit(solution)/shard_map/ppermute | solution.py:31
  29.6 1.7 %collective-permute-done.7 = bf16[2,12,2,128]{3,2,1,0:T(2,128)(2,1)S(1)} collective-permute-done((bf16[2,12,2,128]{3,2,1,0:T(2,128)(2,1)S(1)}, bf16[2,12,2,128]{3,2,1,0:T(2,128)(2,1)S(1)}, u32[]{:S(2)}, u32[]{:S(2)}) %collective-permute-start.7) | collective-permute-done | bytes 12320 | tf_op jit(solution)/shard_map/ppermute | solution.py:31
  31.6 0.2 scatter.29
  31.8 0.2 scatter.26
  32.2 0.2 fusion.48
  32.4 0.6 add_divide_fusion.7
  33.2 0.2 fusion.73
  33.6 4.5 %collective-permute-start.8 = (bf16[2,2,32,128]{3,2,1,0:T(8,128)(2,1)S(1)}, bf16[2,2,32,128]{3,2,1,0:T(8,128)(2,1)S(1)}, u32[]{:S(2)}, u32[]{:S(2)}) collective-permute-start(bf16[2,2,32,128]{3,2,1,0:T(8,128)(2,1)S(1)} %get-tuple-element.218), channel_id=1, source_target_pairs={{0,8},{8,16},{16,24},{1,9},{9,17},{17,25},{2,10},{10,18},{18,26},{... | collective-permute-start | bytes 98312 | tf_op jit(solution)/shard_map/ppermute | solution.py:29
  38.1 1.3 %collective-permute-start.9 = (bf16[2,2,32,128]{3,2,1,0:T(8,128)(2,1)S(1)}, bf16[2,2,32,128]{3,2,1,0:T(8,128)(2,1)S(1)}, u32[]{:S(2)}, u32[]{:S(2)}) collective-permute-start(bf16[2,2,32,128]{3,2,1,0:T(8,128)(2,1)S(1)} %get-tuple-element.219), channel_id=1, source_target_pairs={{8,0},{16,8},{24,16},{9,1},{17,9},{25,17},{10,2},{18,10},{26,18},{... | collective-permute-start | bytes 98312 | tf_op jit(solution)/shard_map/ppermute | solution.py:31
  39.5 0.2 collective-permute-done.8
  39.7 4.2 %collective-permute-done.9 = bf16[2,2,32,128]{3,2,1,0:T(8,128)(2,1)S(1)} collective-permute-done((bf16[2,2,32,128]{3,2,1,0:T(8,128)(2,1)S(1)}, bf16[2,2,32,128]{3,2,1,0:T(8,128)(2,1)S(1)}, u32[]{:S(2)}, u32[]{:S(2)}) %collective-permute-start.9) | collective-permute-done | bytes 32800 | tf_op jit(solution)/shard_map/ppermute | solution.py:31
  44.0 3.2 %collective-permute-start.10 = (bf16[2,12,2,128]{3,2,1,0:T(2,128)(2,1)S(1)}, bf16[2,12,2,128]{3,2,1,0:T(2,128)(2,1)S(1)}, u32[]{:S(2)}, u32[]{:S(2)}) collective-permute-start(bf16[2,12,2,128]{3,2,1,0:T(2,128)(2,1)S(1)} %get-tuple-element.210), channel_id=1, source_target_pairs={{0,1},{1,2},{2,3},{3,4},{4,5},{5,6},{6,7},{8,9},{9,10},{10,11},{11... | collective-permute-start | bytes 36872 | tf_op jit(solution)/shard_map/ppermute | solution.py:29
  47.2 1.3 %collective-permute-start.11 = (bf16[2,12,2,128]{3,2,1,0:T(2,128)(2,1)S(1)}, bf16[2,12,2,128]{3,2,1,0:T(2,128)(2,1)S(1)}, u32[]{:S(2)}, u32[]{:S(2)}) collective-permute-start(bf16[2,12,2,128]{3,2,1,0:T(2,128)(2,1)S(1)} %get-tuple-element.211), channel_id=1, source_target_pairs={{1,0},{2,1},{3,2},{4,3},{5,4},{6,5},{7,6},{9,8},{10,9},{11,10},{12... | collective-permute-start | bytes 36872 | tf_op jit(solution)/shard_map/ppermute | solution.py:31
  48.5 2.7 %collective-permute-done.11 = bf16[2,12,2,128]{3,2,1,0:T(2,128)(2,1)S(1)} collective-permute-done((bf16[2,12,2,128]{3,2,1,0:T(2,128)(2,1)S(1)}, bf16[2,12,2,128]{3,2,1,0:T(2,128)(2,1)S(1)}, u32[]{:S(2)}, u32[]{:S(2)}) %collective-permute-start.11) | collective-permute-done | bytes 12320 | tf_op jit(solution)/shard_map/ppermute | solution.py:31
  51.5 0.2 scatter.30
  51.7 0.2 scatter.31
  52.1 0.2 fusion.32
  52.3 0.6 add_divide_fusion.6
  53.1 0.2 fusion.74
  53.5 3.5 %collective-permute-start.12 = (bf16[2,2,32,128]{3,2,1,0:T(8,128)(2,1)S(1)}, bf16[2,2,32,128]{3,2,1,0:T(8,128)(2,1)S(1)}, u32[]{:S(2)}, u32[]{:S(2)}) collective-permute-start(bf16[2,2,32,128]{3,2,1,0:T(8,128)(2,1)S(1)} %get-tuple-element.216), channel_id=1, source_target_pairs={{0,8},{8,16},{16,24},{1,9},{9,17},{17,25},{2,10},{10,18},{18,26},{... | collective-permute-start | bytes 98312 | tf_op jit(solution)/shard_map/ppermute | solution.py:29
  57.0 1.3 %collective-permute-start.13 = (bf16[2,2,32,128]{3,2,1,0:T(8,128)(2,1)S(1)}, bf16[2,2,32,128]{3,2,1,0:T(8,128)(2,1)S(1)}, u32[]{:S(2)}, u32[]{:S(2)}) collective-permute-start(bf16[2,2,32,128]{3,2,1,0:T(8,128)(2,1)S(1)} %get-tuple-element.217), channel_id=1, source_target_pairs={{8,0},{16,8},{24,16},{9,1},{17,9},{25,17},{10,2},{18,10},{26,18},{... | collective-permute-start | bytes 98312 | tf_op jit(solution)/shard_map/ppermute | solution.py:31
  58.6 4.2 %collective-permute-done.13 = bf16[2,2,32,128]{3,2,1,0:T(8,128)(2,1)S(1)} collective-permute-done((bf16[2,2,32,128]{3,2,1,0:T(8,128)(2,1)S(1)}, bf16[2,2,32,128]{3,2,1,0:T(8,128)(2,1)S(1)}, u32[]{:S(2)}, u32[]{:S(2)}) %collective-permute-start.13) | collective-permute-done | bytes 32800 | tf_op jit(solution)/shard_map/ppermute | solution.py:31
  62.8 2.9 %collective-permute-start.14 = (bf16[2,12,2,128]{3,2,1,0:T(2,128)(2,1)S(1)}, bf16[2,12,2,128]{3,2,1,0:T(2,128)(2,1)S(1)}, u32[]{:S(2)}, u32[]{:S(2)}) collective-permute-start(bf16[2,12,2,128]{3,2,1,0:T(2,128)(2,1)S(1)} %get-tuple-element.206), channel_id=1, source_target_pairs={{0,1},{1,2},{2,3},{3,4},{4,5},{5,6},{6,7},{8,9},{9,10},{10,11},{11... | collective-permute-start | bytes 36872 | tf_op jit(solution)/shard_map/ppermute | solution.py:29
  65.7 1.3 %collective-permute-start.15 = (bf16[2,12,2,128]{3,2,1,0:T(2,128)(2,1)S(1)}, bf16[2,12,2,128]{3,2,1,0:T(2,128)(2,1)S(1)}, u32[]{:S(2)}, u32[]{:S(2)}) collective-permute-start(bf16[2,12,2,128]{3,2,1,0:T(2,128)(2,1)S(1)} %get-tuple-element.207), channel_id=1, source_target_pairs={{1,0},{2,1},{3,2},{4,3},{5,4},{6,5},{7,6},{9,8},{10,9},{11,10},{12... | collective-permute-start | bytes 36872 | tf_op jit(solution)/shard_map/ppermute | solution.py:31
  67.1 2.9 %collective-permute-done.15 = bf16[2,12,2,128]{3,2,1,0:T(2,128)(2,1)S(1)} collective-permute-done((bf16[2,12,2,128]{3,2,1,0:T(2,128)(2,1)S(1)}, bf16[2,12,2,128]{3,2,1,0:T(2,128)(2,1)S(1)}, u32[]{:S(2)}, u32[]{:S(2)}) %collective-permute-start.15) | collective-permute-done | bytes 12320 | tf_op jit(solution)/shard_map/ppermute | solution.py:31
  70.3 0.2 scatter.34
  70.5 0.2 scatter.35
  70.9 0.2 fusion.16
  71.1 0.6 add_divide_fusion.5
  71.9 0.2 fusion.75
  72.3 3.5 %collective-permute-start.16 = (bf16[2,2,32,128]{3,2,1,0:T(8,128)(2,1)S(1)}, bf16[2,2,32,128]{3,2,1,0:T(8,128)(2,1)S(1)}, u32[]{:S(2)}, u32[]{:S(2)}) collective-permute-start(bf16[2,2,32,128]{3,2,1,0:T(8,128)(2,1)S(1)} %get-tuple-element.214), channel_id=1, source_target_pairs={{0,8},{8,16},{16,24},{1,9},{9,17},{17,25},{2,10},{10,18},{18,26},{... | collective-permute-start | bytes 98312 | tf_op jit(solution)/shard_map/ppermute | solution.py:29
  75.8 1.3 %collective-permute-start.17 = (bf16[2,2,32,128]{3,2,1,0:T(8,128)(2,1)S(1)}, bf16[2,2,32,128]{3,2,1,0:T(8,128)(2,1)S(1)}, u32[]{:S(2)}, u32[]{:S(2)}) collective-permute-start(bf16[2,2,32,128]{3,2,1,0:T(8,128)(2,1)S(1)} %get-tuple-element.215), channel_id=1, source_target_pairs={{8,0},{16,8},{24,16},{9,1},{17,9},{25,17},{10,2},{18,10},{26,18},{... | collective-permute-start | bytes 98312 | tf_op jit(solution)/shard_map/ppermute | solution.py:31
  77.4 4.2 %collective-permute-done.17 = bf16[2,2,32,128]{3,2,1,0:T(8,128)(2,1)S(1)} collective-permute-done((bf16[2,2,32,128]{3,2,1,0:T(8,128)(2,1)S(1)}, bf16[2,2,32,128]{3,2,1,0:T(8,128)(2,1)S(1)}, u32[]{:S(2)}, u32[]{:S(2)}) %collective-permute-start.17) | collective-permute-done | bytes 32800 | tf_op jit(solution)/shard_map/ppermute | solution.py:31
  81.6 3.1 %collective-permute-start.18 = (bf16[2,12,2,128]{3,2,1,0:T(2,128)(2,1)S(1)}, bf16[2,12,2,128]{3,2,1,0:T(2,128)(2,1)S(1)}, u32[]{:S(2)}, u32[]{:S(2)}) collective-permute-start(bf16[2,12,2,128]{3,2,1,0:T(2,128)(2,1)S(1)} %get-tuple-element.202), channel_id=1, source_target_pairs={{0,1},{1,2},{2,3},{3,4},{4,5},{5,6},{6,7},{8,9},{9,10},{10,11},{11... | collective-permute-start | bytes 36872 | tf_op jit(solution)/shard_map/ppermute | solution.py:29
  84.7 1.3 %collective-permute-start.19 = (bf16[2,12,2,128]{3,2,1,0:T(2,128)(2,1)S(1)}, bf16[2,12,2,128]{3,2,1,0:T(2,128)(2,1)S(1)}, u32[]{:S(2)}, u32[]{:S(2)}) collective-permute-start(bf16[2,12,2,128]{3,2,1,0:T(2,128)(2,1)S(1)} %get-tuple-element.203), channel_id=1, source_target_pairs={{1,0},{2,1},{3,2},{4,3},{5,4},{6,5},{7,6},{9,8},{10,9},{11,10},{12... | collective-permute-start | bytes 36872 | tf_op jit(solution)/shard_map/ppermute | solution.py:31
  86.1 3.4 %collective-permute-done.19 = bf16[2,12,2,128]{3,2,1,0:T(2,128)(2,1)S(1)} collective-permute-done((bf16[2,12,2,128]{3,2,1,0:T(2,128)(2,1)S(1)}, bf16[2,12,2,128]{3,2,1,0:T(2,128)(2,1)S(1)}, u32[]{:S(2)}, u32[]{:S(2)}) %collective-permute-start.19) | collective-permute-done | bytes 12320 | tf_op jit(solution)/shard_map/ppermute | solution.py:31
  89.7 0.2 scatter.36
  90.0 0.2 scatter.39
  90.4 0.2 fusion
  90.6 0.6 add_divide_fusion.4
  91.4 0.2 fusion.77
  91.8 0.6 gather_fusion
  101.7 0.8 and_reduce_fusion
  102.4 0.6 fusion.151
  103.1 0.7 fusion.152
  103.8 0.6 gather_fusion.1
  104.4 5.1 %collective-permute-start.21 = (f32[2,2,4,16,128]{4,3,2,0,1:T(8,128)S(1)}, f32[2,2,4,16,128]{4,3,2,0,1:T(8,128)S(1)}, u32[]{:S(2)}, u32[]{:S(2)}) collective-permute-start(f32[2,2,4,16,128]{4,3,2,0,1:T(8,128)S(1)} %copy.28), channel_id=1, source_target_pairs={{0,4},{1,5},{2,6},{3,7},{4,0},{5,1},{6,2},{7,3},{8,12},{9,13},{10,... | collective-permute-start | bytes 393224 | tf_op jit(solution)/shard_map/ppermute | solution.py:39
  110.7 1.7 %collective-permute-done.21 = f32[2,2,4,16,128]{4,3,2,0,1:T(8,128)S(1)} collective-permute-done((f32[2,2,4,16,128]{4,3,2,0,1:T(8,128)S(1)}, f32[2,2,4,16,128]{4,3,2,0,1:T(8,128)S(1)}, u32[]{:S(2)}, u32[]{:S(2)}) %collective-permute-start.21) | collective-permute-done | bytes 131104 | tf_op jit(solution)/shard_map/ppermute | solution.py:39
  112.4 0.6 fusion.153
  113.0 0.7 fusion.154
  113.7 0.7 slice_bitcast_fusion.8
  (104 shorter events, 5.4 us)
Async XLA Ops:
  1.4 15.4 %collective-permute-start = (s32[1,2]{1,0:T(1,128)S(1)}, s32[1,2]{1,0:T(1,128)S(1)}, u32[]{:S(2)}, u32[]{:S(2)}) collective-permute-start(s32[1,2]{1,0:T(1,128)S(1)} %get-tuple-element.242), channel_id=1, source_target_pairs={{0,8},{8,16},{16,24},{1,9},{9,17},{17,25},{2,10},{10,18},{18,26},{... | collective-permute-start | bytes 32 | tf_op jit(solution)/shard_map/ppermute | solution.py:29
  6.3 10.5 %collective-permute-start.1 = (s32[1,2]{1,0:T(1,128)S(1)}, s32[1,2]{1,0:T(1,128)S(1)}, u32[]{:S(2)}, u32[]{:S(2)}) collective-permute-start(s32[1,2]{1,0:T(1,128)S(1)} %get-tuple-element.243), channel_id=1, source_target_pairs={{8,0},{16,8},{24,16},{9,1},{17,9},{25,17},{10,2},{18,10},{26,18},{... | collective-permute-start | bytes 32 | tf_op jit(solution)/shard_map/ppermute | solution.py:31
  7.6 7.7 %copy-start.1 = (f32[8,32,128]{2,1,0:T(8,128)S(1)}, f32[8,32,128]{2,1,0:T(8,128)}, u32[]{:S(2)}) copy-start(f32[8,32,128]{2,1,0:T(8,128)} %param.29) | copy-start | bytes 393220
  8.7 6.7 %copy-start = (f32[8,32,128]{2,1,0:T(8,128)S(1)}, f32[8,32,128]{2,1,0:T(8,128)}, u32[]{:S(2)}) copy-start(f32[8,32,128]{2,1,0:T(8,128)} %param.30) | copy-start | bytes 393220
  8.7 6.0 %copy-start.3 = (s32[2,2]{1,0:T(2,128)S(1)}, s32[2,2]{1,0:T(2,128)}, u32[]{:S(2)}) copy-start(s32[2,2]{1,0:T(2,128)} %param.31) | copy-start | bytes 52
  8.7 14.9 %collective-permute-start.4 = (bf16[2,2,32,128]{3,2,1,0:T(8,128)(2,1)S(1)}, bf16[2,2,32,128]{3,2,1,0:T(8,128)(2,1)S(1)}, u32[]{:S(2)}, u32[]{:S(2)}) collective-permute-start(bf16[2,2,32,128]{3,2,1,0:T(8,128)(2,1)S(1)} %get-tuple-element.220), channel_id=1, source_target_pairs={{0,8},{8,16},{16,24},{1,9},{9,17},{17,25},{2,10},{10,18},{18,26},{... | collective-permute-start | bytes 98312 | tf_op jit(solution)/shard_map/ppermute | solution.py:29
  13.4 1.3 %copy-start.2 = (s32[1,1,2,2]{3,2,1,0:T(2,128)S(1)}, s32[1,1,2,2]{3,2,1,0:T(2,128)}, u32[]{:S(2)}) copy-start(s32[1,1,2,2]{3,2,1,0:T(2,128)} %param.33) | copy-start | bytes 52
  13.4 10.3 %collective-permute-start.5 = (bf16[2,2,32,128]{3,2,1,0:T(8,128)(2,1)S(1)}, bf16[2,2,32,128]{3,2,1,0:T(8,128)(2,1)S(1)}, u32[]{:S(2)}, u32[]{:S(2)}) collective-permute-start(bf16[2,2,32,128]{3,2,1,0:T(8,128)(2,1)S(1)} %get-tuple-element.221), channel_id=1, source_target_pairs={{8,0},{16,8},{24,16},{9,1},{17,9},{25,17},{10,2},{18,10},{26,18},{... | collective-permute-start | bytes 98312 | tf_op jit(solution)/shard_map/ppermute | solution.py:31
  15.5 0.7 copy-start.4
  16.9 2.6 %collective-permute-start.2 = (s32[4,1]{1,0:T(4,128)S(1)}, s32[4,1]{1,0:T(4,128)S(1)}, u32[]{:S(2)}, u32[]{:S(2)}) collective-permute-start(s32[4,1]{1,0:T(4,128)S(1)} %get-tuple-element.234), channel_id=1, source_target_pairs={{0,1},{1,2},{2,3},{3,4},{4,5},{5,6},{6,7},{8,9},{9,10},{10,11},{11... | collective-permute-start | bytes 56 | tf_op jit(solution)/shard_map/ppermute | solution.py:29
  18.2 4.8 %collective-permute-start.3 = (s32[4,1]{1,0:T(4,128)S(1)}, s32[4,1]{1,0:T(4,128)S(1)}, u32[]{:S(2)}, u32[]{:S(2)}) collective-permute-start(s32[4,1]{1,0:T(4,128)S(1)} %get-tuple-element.235), channel_id=1, source_target_pairs={{1,0},{2,1},{3,2},{4,3},{5,4},{6,5},{7,6},{9,8},{10,9},{11,10},{12... | collective-permute-start | bytes 56 | tf_op jit(solution)/shard_map/ppermute | solution.py:31
  23.7 5.9 %collective-permute-start.6 = (bf16[2,12,2,128]{3,2,1,0:T(2,128)(2,1)S(1)}, bf16[2,12,2,128]{3,2,1,0:T(2,128)(2,1)S(1)}, u32[]{:S(2)}, u32[]{:S(2)}) collective-permute-start(bf16[2,12,2,128]{3,2,1,0:T(2,128)(2,1)S(1)} %get-tuple-element.212), channel_id=1, source_target_pairs={{0,1},{1,2},{2,3},{3,4},{4,5},{5,6},{6,7},{8,9},{9,10},{10,11},{11... | collective-permute-start | bytes 36872 | tf_op jit(solution)/shard_map/ppermute | solution.py:29
  28.3 3.1 %collective-permute-start.7 = (bf16[2,12,2,128]{3,2,1,0:T(2,128)(2,1)S(1)}, bf16[2,12,2,128]{3,2,1,0:T(2,128)(2,1)S(1)}, u32[]{:S(2)}, u32[]{:S(2)}) collective-permute-start(bf16[2,12,2,128]{3,2,1,0:T(2,128)(2,1)S(1)} %get-tuple-element.213), channel_id=1, source_target_pairs={{1,0},{2,1},{3,2},{4,3},{5,4},{6,5},{7,6},{9,8},{10,9},{11,10},{12... | collective-permute-start | bytes 36872 | tf_op jit(solution)/shard_map/ppermute | solution.py:31
  33.6 6.1 %collective-permute-start.8 = (bf16[2,2,32,128]{3,2,1,0:T(8,128)(2,1)S(1)}, bf16[2,2,32,128]{3,2,1,0:T(8,128)(2,1)S(1)}, u32[]{:S(2)}, u32[]{:S(2)}) collective-permute-start(bf16[2,2,32,128]{3,2,1,0:T(8,128)(2,1)S(1)} %get-tuple-element.218), channel_id=1, source_target_pairs={{0,8},{8,16},{16,24},{1,9},{9,17},{17,25},{2,10},{10,18},{18,26},{... | collective-permute-start | bytes 98312 | tf_op jit(solution)/shard_map/ppermute | solution.py:29
  38.1 5.8 %collective-permute-start.9 = (bf16[2,2,32,128]{3,2,1,0:T(8,128)(2,1)S(1)}, bf16[2,2,32,128]{3,2,1,0:T(8,128)(2,1)S(1)}, u32[]{:S(2)}, u32[]{:S(2)}) collective-permute-start(bf16[2,2,32,128]{3,2,1,0:T(8,128)(2,1)S(1)} %get-tuple-element.219), channel_id=1, source_target_pairs={{8,0},{16,8},{24,16},{9,1},{17,9},{25,17},{10,2},{18,10},{26,18},{... | collective-permute-start | bytes 98312 | tf_op jit(solution)/shard_map/ppermute | solution.py:31
  44.0 4.5 %collective-permute-start.10 = (bf16[2,12,2,128]{3,2,1,0:T(2,128)(2,1)S(1)}, bf16[2,12,2,128]{3,2,1,0:T(2,128)(2,1)S(1)}, u32[]{:S(2)}, u32[]{:S(2)}) collective-permute-start(bf16[2,12,2,128]{3,2,1,0:T(2,128)(2,1)S(1)} %get-tuple-element.210), channel_id=1, source_target_pairs={{0,1},{1,2},{2,3},{3,4},{4,5},{5,6},{6,7},{8,9},{9,10},{10,11},{11... | collective-permute-start | bytes 36872 | tf_op jit(solution)/shard_map/ppermute | solution.py:29
  47.2 4.0 %collective-permute-start.11 = (bf16[2,12,2,128]{3,2,1,0:T(2,128)(2,1)S(1)}, bf16[2,12,2,128]{3,2,1,0:T(2,128)(2,1)S(1)}, u32[]{:S(2)}, u32[]{:S(2)}) collective-permute-start(bf16[2,12,2,128]{3,2,1,0:T(2,128)(2,1)S(1)} %get-tuple-element.211), channel_id=1, source_target_pairs={{1,0},{2,1},{3,2},{4,3},{5,4},{6,5},{7,6},{9,8},{10,9},{11,10},{12... | collective-permute-start | bytes 36872 | tf_op jit(solution)/shard_map/ppermute | solution.py:31
  53.5 5.1 %collective-permute-start.12 = (bf16[2,2,32,128]{3,2,1,0:T(8,128)(2,1)S(1)}, bf16[2,2,32,128]{3,2,1,0:T(8,128)(2,1)S(1)}, u32[]{:S(2)}, u32[]{:S(2)}) collective-permute-start(bf16[2,2,32,128]{3,2,1,0:T(8,128)(2,1)S(1)} %get-tuple-element.216), channel_id=1, source_target_pairs={{0,8},{8,16},{16,24},{1,9},{9,17},{17,25},{2,10},{10,18},{18,26},{... | collective-permute-start | bytes 98312 | tf_op jit(solution)/shard_map/ppermute | solution.py:29
  57.0 5.8 %collective-permute-start.13 = (bf16[2,2,32,128]{3,2,1,0:T(8,128)(2,1)S(1)}, bf16[2,2,32,128]{3,2,1,0:T(8,128)(2,1)S(1)}, u32[]{:S(2)}, u32[]{:S(2)}) collective-permute-start(bf16[2,2,32,128]{3,2,1,0:T(8,128)(2,1)S(1)} %get-tuple-element.217), channel_id=1, source_target_pairs={{8,0},{16,8},{24,16},{9,1},{17,9},{25,17},{10,2},{18,10},{26,18},{... | collective-permute-start | bytes 98312 | tf_op jit(solution)/shard_map/ppermute | solution.py:31
  62.8 4.3 %collective-permute-start.14 = (bf16[2,12,2,128]{3,2,1,0:T(2,128)(2,1)S(1)}, bf16[2,12,2,128]{3,2,1,0:T(2,128)(2,1)S(1)}, u32[]{:S(2)}, u32[]{:S(2)}) collective-permute-start(bf16[2,12,2,128]{3,2,1,0:T(2,128)(2,1)S(1)} %get-tuple-element.206), channel_id=1, source_target_pairs={{0,1},{1,2},{2,3},{3,4},{4,5},{5,6},{6,7},{8,9},{9,10},{10,11},{11... | collective-permute-start | bytes 36872 | tf_op jit(solution)/shard_map/ppermute | solution.py:29
  65.7 4.2 %collective-permute-start.15 = (bf16[2,12,2,128]{3,2,1,0:T(2,128)(2,1)S(1)}, bf16[2,12,2,128]{3,2,1,0:T(2,128)(2,1)S(1)}, u32[]{:S(2)}, u32[]{:S(2)}) collective-permute-start(bf16[2,12,2,128]{3,2,1,0:T(2,128)(2,1)S(1)} %get-tuple-element.207), channel_id=1, source_target_pairs={{1,0},{2,1},{3,2},{4,3},{5,4},{6,5},{7,6},{9,8},{10,9},{11,10},{12... | collective-permute-start | bytes 36872 | tf_op jit(solution)/shard_map/ppermute | solution.py:31
  72.3 5.1 %collective-permute-start.16 = (bf16[2,2,32,128]{3,2,1,0:T(8,128)(2,1)S(1)}, bf16[2,2,32,128]{3,2,1,0:T(8,128)(2,1)S(1)}, u32[]{:S(2)}, u32[]{:S(2)}) collective-permute-start(bf16[2,2,32,128]{3,2,1,0:T(8,128)(2,1)S(1)} %get-tuple-element.214), channel_id=1, source_target_pairs={{0,8},{8,16},{16,24},{1,9},{9,17},{17,25},{2,10},{10,18},{18,26},{... | collective-permute-start | bytes 98312 | tf_op jit(solution)/shard_map/ppermute | solution.py:29
  75.8 5.8 %collective-permute-start.17 = (bf16[2,2,32,128]{3,2,1,0:T(8,128)(2,1)S(1)}, bf16[2,2,32,128]{3,2,1,0:T(8,128)(2,1)S(1)}, u32[]{:S(2)}, u32[]{:S(2)}) collective-permute-start(bf16[2,2,32,128]{3,2,1,0:T(8,128)(2,1)S(1)} %get-tuple-element.215), channel_id=1, source_target_pairs={{8,0},{16,8},{24,16},{9,1},{17,9},{25,17},{10,2},{18,10},{26,18},{... | collective-permute-start | bytes 98312 | tf_op jit(solution)/shard_map/ppermute | solution.py:31
  81.6 4.4 %collective-permute-start.18 = (bf16[2,12,2,128]{3,2,1,0:T(2,128)(2,1)S(1)}, bf16[2,12,2,128]{3,2,1,0:T(2,128)(2,1)S(1)}, u32[]{:S(2)}, u32[]{:S(2)}) collective-permute-start(bf16[2,12,2,128]{3,2,1,0:T(2,128)(2,1)S(1)} %get-tuple-element.202), channel_id=1, source_target_pairs={{0,1},{1,2},{2,3},{3,4},{4,5},{5,6},{6,7},{8,9},{9,10},{10,11},{11... | collective-permute-start | bytes 36872 | tf_op jit(solution)/shard_map/ppermute | solution.py:29
  84.7 4.8 %collective-permute-start.19 = (bf16[2,12,2,128]{3,2,1,0:T(2,128)(2,1)S(1)}, bf16[2,12,2,128]{3,2,1,0:T(2,128)(2,1)S(1)}, u32[]{:S(2)}, u32[]{:S(2)}) collective-permute-start(bf16[2,12,2,128]{3,2,1,0:T(2,128)(2,1)S(1)} %get-tuple-element.203), channel_id=1, source_target_pairs={{1,0},{2,1},{3,2},{4,3},{5,4},{6,5},{7,6},{9,8},{10,9},{11,10},{12... | collective-permute-start | bytes 36872 | tf_op jit(solution)/shard_map/ppermute | solution.py:31
  92.3 10.1 %collective-permute-start.20 = (f32[2,2,4,16,128]{4,3,2,0,1:T(8,128)S(1)}, f32[2,2,4,16,128]{4,3,2,0,1:T(8,128)S(1)}, u32[]{:S(2)}, u32[]{:S(2)}) collective-permute-start(f32[2,2,4,16,128]{4,3,2,0,1:T(8,128)S(1)} %copy.27), channel_id=1, source_target_pairs={{0,16},{8,24},{16,0},{24,8},{1,17},{9,25},{17,1},{25,9},{2,18},{10... | collective-permute-start | bytes 393224 | tf_op jit(solution)/shard_map/ppermute | solution.py:39
  100.9 0.7 copy-start.5
  104.4 8.1 %collective-permute-start.21 = (f32[2,2,4,16,128]{4,3,2,0,1:T(8,128)S(1)}, f32[2,2,4,16,128]{4,3,2,0,1:T(8,128)S(1)}, u32[]{:S(2)}, u32[]{:S(2)}) collective-permute-start(f32[2,2,4,16,128]{4,3,2,0,1:T(8,128)S(1)} %copy.28), channel_id=1, source_target_pairs={{0,4},{1,5},{2,6},{3,7},{4,0},{5,1},{6,2},{7,3},{8,12},{9,13},{10,... | collective-permute-start | bytes 393224 | tf_op jit(solution)/shard_map/ppermute | solution.py:39
where the time goes:
time: 115 us; the launch traced here: 114 us
  starting transfers between devices  54 us (47%)
  waiting for transfers between devices  29.1 us (25%)
  other arithmetic  12 us (10%)
  between operations  11.6 us (10%)
  local copies, waits for them, and re-layouts  7.74 us (7%)
    ppermute x10, starting transfers between devices, with_halo(): lax.ppermute(tail, axis, [(i, (i + 1) % count) for i in range(ends)])  35.9 us
    ppermute x10, waiting for transfers between devices, with_halo(): lax.ppermute(head, axis, [((i + 1) % count, i) for i in range(ends)])  26.9 us
    ppermute x10, starting transfers between devices, with_halo(): lax.ppermute(head, axis, [((i + 1) % count, i) for i in range(ends)])  12.9 us
    ppermute x2, starting transfers between devices, swapped(): lax.ppermute(shard, axis, [(i, i ^ 1 << distance) for i in range(lax.axis...  5.18 us
    select_n x4, other arithmetic, place_moved(): member = jnp.where(position < count, updated, member)  2.61 us
    div x4, other arithmetic, liquid(): return jax.nn.sigmoid((values - melt_point) / melt_width)  2.47 us
  transfers between devices with their start and end apart: 22, of which 12 were waited for; matrix products, arithmetic and copies ran while one was open for 4% of the time, Pallas kernels for 0%

commit v1 on v0

v1 whole, which is shorter than its diff:
```python
import functools

import jax
import jax.numpy as jnp
from jax import lax
from jax.experimental import pallas as pl
from jax.experimental.pallas import tpu as pltpu
from jax.sharding import PartitionSpec as P

PAIRS = 4
DEEP = 2 * PAIRS
SUB = 8
LANES = 128

HEAT_SCALE = 25000.0
HEAT_SHIFT = 32000.0
PORE_SCALE = 40000.0
PORE_SHIFT = 7000.0


def encode(values, scale, shift):
    return jnp.floor(values * scale + (0.5 - shift)).astype(jnp.int32).astype(jnp.int16)


def decode(codes, scale, shift):
    return (codes.astype(jnp.int32).astype(jnp.float32) + shift) * (1.0 / scale)


def tile_slice(slot, tx, ty):
    return pl.ds((slot // 2) * tx, tx), pl.ds((slot % 2) * ty, ty)


def flag_rows(active_ref, cols):
    lane = lax.broadcasted_iota(jnp.int32, (cols, LANES), 1)
    col = lax.broadcasted_iota(jnp.int32, (cols, LANES), 0)

    def flag(i):
        return jnp.where(col < cols // 2, active_ref[i, 0], active_ref[i, 1])

    return jnp.where(lane < LANES // 2, flag(0), flag(1)).astype(jnp.float32)


def pack_x(active_ref, heat_ref, pore_ref, out_ref):
    rows, cols = heat_ref.shape[0], heat_ref.shape[1]
    out_ref[0:rows] = heat_ref[...].astype(jnp.bfloat16)
    out_ref[rows : 2 * rows] = pore_ref[...].astype(jnp.bfloat16)
    out_ref[2 * rows] = flag_rows(active_ref, cols).astype(jnp.bfloat16)


def pack_y(own_ref, up_ref, down_ref, left_ref, right_ref):
    rows = (own_ref.shape[0] - 1) // 2
    cols = own_ref.shape[1]
    parts = (up_ref, own_ref, down_ref)
    for out_ref, start in ((left_ref, 0), (right_ref, cols - DEEP)):
        for i, part in enumerate(parts):
            for f in range(2):
                out_ref[pl.ds(f * 3 * rows + i * rows, rows)] = part[
                    pl.ds(f * rows, rows), pl.ds(start, DEEP), :
                ]
            out_ref[6 * rows + i] = part[2 * rows, pl.ds(start, DEEP), :]


def row_flux(vals, weights, lane_open):
    n = len(vals)
    acc = [None] * n

    def add(j, v):
        acc[j] = v if acc[j] is None else acc[j] + v

    def sub(j, v):
        acc[j] = -v if acc[j] is None else acc[j] - v

    for j in range(n):
        beyond = pltpu.roll(vals[j], LANES - 1, 1)
        beyond_w = pltpu.roll(weights[j], LANES - 1, 1)
        f = (weights[j] + beyond_w) * (beyond - vals[j])
        f = jnp.where(lane_open, f, 0.0)
        add(j, f)
        sub(j, pltpu.roll(f, 1, 1))
    for j in range(n - 1):
        f = (weights[j] + weights[j + 1]) * (vals[j + 1] - vals[j])
        add(j, f)
        sub(j + 1, f)
    f = (weights[n - 1] + pltpu.roll(weights[0], SUB - 1, 0)) * (
        pltpu.roll(vals[0], SUB - 1, 0) - vals[n - 1]
    )
    add(n - 1, f)
    sub(0, pltpu.roll(f, 1, 0))
    return acc


def step(
    active_ref, count_ref, slot_ref, heat_ref, pore_ref, up_ref, down_ref, left_ref, right_ref,
    heat_out, pore_out, send_ref, wide, hs, qs, ms,
):
    rows, cols = heat_ref.shape[0], heat_ref.shape[1]
    tx, ty = rows // 2, cols // 2
    total = rows + 2 * DEEP
    width = cols + 2 * DEEP
    groups = width // SUB
    lane = lax.broadcasted_iota(jnp.int32, (SUB, LANES), 1)
    lane_open = lane < LANES - 1
    low_half = lane < LANES // 2

    def spread_row(x, store):
        for j in range(groups):
            store(j, wide[x, pl.ds(j, SUB, stride=groups), :])

    for i, part in enumerate((up_ref, None, down_ref)):
        if part is None:
            mid = flag_rows(active_ref, cols)
        else:
            mid = part[2 * rows].astype(jnp.float32)
        wide[i, 0:DEEP, :] = left_ref[6 * rows + i].astype(jnp.float32)
        wide[i, DEEP : DEEP + cols, :] = mid
        wide[i, DEEP + cols :, :] = right_ref[6 * rows + i].astype(jnp.float32)
    for i in range(3):
        for j in range(groups):
            f = wide[i, pl.ds(j, SUB, stride=groups), :]
            r = pltpu.roll(f, LANES // 2, 1)
            ms[2 * i, j] = jnp.where(low_half, f, r)
            ms[2 * i + 1, j] = jnp.where(low_half, r, f)

    for field, own_ref, store_ref in ((0, heat_ref, hs), (1, pore_ref, qs)):
        for i, part in enumerate((up_ref, None, down_ref)):
            for r in range(rows):
                x = i * rows + r
                if part is None:
                    mid = own_ref[r]
                else:
                    mid = part[field * rows + r].astype(jnp.float32)
                y = field * 3 * rows + x
                wide[x, 0:DEEP, :] = left_ref[y].astype(jnp.float32)
                wide[x, DEEP : DEEP + cols, :] = mid
                wide[x, DEEP + cols :, :] = right_ref[y].astype(jnp.float32)
        for x in range(total):
            for j in range(groups):
                v = wide[x, pl.ds(j, SUB, stride=groups), :]
                store_ref[x, j] = 2.0 * v - 2.0 if field == 0 else v

    span = range(groups)
    for p in range(PAIRS):
        lo, hi = 2 * p, total - 2 * p
        before = None
        for x in range(lo, hi):
            h = [hs[x, j] for j in span]
            t = [jnp.tanh(h[j]) for j in span]
            temp = [h[j] - 0.4 * t[j] for j in span]
            cond = []
            for j in span:
                solid = 1.0 - qs[x, j]
                cond.append(solid * solid * (t[j] + 7.0 / 3.0))
            if before is not None:
                last_h, last_temp, last_cond, last_flux = before
                flux = [(last_cond[j] + cond[j]) * (temp[j] - last_temp[j]) for j in span]
                if last_flux is not None:
                    acc = row_flux(last_temp, last_cond, lane_open)
                    m = (x - 1) // tx
                    for j in span:
                        hs[x - 1, j] = last_h[j] + (0.0225 * ms[m, j]) * (
                            acc[j] + (flux[j] - last_flux[j])
                        )
            else:
                flux = None
            before = (h, temp, cond, flux)
        before = None
        for x in range(lo + 1, hi - 1):
            rate = []
            for j in span:
                g = hs[x, j]
                rate.append(1.0 + jnp.tanh(2.5 * g - jnp.tanh(g)))
            q = [qs[x, j] for j in span]
            if before is not None:
                last_q, last_rate, last_flux = before
                flux = [(last_rate[j] + rate[j]) * (q[j] - last_q[j]) for j in span]
                if last_flux is not None:
                    acc = row_flux(last_q, last_rate, lane_open)
                    m = (x - 1) // tx
                    for j in span:
                        qs[x - 1, j] = last_q[j] + (0.0375 * ms[m, j]) * (
                            acc[j] + (flux[j] - last_flux[j]) - 4.0 * last_rate[j] * last_q[j]
                        )
            else:
                flux = None
            before = (q, rate, flux)

    for src, out, field in ((hs, heat_out, 0), (qs, pore_out, 1)):
        for r in range(rows):
            for j in span:
                v = src[DEEP + r, j]
                wide[r, pl.ds(j, SUB, stride=groups), :] = 0.5 * v + 1.0 if field == 0 else v
        for i in range(2):
            for k in range(2):
                out[2 * i + k] = wide[i * tx : (i + 1) * tx, DEEP + k * ty : DEEP + (k + 1) * ty, :]
    for k in range(slot_ref.shape[1]):
        s = slot_ref[0, k]
        send_ref[k, 0] = encode(heat_out[s], HEAT_SCALE, HEAT_SHIFT)
        send_ref[k, 1] = encode(pore_out[s], PORE_SCALE, PORE_SHIFT)


def resend(count_ref, slot_ref, heat_ref, pore_ref, got_ref, send_ref):
    ranks = slot_ref.shape[1]
    for k in range(ranks):
        s = slot_ref[1, k]
        send_ref[k, 0] = encode(heat_ref[s], HEAT_SCALE, HEAT_SHIFT)
        send_ref[k, 1] = encode(pore_ref[s], PORE_SCALE, PORE_SHIFT)
        for r in range(ranks):

            @pl.when((r < count_ref[0]) & (slot_ref[0, r] == s))
            def _():
                send_ref[k] = got_ref[r]


def place(count_ref, slot_ref, heat_ref, pore_ref, first_ref, second_ref, heat_out, pore_out):
    ranks = slot_ref.shape[1]
    heat_out[...] = heat_ref[...]
    pore_out[...] = pore_ref[...]
    for i, got_ref in ((0, first_ref), (1, second_ref)):
        for r in range(ranks):

            @pl.when(r < count_ref[i])
            def _():
                s = slot_ref[i, r]
                heat_out[s] = decode(got_ref[r, 0], HEAT_SCALE, HEAT_SHIFT)
                pore_out[s] = decode(got_ref[r, 1], PORE_SCALE, PORE_SHIFT)


def call(body, spec, outs, scratch=(), name=None):
    space = {"s": pltpu.SMEM, "v": pltpu.VMEM}
    return pl.pallas_call(
        body,
        in_specs=[pl.BlockSpec(memory_space=space[c]) for c in spec],
        out_specs=[pl.BlockSpec(memory_space=pltpu.VMEM) for _ in outs],
        out_shape=[jax.ShapeDtypeStruct(s, d) for s, d in outs],
        scratch_shapes=list(scratch),
        name=name,
    )


def shift(value, axis, up):
    n = lax.axis_size(axis)
    pairs = [(i, i + 1) if up else (i + 1, i) for i in range(n - 1)]
    return lax.ppermute(value, axis, pairs)


def swap(value, axis):
    n = lax.axis_size(axis)
    return lax.ppermute(value, axis, [(i, (i + n // 2) % n) for i in range(n)])


def per_device(enthalpy, porosity, active, move_count, move_slot):
    rows, cols, depth = enthalpy.shape
    tx, ty = rows // 2, cols // 2
    count = move_count.reshape(2)
    slots = move_slot.reshape(2, move_slot.shape[-1])
    ranks = slots.shape[1]
    f32, bf16, i16 = jnp.float32, jnp.bfloat16, jnp.int16

    (own,) = call(pack_x, "svv", [((2 * rows + 1, cols, depth), bf16)], name="pack_x")(
        active, enthalpy, porosity
    )
    up = shift(own, "gx", True)
    down = shift(own, "gx", False)
    side = ((6 * rows + 3, DEEP, depth), bf16)
    to_left, to_right = call(pack_y, "vvv", [side, side], name="pack_y")(own, up, down)
    left = shift(to_right, "gy", True)
    right = shift(to_left, "gy", False)
    total, width = rows + 2 * DEEP, cols + 2 * DEEP
    tiles = ((4, tx, ty, depth), f32)
    parcel = ((ranks, 2, tx, ty, depth), i16)
    split = pltpu.VMEM((total, width // SUB, SUB, depth), f32)
    heat, pore, first = call(
        step, "sssvvvvvv", [tiles, tiles, parcel],
        [
            pltpu.VMEM((total, width, depth), f32),
            split,
            split,
            pltpu.VMEM((total // tx, width // SUB, SUB, depth), f32),
        ],
        name="step",
    )(active, count, slots, enthalpy, porosity, up, down, left, right)
    first = swap(first, "gx")
    (second,) = call(resend, "ssvvv", [parcel], name="resend")(count, slots, heat, pore, first)
    second = swap(second, "gy")
    heat, pore = call(place, "ssvvvv", [tiles, tiles], name="place")(
        count, slots, heat, pore, first, second
    )
    return heat[None, None], pore[None, None]


def solution(mesh):
    placed = (
        P("gx", "gy", None),
        P("gx", "gy", None),
        P("gx", "gy"),
        P("gx", "gy", None),
        P("gx", "gy", None, None),
    )
    out = P("gx", "gy", None, None, None, None)
    return jax.shard_map(
        per_device, mesh=mesh, in_specs=placed, out_specs=(out, out), check_vma=False
    )
```

time: 115 us -> 89.1 us (0.77)
  Pallas kernels: 0 us -> 54.2 us
  starting transfers between devices: 54 us -> 19.1 us
  waiting for transfers between devices: 29.1 us -> 12.2 us
  other arithmetic: 12 us -> 0 us
  between operations: 11.6 us -> 0.69 us
  local copies, waits for them, and re-layouts: 7.74 us -> 2.56 us
    pallas_call x0 -> x5, Pallas kernels: none -> 54.2 us  [the longest x1 47.4 us: per_device(): call(step, 'sssvvvvvv', [tiles, tiles, parcel], [pltpu.VMEM((total, width...]
    ppermute x22 -> x6, starting transfers between devices: 54 us -> 19.1 us  [the longest x2 9.61 us: swap(): return lax.ppermute(value, axis, [(i, (i + n // 2) % n) for i in range(n)])]
    ppermute x22 -> x6, waiting for transfers between devices: 29.1 us -> 12.2 us  [the longest x4 7.19 us: shift(): return lax.ppermute(value, axis, pairs)]
    select_n x9 -> x0, other arithmetic: 3.1 us -> none  [the longest x4 2.61 us: place_moved(): member = jnp.where(position < count, updated, member)]
    another operation x13 -> x0, other arithmetic: 2.76 us -> none  [the longest x2 1.04 us: per_device(): tile_state = to_tiles(jnp.stack([enthalpy, porosity]))]
    div x4 -> x0, other arithmetic: 2.47 us -> none  [liquid(): return jax.nn.sigmoid((values - melt_point) / melt_width)]
    slice x14 -> x0, local copies, waits for them, and re-layouts: 2.42 us -> none  [the longest x5 0.85 us: with_halo(): lax.slice_in_dim(cells, cells.shape[dim] - width, cells.shape[dim], axis=...]
    mul x12 -> x0, other arithmetic: 2.15 us -> none  [the longest x8 1.45 us: neighbour_sum(): 0.5 * (weight[..., 1:] + weight[..., :-1])]
  transfers between devices with their start and end apart: 22 -> 6, of which waited for: 12 -> 5; matrix products, arithmetic and copies ran while one was open for 4% -> 0% of each run, Pallas kernels for 0% -> 0%
where the time goes in v1:
time: 89.1 us; the launch traced here: 88.8 us
  Pallas kernels  54.2 us (61%)
  starting transfers between devices  19.1 us (21%)
  waiting for transfers between devices  12.2 us (14%)
  local copies, waits for them, and re-layouts  2.56 us (3%)
    pallas_call x1, Pallas kernels, per_device(): call(step, 'sssvvvvvv', [tiles, tiles, parcel], [pltpu.VMEM((total, width...  47.4 us
    ppermute x2, starting transfers between devices, swap(): return lax.ppermute(value, axis, [(i, (i + n // 2) % n) for i in range(n)])  9.61 us
    ppermute x4, starting transfers between devices, shift(): return lax.ppermute(value, axis, pairs)  9.45 us
    ppermute x4, waiting for transfers between devices, shift(): return lax.ppermute(value, axis, pairs)  7.19 us
    ppermute x2, waiting for transfers between devices, swap(): return lax.ppermute(value, axis, [(i, (i + n // 2) % n) for i in range(n)])  5.03 us
    unnamed x12, local copies, waits for them, and re-layouts  2.56 us
  transfers between devices with their start and end apart: 6, of which 5 were waited for; matrix products, arithmetic and copies ran while one was open for 0% of the time, Pallas kernels for 0%

profile of v1, /device:TPU:0, one launch (start us, length us, event | category | flops | bytes accessed | tf_op | source)
XLA Modules:
  0.0 88.8 jit_solution(8793105904355211805)
XLA Ops:
  0.6 1.6 %pack_x.1.own_ref = bf16[17,32,128]{2,1,0:T(8,128)(2,1)} custom-call(s32[2,2]{1,0:T(2,128)} %active_ref.3, f32[8,32,128]{2,1,0:T(8,128)} %heat_ref.3, f32[8,32,128]{2,1,0:T(8,128)} %pore_ref.3), custom_call_target="tpu_custom_call" | custom-call | tf_op jit(solution)/shard_map/pack_x/pallas_call | solution.py:259
  2.3 1.3 %collective-permute-start.1 = (bf16[17,32,128]{2,1,0:T(8,128)(2,1)}, bf16[17,32,128]{2,1,0:T(8,128)(2,1)S(1)}, u32[]{:S(2)}, u32[]{:S(2)}) collective-permute-start(bf16[17,32,128]{2,1,0:T(8,128)(2,1)} %pack_x.1.own_ref), channel_id=1, source_target_pairs={{8,0},{16,8},{24,16},{9,1},{17,9},{25,17},{10,2},{18,10},{26,18},{... | collective-permute-start | bytes 417800 | tf_op jit(solution)/shard_map/ppermute | solution.py:243
  3.6 5.6 %collective-permute-start = (bf16[17,32,128]{2,1,0:T(8,128)(2,1)}, bf16[17,32,128]{2,1,0:T(8,128)(2,1)S(1)}, u32[]{:S(2)}, u32[]{:S(2)}) collective-permute-start(bf16[17,32,128]{2,1,0:T(8,128)(2,1)} %pack_x.1.own_ref), channel_id=1, source_target_pairs={{0,8},{8,16},{16,24},{1,9},{9,17},{17,25},{2,10},{10,18},{18,26},{... | collective-permute-start | bytes 417800 | tf_op jit(solution)/shard_map/ppermute | solution.py:243
  9.2 1.9 %collective-permute-done.1.down_ref = bf16[17,32,128]{2,1,0:T(8,128)(2,1)S(1)} collective-permute-done((bf16[17,32,128]{2,1,0:T(8,128)(2,1)}, bf16[17,32,128]{2,1,0:T(8,128)(2,1)S(1)}, u32[]{:S(2)}, u32[]{:S(2)}) %collective-permute-start.1) | collective-permute-done | bytes 139296 | tf_op jit(solution)/shard_map/ppermute | solution.py:243
  11.1 0.0 copy-start
  11.1 1.3 %collective-permute-done.up_ref = bf16[17,32,128]{2,1,0:T(8,128)(2,1)S(1)} collective-permute-done((bf16[17,32,128]{2,1,0:T(8,128)(2,1)}, bf16[17,32,128]{2,1,0:T(8,128)(2,1)S(1)}, u32[]{:S(2)}, u32[]{:S(2)}) %collective-permute-start) | collective-permute-done | bytes 139296 | tf_op jit(solution)/shard_map/ppermute | solution.py:243
  12.4 0.0 copy-done
  12.4 0.0 copy-start.1
  12.4 0.7 copy-done.1
  13.1 1.8 %pack_y.1 = (bf16[51,8,128]{2,1,0:T(8,128)(2,1)}, bf16[51,8,128]{2,1,0:T(8,128)(2,1)}) custom-call(bf16[17,32,128]{2,1,0:T(8,128)(2,1)} %pack_x.1.own_ref, bf16[17,32,128]{2,1,0:T(8,128)(2,1)} %copy-done.1, bf16[17,32,128]{2,1,0:T(8,128)(2,1)} %copy-done), custom_call_target="tpu_custom_call" | custom-call | tf_op jit(solution)/shard_map/pack_y/pallas_call | solution.py:265
  14.8 1.3 %collective-permute-start.2 = (bf16[51,8,128]{2,1,0:T(8,128)(2,1)}, bf16[51,8,128]{2,1,0:T(8,128)(2,1)S(1)}, u32[]{:S(2)}, u32[]{:S(2)}) collective-permute-start(bf16[51,8,128]{2,1,0:T(8,128)(2,1)} %get-tuple-element.9), channel_id=1, source_target_pairs={{0,1},{1,2},{2,3},{3,4},{4,5},{5,6},{6,7},{8,9},{9,10},{10,11},{11... | collective-permute-start | bytes 313352 | tf_op jit(solution)/shard_map/ppermute | solution.py:243
  16.1 1.3 %collective-permute-start.3 = (bf16[51,8,128]{2,1,0:T(8,128)(2,1)}, bf16[51,8,128]{2,1,0:T(8,128)(2,1)S(1)}, u32[]{:S(2)}, u32[]{:S(2)}) collective-permute-start(bf16[51,8,128]{2,1,0:T(8,128)(2,1)} %get-tuple-element.10), channel_id=1, source_target_pairs={{1,0},{2,1},{3,2},{4,3},{5,4},{6,5},{7,6},{9,8},{10,9},{11,10},{12... | collective-permute-start | bytes 313352 | tf_op jit(solution)/shard_map/ppermute | solution.py:243
  17.4 0.0 collective-permute-done.2.left_ref
  17.4 0.0 copy-start.3
  17.4 4.0 %collective-permute-done.3.right_ref = bf16[51,8,128]{2,1,0:T(8,128)(2,1)S(1)} collective-permute-done((bf16[51,8,128]{2,1,0:T(8,128)(2,1)}, bf16[51,8,128]{2,1,0:T(8,128)(2,1)S(1)}, u32[]{:S(2)}, u32[]{:S(2)}) %collective-permute-start.3) | collective-permute-done | bytes 104480 | tf_op jit(solution)/shard_map/ppermute | solution.py:243
  21.4 0.0 copy-start.4
  21.4 0.0 copy-done.3
  21.4 0.6 copy-done.4
  22.0 47.4 %step.1 = (f32[4,4,16,128]{3,2,1,0:T(8,128)}, f32[4,4,16,128]{3,2,1,0:T(8,128)}, s16[2,2,4,16,128]{4,3,2,1,0:T(8,128)(2,1)}) custom-call(s32[2,2]{1,0:T(2,128)} %active_ref.3, s32[2]{0:T(128)} %bitcast.7, s32[2,2]{1,0:T(2,128)} %bitcast.4, f32[8,32,128]{2,1,0:T(8,128)} %heat_ref.3, f32[8,32,128]{2,1,0:T(8,128)} %pore_ref.3, bf16[17,32,128]{2,1,0:T(8,128)(2,1)} %copy-done.1, ...), custom_call_target="tpu_custom_call" | custom-call | tf_op jit(solution)/shard_map/step/pallas_call | solution.py:272
  69.4 3.4 %collective-permute-start.4 = (s16[2,2,4,16,128]{4,3,2,1,0:T(8,128)(2,1)}, s16[2,2,4,16,128]{4,3,2,1,0:T(8,128)(2,1)S(1)}, u32[]{:S(2)}, u32[]{:S(2)}) collective-permute-start(s16[2,2,4,16,128]{4,3,2,1,0:T(8,128)(2,1)} %get-tuple-element.13), channel_id=1, source_target_pairs={{0,16},{8,24},{16,0},{24,8},{1,17},{9,25},{17,1},{25,9},{2,18},{10... | collective-permute-start | bytes 196616 | tf_op jit(solution)/shard_map/ppermute | solution.py:248
  72.8 2.5 %collective-permute-done.4.got_ref.first_ref = s16[2,2,4,16,128]{4,3,2,1,0:T(8,128)(2,1)S(1)} collective-permute-done((s16[2,2,4,16,128]{4,3,2,1,0:T(8,128)(2,1)}, s16[2,2,4,16,128]{4,3,2,1,0:T(8,128)(2,1)S(1)}, u32[]{:S(2)}, u32[]{:S(2)}) %collective-permute-start.4) | collective-permute-done | bytes 65568 | tf_op jit(solution)/shard_map/ppermute | solution.py:248
  75.3 0.0 copy-start.2
  75.3 0.6 copy-done.2
  75.9 1.7 %resend.1 = s16[2,2,4,16,128]{4,3,2,1,0:T(8,128)(2,1)} custom-call(s32[2]{0:T(128)} %bitcast.8, s32[2,2]{1,0:T(2,128)} %bitcast.5, f32[4,4,16,128]{3,2,1,0:T(8,128)} %get-tuple-element.11.heat_ref, f32[4,4,16,128]{3,2,1,0:T(8,128)} %get-tuple-element.12.pore_ref, s16[2,2,4,16,128]{4,3,2,1,0:T(8,128)(2,1)} %copy-done.2), custom_call_target="tpu_custom_call" | custom-call | tf_op jit(solution)/shard_map/resend/pallas_call | solution.py:283
  77.6 6.2 %collective-permute-start.5 = (s16[2,2,4,16,128]{4,3,2,1,0:T(8,128)(2,1)}, s16[2,2,4,16,128]{4,3,2,1,0:T(8,128)(2,1)S(1)}, u32[]{:S(2)}, u32[]{:S(2)}) collective-permute-start(s16[2,2,4,16,128]{4,3,2,1,0:T(8,128)(2,1)} %resend.1), channel_id=1, source_target_pairs={{0,4},{1,5},{2,6},{3,7},{4,0},{5,1},{6,2},{7,3},{8,12},{9,13},{10,... | collective-permute-start | bytes 196616 | tf_op jit(solution)/shard_map/ppermute | solution.py:248
  83.8 2.6 %collective-permute-done.5.second_ref = s16[2,2,4,16,128]{4,3,2,1,0:T(8,128)(2,1)S(1)} collective-permute-done((s16[2,2,4,16,128]{4,3,2,1,0:T(8,128)(2,1)}, s16[2,2,4,16,128]{4,3,2,1,0:T(8,128)(2,1)S(1)}, u32[]{:S(2)}, u32[]{:S(2)}) %collective-permute-start.5) | collective-permute-done | bytes 65568 | tf_op jit(solution)/shard_map/ppermute | solution.py:248
  86.4 0.0 copy-start.5
  86.4 0.6 copy-done.5
  87.0 1.8 %place.1 = (f32[4,4,16,128]{3,2,1,0:T(8,128)}, f32[4,4,16,128]{3,2,1,0:T(8,128)}) custom-call(s32[2]{0:T(128)} %bitcast.9, s32[2,2]{1,0:T(2,128)} %bitcast.6, f32[4,4,16,128]{3,2,1,0:T(8,128)} %get-tuple-element.11.heat_ref, f32[4,4,16,128]{3,2,1,0:T(8,128)} %get-tuple-element.12.pore_ref, s16[2,2,4,16,128]{4,3,2,1,0:T(8,128)(2,1)} %copy-done.2, ...), custom_call_target="tpu_custom_call" | custom-call | tf_op jit(solution)/shard_map/place/pallas_call | solution.py:285
Async XLA Ops:
  2.3 8.8 %collective-permute-start.1 = (bf16[17,32,128]{2,1,0:T(8,128)(2,1)}, bf16[17,32,128]{2,1,0:T(8,128)(2,1)S(1)}, u32[]{:S(2)}, u32[]{:S(2)}) collective-permute-start(bf16[17,32,128]{2,1,0:T(8,128)(2,1)} %pack_x.1.own_ref), channel_id=1, source_target_pairs={{8,0},{16,8},{24,16},{9,1},{17,9},{25,17},{10,2},{18,10},{26,18},{... | collective-permute-start | bytes 417800 | tf_op jit(solution)/shard_map/ppermute | solution.py:243
  3.6 8.8 %collective-permute-start = (bf16[17,32,128]{2,1,0:T(8,128)(2,1)}, bf16[17,32,128]{2,1,0:T(8,128)(2,1)S(1)}, u32[]{:S(2)}, u32[]{:S(2)}) collective-permute-start(bf16[17,32,128]{2,1,0:T(8,128)(2,1)} %pack_x.1.own_ref), channel_id=1, source_target_pairs={{0,8},{8,16},{16,24},{1,9},{9,17},{17,25},{2,10},{10,18},{18,26},{... | collective-permute-start | bytes 417800 | tf_op jit(solution)/shard_map/ppermute | solution.py:243
  11.1 1.3 %copy-start = (bf16[17,32,128]{2,1,0:T(8,128)(2,1)}, bf16[17,32,128]{2,1,0:T(8,128)(2,1)S(1)}, u32[]{:S(2)}) copy-start(bf16[17,32,128]{2,1,0:T(8,128)(2,1)S(1)} %collective-permute-done.1.down_ref) | copy-start | bytes 417796
  12.4 0.7 copy-start.1
  14.8 2.6 %collective-permute-start.2 = (bf16[51,8,128]{2,1,0:T(8,128)(2,1)}, bf16[51,8,128]{2,1,0:T(8,128)(2,1)S(1)}, u32[]{:S(2)}, u32[]{:S(2)}) collective-permute-start(bf16[51,8,128]{2,1,0:T(8,128)(2,1)} %get-tuple-element.9), channel_id=1, source_target_pairs={{0,1},{1,2},{2,3},{3,4},{4,5},{5,6},{6,7},{8,9},{9,10},{10,11},{11... | collective-permute-start | bytes 313352 | tf_op jit(solution)/shard_map/ppermute | solution.py:243
  16.1 5.3 %collective-permute-start.3 = (bf16[51,8,128]{2,1,0:T(8,128)(2,1)}, bf16[51,8,128]{2,1,0:T(8,128)(2,1)S(1)}, u32[]{:S(2)}, u32[]{:S(2)}) collective-permute-start(bf16[51,8,128]{2,1,0:T(8,128)(2,1)} %get-tuple-element.10), channel_id=1, source_target_pairs={{1,0},{2,1},{3,2},{4,3},{5,4},{6,5},{7,6},{9,8},{10,9},{11,10},{12... | collective-permute-start | bytes 313352 | tf_op jit(solution)/shard_map/ppermute | solution.py:243
  17.4 4.0 %copy-start.3 = (bf16[51,8,128]{2,1,0:T(8,128)(2,1)}, bf16[51,8,128]{2,1,0:T(8,128)(2,1)S(1)}, u32[]{:S(2)}) copy-start(bf16[51,8,128]{2,1,0:T(8,128)(2,1)S(1)} %collective-permute-done.2.left_ref) | copy-start | bytes 313348
  21.4 0.6 copy-start.4
  69.4 5.8 %collective-permute-start.4 = (s16[2,2,4,16,128]{4,3,2,1,0:T(8,128)(2,1)}, s16[2,2,4,16,128]{4,3,2,1,0:T(8,128)(2,1)S(1)}, u32[]{:S(2)}, u32[]{:S(2)}) collective-permute-start(s16[2,2,4,16,128]{4,3,2,1,0:T(8,128)(2,1)} %get-tuple-element.13), channel_id=1, source_target_pairs={{0,16},{8,24},{16,0},{24,8},{1,17},{9,25},{17,1},{25,9},{2,18},{10... | collective-permute-start | bytes 196616 | tf_op jit(solution)/shard_map/ppermute | solution.py:248
  75.3 0.6 copy-start.2
  77.6 8.8 %collective-permute-start.5 = (s16[2,2,4,16,128]{4,3,2,1,0:T(8,128)(2,1)}, s16[2,2,4,16,128]{4,3,2,1,0:T(8,128)(2,1)S(1)}, u32[]{:S(2)}, u32[]{:S(2)}) collective-permute-start(s16[2,2,4,16,128]{4,3,2,1,0:T(8,128)(2,1)} %resend.1), channel_id=1, source_target_pairs={{0,4},{1,5},{2,6},{3,7},{4,0},{5,1},{6,2},{7,3},{8,12},{9,13},{10,... | collective-permute-start | bytes 196616 | tf_op jit(solution)/shard_map/ppermute | solution.py:248
  86.4 0.6 copy-start.5

commit v2 on v1

v2 whole, which is shorter than its diff:
```python
import functools

import jax
import jax.numpy as jnp
from jax import lax
from jax.experimental import pallas as pl
from jax.experimental.pallas import tpu as pltpu
from jax.sharding import PartitionSpec as P

PAIRS = 4
DEEP = 2 * PAIRS
SUB = 8
LANES = 128
VMEM_LIMIT = 16 * 2**20

HEAT_SCALE = 25000.0
HEAT_SHIFT = 32000.0
PORE_SCALE = 40000.0
PORE_SHIFT = 7000.0


def encode(values, scale, shift):
    return jnp.floor(values * scale + (0.5 - shift)).astype(jnp.int32).astype(jnp.int16)


def decode(codes, scale, shift):
    return (codes.astype(jnp.int32).astype(jnp.float32) + shift) * (1.0 / scale)


def tile_slice(slot, tx, ty):
    return pl.ds((slot // 2) * tx, tx), pl.ds((slot % 2) * ty, ty)


def flag_rows(active_ref, cols):
    lane = lax.broadcasted_iota(jnp.int32, (cols, LANES), 1)
    col = lax.broadcasted_iota(jnp.int32, (cols, LANES), 0)

    def flag(i):
        return jnp.where(col < cols // 2, active_ref[i, 0], active_ref[i, 1])

    return jnp.where(lane < LANES // 2, flag(0), flag(1)).astype(jnp.float32)


def pack_x(active_ref, heat_ref, pore_ref, out_ref, heat_out, pore_out):
    rows, cols = heat_ref.shape[0], heat_ref.shape[1]
    heat_out[...] = heat_ref[...]
    pore_out[...] = pore_ref[...]
    out_ref[0:rows] = heat_ref[...].astype(jnp.bfloat16)
    out_ref[rows : 2 * rows] = pore_ref[...].astype(jnp.bfloat16)
    out_ref[2 * rows] = flag_rows(active_ref, cols).astype(jnp.bfloat16)


def x_parts(own_ref, near_ref, far_ref):
    odd = lax.rem(lax.axis_index("gx"), 2)
    return ((2 - 2 * odd, near_ref), (1, own_ref), (2 * odd, far_ref))


def pack_y(own_ref, near_ref, far_ref, near_out, far_out):
    rows = (own_ref.shape[0] - 1) // 2
    cols = own_ref.shape[1]
    odd = lax.rem(lax.axis_index("gy"), 2)
    edge = cols - DEEP
    for out_ref, start in ((near_out, edge - edge * odd), (far_out, edge * odd)):
        at = pl.ds(pl.multiple_of(start, DEEP), DEEP)
        for i, part in x_parts(own_ref, near_ref, far_ref):
            for f in range(2):
                out_ref[pl.ds((3 * f + i) * rows, rows)] = part[pl.ds(f * rows, rows), at, :]
            out_ref[6 * rows + i] = part[2 * rows, at, :]


def step(
    active_ref, slot_ref, heat_ref, pore_ref, xn_ref, xf_ref, yn_ref, yf_ref,
    heat_out, pore_out, send_ref, wide, hs, qa, qb, vs, ks, vz, wz, ms,
):
    rows, cols = heat_ref.shape[0], heat_ref.shape[1]
    tx, ty = rows // 2, cols // 2
    total = rows + 2 * DEEP
    width = cols + 2 * DEEP
    n = width // SUB
    span = range(n)
    lane = lax.broadcasted_iota(jnp.int32, (SUB, LANES), 1)
    lane_open = lane < LANES - 1
    low_half = lane < LANES // 2
    f32 = jnp.float32
    odd = lax.rem(lax.axis_index("gy"), 2)
    edge = width - DEEP
    y_parts = (
        (pl.ds(pl.multiple_of(edge - edge * odd, DEEP), DEEP), yn_ref),
        (pl.ds(pl.multiple_of(edge * odd, DEEP), DEEP), yf_ref),
    )
    own = pl.ds(DEEP, cols)

    for i, part in x_parts(None, xn_ref, xf_ref):
        mid = flag_rows(active_ref, cols) if part is None else part[2 * rows].astype(f32)
        wide[i, own, :] = mid
    for at, part in y_parts:
        for i in range(3):
            wide[i, at, :] = part[6 * rows + i].astype(f32)
    for i in range(3):
        for j in span:
            f = wide[i, pl.ds(j, SUB, stride=n), :]
            r = pltpu.roll(f, LANES // 2, 1)
            ms[2 * i, j] = jnp.where(low_half, f, r)
            ms[2 * i + 1, j] = jnp.where(low_half, r, f)

    for field, own_ref, into in ((0, heat_ref, hs), (1, pore_ref, qa)):
        for i, part in x_parts(None, xn_ref, xf_ref):
            for r in range(rows):
                mid = own_ref[r] if part is None else part[field * rows + r].astype(f32)
                wide[i * rows + r, own, :] = mid
        for at, part in y_parts:
            for x in range(total):
                wide[x, at, :] = part[field * total + x].astype(f32)
        for x in range(total):
            for j in span:
                v = wide[x, pl.ds(j, SUB, stride=n), :]
                into[x, j] = 2.0 * v - 2.0 if field == 0 else v

    def beside(x, j, v, w):
        vz[x, j] = pltpu.roll(v, LANES - 1, 1)
        wz[x, j] = pltpu.roll(w, LANES - 1, 1)

    def along_depth(val, lo, hi):
        for x in range(lo, hi):
            for j in span:
                f = (ks[x, j] + wz[x, j]) * (vz[x, j] - val[x, j])
                f = jnp.where(lane_open, f, 0.0)
                vz[x, j] = f - pltpu.roll(f, 1, 1)

    def across(val, lo, hi, finish):
        prev = [(ks[lo - 1, j] + ks[lo, j]) * (val[lo, j] - val[lo - 1, j]) for j in span]
        for x in range(lo, hi):
            v = [val[x, j] for j in span]
            w = [ks[x, j] for j in span]
            down = [(w[j] + ks[x + 1, j]) * (val[x + 1, j] - v[j]) for j in span]
            flux = [(w[j] + w[j + 1]) * (v[j + 1] - v[j]) for j in range(n - 1)]
            flux.append(
                (w[n - 1] + pltpu.roll(w[0], SUB - 1, 0)) * (pltpu.roll(v[0], SUB - 1, 0) - v[n - 1])
            )
            left = [pltpu.roll(flux[-1], 1, 0)] + flux[:-1]
            for j in span:
                acc = (down[j] - prev[j]) + (flux[j] - left[j]) + vz[x, j]
                finish(x, j, v[j], w[j], acc)
            prev = down

    q, q_next = qa, qb
    for p in range(PAIRS):
        lo, hi = 2 * p, total - 2 * p
        for x in range(lo, hi):
            for j in span:
                h = hs[x, j]
                t = jnp.tanh(h)
                solid = 1.0 - q[x, j]
                k = solid * solid * (t + 7.0 / 3.0)
                v = h - 0.4 * t
                ks[x, j] = k
                vs[x, j] = v
                beside(x, j, v, k)
        along_depth(vs, lo + 1, hi - 1)

        def warm(x, j, v, w, acc):
            hs[x, j] = hs[x, j] + (0.0225 * ms[x // tx, j]) * acc

        across(vs, lo + 1, hi - 1, warm)
        for x in range(lo + 1, hi - 1):
            for j in span:
                g = hs[x, j]
                rate = 1.0 + jnp.tanh(2.5 * g - jnp.tanh(g))
                ks[x, j] = rate
                beside(x, j, q[x, j], rate)
        along_depth(q, lo + 2, hi - 2)

        def fill(x, j, v, w, acc, q_next=q_next):
            q_next[x, j] = v + (0.0375 * ms[x // tx, j]) * (acc - 4.0 * w * v)

        across(q, lo + 2, hi - 2, fill)
        q, q_next = q_next, q

    for src, out, field in ((hs, heat_out, 0), (q, pore_out, 1)):
        for r in range(rows):
            for j in span:
                v = src[DEEP + r, j]
                wide[r, pl.ds(j, SUB, stride=n), :] = 0.5 * v + 1.0 if field == 0 else v
        for i in range(2):
            for k in range(2):
                out[2 * i + k] = wide[i * tx : (i + 1) * tx, DEEP + k * ty : DEEP + (k + 1) * ty, :]
    for k in range(slot_ref.shape[1]):
        s = slot_ref[0, k]
        send_ref[k, 0] = encode(heat_out[s], HEAT_SCALE, HEAT_SHIFT)
        send_ref[k, 1] = encode(pore_out[s], PORE_SCALE, PORE_SHIFT)


def resend(count_ref, slot_ref, heat_ref, pore_ref, got_ref, send_ref):
    ranks = slot_ref.shape[1]
    for k in range(ranks):
        s = slot_ref[1, k]
        send_ref[k, 0] = encode(heat_ref[s], HEAT_SCALE, HEAT_SHIFT)
        send_ref[k, 1] = encode(pore_ref[s], PORE_SCALE, PORE_SHIFT)
        for r in range(ranks):

            @pl.when((r < count_ref[0]) & (slot_ref[0, r] == s))
            def _():
                send_ref[k] = got_ref[r]


def place(count_ref, slot_ref, heat_ref, pore_ref, first_ref, second_ref, heat_out, pore_out):
    ranks = slot_ref.shape[1]
    heat_out[...] = heat_ref[...]
    pore_out[...] = pore_ref[...]
    for i, got_ref in ((0, first_ref), (1, second_ref)):
        for r in range(ranks):

            @pl.when(r < count_ref[i])
            def _():
                s = slot_ref[i, r]
                heat_out[s] = decode(got_ref[r, 0], HEAT_SCALE, HEAT_SHIFT)
                pore_out[s] = decode(got_ref[r, 1], PORE_SCALE, PORE_SHIFT)


def call(body, spec, outs, scratch=(), name=None, out_space=pltpu.VMEM):
    def run(*args):
        space = {"s": pltpu.SMEM, "v": pltpu.VMEM, "V": pltpu.VMEM}
        args = [
            pltpu.with_memory_space_constraint(a, pltpu.VMEM) if c == "V" else a
            for c, a in zip(spec, args)
        ]
        shapes = [
            pltpu.VMEM(s, d) if out_space is not None else jax.ShapeDtypeStruct(s, d)
            for s, d in outs
        ]
        return pl.pallas_call(
            body,
            in_specs=[pl.BlockSpec(memory_space=space[c]) for c in spec],
            out_specs=[pl.BlockSpec(memory_space=pltpu.VMEM) for _ in outs],
            out_shape=shapes,
            scratch_shapes=list(scratch),
            compiler_params=pltpu.CompilerParams(vmem_limit_bytes=VMEM_LIMIT),
            name=name,
        )(*args)

    return run


def exchange(near, far, axis):
    n = lax.axis_size(axis)
    near_pairs = [(i, i ^ 1) for i in range(n) if i ^ 1 < n]
    far_pairs = [(i, ((i + 1) ^ 1) - 1) for i in range(1, n) if ((i + 1) ^ 1) - 1 < n]
    far = lax.ppermute(far, axis, far_pairs)
    near = lax.ppermute(near, axis, near_pairs)
    return near, far


def swap(value, axis):
    n = lax.axis_size(axis)
    return lax.ppermute(value, axis, [(i, (i + n // 2) % n) for i in range(n)])


def per_device(enthalpy, porosity, active, move_count, move_slot):
    rows, cols, depth = enthalpy.shape
    tx, ty = rows // 2, cols // 2
    count = move_count.reshape(2)
    slots = move_slot.reshape(2, move_slot.shape[-1])
    ranks = slots.shape[1]
    f32, bf16, i16 = jnp.float32, jnp.bfloat16, jnp.int16

    block = ((rows, cols, depth), f32)
    own, enthalpy, porosity = call(
        pack_x, "svv", [((2 * rows + 1, cols, depth), bf16), block, block], name="pack_x"
    )(active, enthalpy, porosity)
    x_near, x_far = exchange(own, own, "gx")
    side = ((6 * rows + 3, DEEP, depth), bf16)
    near, far = call(pack_y, "VVV", [side, side], name="pack_y")(own, x_near, x_far)
    y_near, y_far = exchange(near, far, "gy")
    total, width = rows + 2 * DEEP, cols + 2 * DEEP
    tiles = ((4, tx, ty, depth), f32)
    parcel = ((ranks, 2, tx, ty, depth), i16)
    split = pltpu.VMEM((total, width // SUB, SUB, depth), f32)
    heat, pore, first = call(
        step, "ssVVVVVV", [tiles, tiles, parcel],
        [pltpu.VMEM((total, width, depth), f32)]
        + [split] * 7
        + [pltpu.VMEM((total // tx, width // SUB, SUB, depth), f32)],
        name="step",
    )(active, slots, enthalpy, porosity, x_near, x_far, y_near, y_far)
    first = swap(first, "gx")
    (second,) = call(resend, "ssVVV", [parcel], name="resend")(count, slots, heat, pore, first)
    second = swap(second, "gy")
    heat, pore = call(place, "ssVVVV", [tiles, tiles], name="place", out_space=None)(
        count, slots, heat, pore, first, second
    )
    return heat[None, None], pore[None, None]


def solution(mesh):
    placed = (
        P("gx", "gy", None),
        P("gx", "gy", None),
        P("gx", "gy"),
        P("gx", "gy", None),
        P("gx", "gy", None, None),
    )
    out = P("gx", "gy", None, None, None, None)
    return jax.shard_map(
        per_device, mesh=mesh, in_specs=placed, out_specs=(out, out), check_vma=False
    )
```

time: 89.1 us -> 38.2 us (0.43)
  Pallas kernels: 54.2 us -> 6.59 us
  waiting for transfers between devices: 12.2 us -> 9.8 us
  starting transfers between devices: 19.1 us -> 17 us
  local copies, waits for them, and re-layouts: 2.56 us -> 3.81 us
    pallas_call x5, Pallas kernels: 54.2 us -> 6.59 us  [run(): pl.pallas_call(body, in_specs=[pl.BlockSpec(memory_space=space[c]) for c...]
    ppermute x4, waiting for transfers between devices: 7.19 us -> 4.02 us  [the longest x2 4.01 us: exchange(): near = lax.ppermute(near, axis, near_pairs)]
    ppermute x4, starting transfers between devices: 9.45 us -> 7.34 us  [the longest x2 6 us: exchange(): near = lax.ppermute(near, axis, near_pairs)]
    unnamed x12 -> x10, local copies, waits for them, and re-layouts: 2.56 us -> 3.81 us
  transfers between devices with their start and end apart: 6 -> 6, of which waited for: 5 -> 4; matrix products, arithmetic and copies ran while one was open for 0% -> 0% of each run, Pallas kernels for 0% -> 0%
where the time goes in v2:
time: 38.2 us; the launch traced here: 37.9 us
  starting transfers between devices  17 us (45%)
  waiting for transfers between devices  9.8 us (26%)
  Pallas kernels  6.59 us (17%)
  local copies, waits for them, and re-layouts  3.81 us (10%)
  between operations  0.7 us (2%)
    ppermute x2, starting transfers between devices, swap(): return lax.ppermute(value, axis, [(i, (i + n // 2) % n) for i in range(n)])  9.7 us
    pallas_call x5, Pallas kernels, run(): pl.pallas_call(body, in_specs=[pl.BlockSpec(memory_space=space[c]) for c...  6.59 us
    ppermute x2, starting transfers between devices, exchange(): near = lax.ppermute(near, axis, near_pairs)  6 us
    ppermute x2, waiting for transfers between devices, swap(): return lax.ppermute(value, axis, [(i, (i + n // 2) % n) for i in range(n)])  5.78 us
    ppermute x2, waiting for transfers between devices, exchange(): near = lax.ppermute(near, axis, near_pairs)  4.01 us
    unnamed x10, local copies, waits for them, and re-layouts  3.81 us
    ppermute x2, starting transfers between devices, exchange(): far = lax.ppermute(far, axis, far_pairs)  1.34 us
  transfers between devices with their start and end apart: 6, of which 4 were waited for; matrix products, arithmetic and copies ran while one was open for 0% of the time, Pallas kernels for 0%

profile of v2, /device:TPU:0, one launch (start us, length us, event | category | flops | bytes accessed | tf_op | source)
XLA Modules:
  0.0 37.9 jit_solution(7444343456042655941)
XLA Ops:
  0.6 0.0 copy-start
  0.6 0.9 %copy-done = f32[8,32,128]{2,1,0:T(8,128)S(1)} copy-done((f32[8,32,128]{2,1,0:T(8,128)S(1)}, f32[8,32,128]{2,1,0:T(8,128)}, u32[]{:S(2)}) %copy-start) | copy-done | bytes 131096
  1.5 0.0 copy-start.1
  1.5 0.9 %copy-done.1 = f32[8,32,128]{2,1,0:T(8,128)S(1)} copy-done((f32[8,32,128]{2,1,0:T(8,128)S(1)}, f32[8,32,128]{2,1,0:T(8,128)}, u32[]{:S(2)}) %copy-start.1) | copy-done | bytes 131096
  2.4 0.0 copy-start.3
  2.4 0.7 %copy-done.3 = s32[2,2]{1,0:T(2,128)S(1)} copy-done((s32[2,2]{1,0:T(2,128)S(1)}, s32[2,2]{1,0:T(2,128)}, u32[]{:S(2)}) %copy-start.3) | copy-done | bytes 40
  3.1 0.6 %pack_x.1 = (bf16[17,32,128]{2,1,0:T(8,128)(2,1)S(1)}, f32[8,32,128]{2,1,0:T(8,128)S(1)}, f32[8,32,128]{2,1,0:T(8,128)S(1)}) custom-call(s32[2,2]{1,0:T(2,128)S(1)} %copy-done.3, f32[8,32,128]{2,1,0:T(8,128)S(1)} %copy-done, f32[8,32,128]{2,1,0:T(8,128)S(1)} %copy-done.1), custom_call_target="tpu_custom_call" | custom-call | tf_op jit(solution)/shard_map/pack_x/pallas_call | solution.py:231
  3.7 0.7 %collective-permute-start.1 = (bf16[17,32,128]{2,1,0:T(8,128)(2,1)S(1)}, bf16[17,32,128]{2,1,0:T(8,128)(2,1)S(1)}, u32[]{:S(2)}, u32[]{:S(2)}) collective-permute-start(bf16[17,32,128]{2,1,0:T(8,128)(2,1)S(1)} %get-tuple-element.14.own_ref), channel_id=1, source_target_pairs={{8,16},{16,8},{9,17},{17,9},{10,18},{18,10},{11,19},{19,11},{12,20... | collective-permute-start | bytes 417800 | tf_op jit(solution)/shard_map/ppermute | solution.py:248
  4.4 5.9 %collective-permute-start = (bf16[17,32,128]{2,1,0:T(8,128)(2,1)S(1)}, bf16[17,32,128]{2,1,0:T(8,128)(2,1)S(1)}, u32[]{:S(2)}, u32[]{:S(2)}) collective-permute-start(bf16[17,32,128]{2,1,0:T(8,128)(2,1)S(1)} %get-tuple-element.14.own_ref), channel_id=1, source_target_pairs={{0,8},{8,0},{16,24},{24,16},{1,9},{9,1},{17,25},{25,17},{2,10},{10... | collective-permute-start | bytes 417800 | tf_op jit(solution)/shard_map/ppermute | solution.py:249
  10.3 0.0 collective-permute-done.1.far_ref.xf_ref
  10.3 3.4 %collective-permute-done.near_ref.xn_ref = bf16[17,32,128]{2,1,0:T(8,128)(2,1)S(1)} collective-permute-done((bf16[17,32,128]{2,1,0:T(8,128)(2,1)S(1)}, bf16[17,32,128]{2,1,0:T(8,128)(2,1)S(1)}, u32[]{:S(2)}, u32[]{:S(2)}) %collective-permute-start) | collective-permute-done | bytes 139296 | tf_op jit(solution)/shard_map/ppermute | solution.py:249
  13.7 0.1 collective-permute-start.2
  13.8 0.7 %collective-permute-start.3 = (bf16[51,8,128]{2,1,0:T(8,128)(2,1)S(1)}, bf16[51,8,128]{2,1,0:T(8,128)(2,1)S(1)}, u32[]{:S(2)}, u32[]{:S(2)}) collective-permute-start(bf16[51,8,128]{2,1,0:T(8,128)(2,1)S(1)} %get-tuple-element.16), channel_id=1, source_target_pairs={{1,2},{2,1},{3,4},{4,3},{5,6},{6,5},{9,10},{10,9},{11,12},{12,11},... | collective-permute-start | bytes 313352 | tf_op jit(solution)/shard_map/ppermute | solution.py:248
  14.5 0.6 %collective-permute-done.2.yn_ref = bf16[51,8,128]{2,1,0:T(8,128)(2,1)S(1)} collective-permute-done((bf16[51,8,128]{2,1,0:T(8,128)(2,1)S(1)}, bf16[51,8,128]{2,1,0:T(8,128)(2,1)S(1)}, u32[]{:S(2)}, u32[]{:S(2)}) %collective-permute-start.2) | collective-permute-done | bytes 104480 | tf_op jit(solution)/shard_map/ppermute | solution.py:249
  15.1 0.0 collective-permute-done.3.yf_ref
  15.1 0.0 copy-start.2
  15.1 0.7 %copy-done.2 = s32[1,1,2,2]{3,2,1,0:T(2,128)S(1)} copy-done((s32[1,1,2,2]{3,2,1,0:T(2,128)S(1)}, s32[1,1,2,2]{3,2,1,0:T(2,128)}, u32[]{:S(2)}) %copy-start.2) | copy-done | bytes 40
  15.8 4.0 %step.1 = (f32[4,4,16,128]{3,2,1,0:T(8,128)S(1)}, f32[4,4,16,128]{3,2,1,0:T(8,128)S(1)}, s16[2,2,4,16,128]{4,3,2,1,0:T(8,128)(2,1)S(1)}) custom-call(s32[2,2]{1,0:T(2,128)S(1)} %copy-done.3, s32[2,2]{1,0:T(2,128)S(1)} %bitcast.4, f32[8,32,128]{2,1,0:T(8,128)S(1)} %get-tuple-element.12.heat_ref, f32[8,32,128]{2,1,0:T(8,128)S(1)} %get-tuple-element.13.pore_ref, ...), custom_call_target="tpu_custom_call" | custom-call | tf_op jit(solution)/shard_map/step/pallas_call | solution.py:231
  19.9 1.7 %collective-permute-start.4 = (s16[2,2,4,16,128]{4,3,2,1,0:T(8,128)(2,1)S(1)}, s16[2,2,4,16,128]{4,3,2,1,0:T(8,128)(2,1)S(1)}, u32[]{:S(2)}, u32[]{:S(2)}) collective-permute-start(s16[2,2,4,16,128]{4,3,2,1,0:T(8,128)(2,1)S(1)} %get-tuple-element.19), channel_id=1, source_target_pairs={{0,16},{8,24},{16,0},{24,8},{1,17},{9,25},{17,1},{25,9},{2,18},{10... | collective-permute-start | bytes 196616 | tf_op jit(solution)/shard_map/ppermute | solution.py:255
  21.6 3.5 %collective-permute-done.4.got_ref.first_ref = s16[2,2,4,16,128]{4,3,2,1,0:T(8,128)(2,1)S(1)} collective-permute-done((s16[2,2,4,16,128]{4,3,2,1,0:T(8,128)(2,1)S(1)}, s16[2,2,4,16,128]{4,3,2,1,0:T(8,128)(2,1)S(1)}, u32[]{:S(2)}, u32[]{:S(2)}) %collective-permute-start.4) | collective-permute-done | bytes 65568 | tf_op jit(solution)/shard_map/ppermute | solution.py:255
  25.1 0.0 copy-start.4
  25.1 0.7 %copy-done.4 = s32[1,1,2]{2,1,0:T(1,128)S(1)} copy-done((s32[1,1,2]{2,1,0:T(1,128)S(1)}, s32[1,1,2]{2,1,0:T(1,128)}, u32[]{:S(2)}) %copy-start.4) | copy-done | bytes 32
  25.7 0.6 %resend.1 = s16[2,2,4,16,128]{4,3,2,1,0:T(8,128)(2,1)S(1)} custom-call(s32[2]{0:T(128)S(1)} %bitcast.7, s32[2,2]{1,0:T(2,128)S(1)} %bitcast.5, f32[4,4,16,128]{3,2,1,0:T(8,128)S(1)} %get-tuple-element.17.heat_ref, f32[4,4,16,128]{3,2,1,0:T(8,128)S(1)} %get-tuple-element.18.pore_ref, s16[2,2,4,16,128]{4,3,2,1,0:T(8,128)(2,1)S(1)} %collective-permute-done.4.got_ref.first_ref), custom_call_target="tpu_custom_call" | custom-call | tf_op jit(solution)/shard_map/resend/pallas_call | solution.py:231
  26.4 8.0 %collective-permute-start.5 = (s16[2,2,4,16,128]{4,3,2,1,0:T(8,128)(2,1)S(1)}, s16[2,2,4,16,128]{4,3,2,1,0:T(8,128)(2,1)S(1)}, u32[]{:S(2)}, u32[]{:S(2)}) collective-permute-start(s16[2,2,4,16,128]{4,3,2,1,0:T(8,128)(2,1)S(1)} %resend.1), channel_id=1, source_target_pairs={{0,4},{1,5},{2,6},{3,7},{4,0},{5,1},{6,2},{7,3},{8,12},{9,13},{10,... | collective-permute-start | bytes 196616 | tf_op jit(solution)/shard_map/ppermute | solution.py:255
  34.4 2.2 %collective-permute-done.5.second_ref = s16[2,2,4,16,128]{4,3,2,1,0:T(8,128)(2,1)S(1)} collective-permute-done((s16[2,2,4,16,128]{4,3,2,1,0:T(8,128)(2,1)S(1)}, s16[2,2,4,16,128]{4,3,2,1,0:T(8,128)(2,1)S(1)}, u32[]{:S(2)}, u32[]{:S(2)}) %collective-permute-start.5) | collective-permute-done | bytes 65568 | tf_op jit(solution)/shard_map/ppermute | solution.py:255
  36.6 1.3 %place.1 = (f32[4,4,16,128]{3,2,1,0:T(8,128)}, f32[4,4,16,128]{3,2,1,0:T(8,128)}) custom-call(s32[2]{0:T(128)S(1)} %bitcast.8, s32[2,2]{1,0:T(2,128)S(1)} %bitcast.6, f32[4,4,16,128]{3,2,1,0:T(8,128)S(1)} %get-tuple-element.17.heat_ref, f32[4,4,16,128]{3,2,1,0:T(8,128)S(1)} %get-tuple-element.18.pore_ref, ...), custom_call_target="tpu_custom_call" | custom-call | tf_op jit(solution)/shard_map/place/pallas_call | solution.py:231
  (1 shorter events, 0.0 us)
Async XLA Ops:
  0.6 0.9 %copy-start = (f32[8,32,128]{2,1,0:T(8,128)S(1)}, f32[8,32,128]{2,1,0:T(8,128)}, u32[]{:S(2)}) copy-start(f32[8,32,128]{2,1,0:T(8,128)} %heat_ref.1) | copy-start | bytes 393220
  1.5 0.9 %copy-start.1 = (f32[8,32,128]{2,1,0:T(8,128)S(1)}, f32[8,32,128]{2,1,0:T(8,128)}, u32[]{:S(2)}) copy-start(f32[8,32,128]{2,1,0:T(8,128)} %pore_ref.1) | copy-start | bytes 393220
  2.4 0.7 %copy-start.3 = (s32[2,2]{1,0:T(2,128)S(1)}, s32[2,2]{1,0:T(2,128)}, u32[]{:S(2)}) copy-start(s32[2,2]{1,0:T(2,128)} %active_ref.3) | copy-start | bytes 52
  3.7 6.6 %collective-permute-start.1 = (bf16[17,32,128]{2,1,0:T(8,128)(2,1)S(1)}, bf16[17,32,128]{2,1,0:T(8,128)(2,1)S(1)}, u32[]{:S(2)}, u32[]{:S(2)}) collective-permute-start(bf16[17,32,128]{2,1,0:T(8,128)(2,1)S(1)} %get-tuple-element.14.own_ref), channel_id=1, source_target_pairs={{8,16},{16,8},{9,17},{17,9},{10,18},{18,10},{11,19},{19,11},{12,20... | collective-permute-start | bytes 417800 | tf_op jit(solution)/shard_map/ppermute | solution.py:248
  4.4 9.3 %collective-permute-start = (bf16[17,32,128]{2,1,0:T(8,128)(2,1)S(1)}, bf16[17,32,128]{2,1,0:T(8,128)(2,1)S(1)}, u32[]{:S(2)}, u32[]{:S(2)}) collective-permute-start(bf16[17,32,128]{2,1,0:T(8,128)(2,1)S(1)} %get-tuple-element.14.own_ref), channel_id=1, source_target_pairs={{0,8},{8,0},{16,24},{24,16},{1,9},{9,1},{17,25},{25,17},{2,10},{10... | collective-permute-start | bytes 417800 | tf_op jit(solution)/shard_map/ppermute | solution.py:249
  13.7 1.4 %collective-permute-start.2 = (bf16[51,8,128]{2,1,0:T(8,128)(2,1)S(1)}, bf16[51,8,128]{2,1,0:T(8,128)(2,1)S(1)}, u32[]{:S(2)}, u32[]{:S(2)}) collective-permute-start(bf16[51,8,128]{2,1,0:T(8,128)(2,1)S(1)} %get-tuple-element.15), channel_id=1, source_target_pairs={{0,1},{1,0},{2,3},{3,2},{4,5},{5,4},{6,7},{7,6},{8,9},{9,8},{10,11... | collective-permute-start | bytes 313352 | tf_op jit(solution)/shard_map/ppermute | solution.py:249
  13.8 1.3 %collective-permute-start.3 = (bf16[51,8,128]{2,1,0:T(8,128)(2,1)S(1)}, bf16[51,8,128]{2,1,0:T(8,128)(2,1)S(1)}, u32[]{:S(2)}, u32[]{:S(2)}) collective-permute-start(bf16[51,8,128]{2,1,0:T(8,128)(2,1)S(1)} %get-tuple-element.16), channel_id=1, source_target_pairs={{1,2},{2,1},{3,4},{4,3},{5,6},{6,5},{9,10},{10,9},{11,12},{12,11},... | collective-permute-start | bytes 313352 | tf_op jit(solution)/shard_map/ppermute | solution.py:248
  15.1 0.7 %copy-start.2 = (s32[1,1,2,2]{3,2,1,0:T(2,128)S(1)}, s32[1,1,2,2]{3,2,1,0:T(2,128)}, u32[]{:S(2)}) copy-start(s32[1,1,2,2]{3,2,1,0:T(2,128)} %param.9) | copy-start | bytes 52
  19.9 5.2 %collective-permute-start.4 = (s16[2,2,4,16,128]{4,3,2,1,0:T(8,128)(2,1)S(1)}, s16[2,2,4,16,128]{4,3,2,1,0:T(8,128)(2,1)S(1)}, u32[]{:S(2)}, u32[]{:S(2)}) collective-permute-start(s16[2,2,4,16,128]{4,3,2,1,0:T(8,128)(2,1)S(1)} %get-tuple-element.19), channel_id=1, source_target_pairs={{0,16},{8,24},{16,0},{24,8},{1,17},{9,25},{17,1},{25,9},{2,18},{10... | collective-permute-start | bytes 196616 | tf_op jit(solution)/shard_map/ppermute | solution.py:255
  25.1 0.7 %copy-start.4 = (s32[1,1,2]{2,1,0:T(1,128)S(1)}, s32[1,1,2]{2,1,0:T(1,128)}, u32[]{:S(2)}) copy-start(s32[1,1,2]{2,1,0:T(1,128)} %param.8) | copy-start | bytes 28
  26.4 10.3 %collective-permute-start.5 = (s16[2,2,4,16,128]{4,3,2,1,0:T(8,128)(2,1)S(1)}, s16[2,2,4,16,128]{4,3,2,1,0:T(8,128)(2,1)S(1)}, u32[]{:S(2)}, u32[]{:S(2)}) collective-permute-start(s16[2,2,4,16,128]{4,3,2,1,0:T(8,128)(2,1)S(1)} %resend.1), channel_id=1, source_target_pairs={{0,4},{1,5},{2,6},{3,7},{4,0},{5,1},{6,2},{7,3},{8,12},{9,13},{10,... | collective-permute-start | bytes 196616 | tf_op jit(solution)/shard_map/ppermute | solution.py:255

commit v3 on v2

--- a/solution.py
+++ b/solution.py
@@ -1,5 +1,3 @@
-import functools
-
 import jax
 import jax.numpy as jnp
 from jax import lax
@@ -7,6 +5,7 @@
 from jax.experimental.pallas import tpu as pltpu
 from jax.sharding import PartitionSpec as P
 
+
 PAIRS = 4
 DEEP = 2 * PAIRS
 SUB = 8
@@ -27,10 +26,6 @@
     return (codes.astype(jnp.int32).astype(jnp.float32) + shift) * (1.0 / scale)
 
 
-def tile_slice(slot, tx, ty):
-    return pl.ds((slot // 2) * tx, tx), pl.ds((slot % 2) * ty, ty)
-
-
 def flag_rows(active_ref, cols):
     lane = lax.broadcasted_iota(jnp.int32, (cols, LANES), 1)
     col = lax.broadcasted_iota(jnp.int32, (cols, LANES), 0)
@@ -41,13 +36,42 @@
     return jnp.where(lane < LANES // 2, flag(0), flag(1)).astype(jnp.float32)
 
 
-def pack_x(active_ref, heat_ref, pore_ref, out_ref, heat_out, pore_out):
+def mask_at(ranks):
+    choose = lambda i, k, s: (i * ranks + k) * 4 + s
+    taken = lambda i, r, s: 8 * ranks + (i * ranks + r) * 4 + s
+    again = lambda k, r: 16 * ranks + k * ranks + r
+    return choose, taken, again, 16 * ranks + ranks * ranks
+
+
+def pack_x(
+    active_ref, count_ref, slot_ref, heat_ref, pore_ref, out_ref, heat_out, pore_out, mask_ref
+):
     rows, cols = heat_ref.shape[0], heat_ref.shape[1]
-    heat_out[...] = heat_ref[...]
-    pore_out[...] = pore_ref[...]
+    ranks = slot_ref.shape[1]
     out_ref[0:rows] = heat_ref[...].astype(jnp.bfloat16)
     out_ref[rows : 2 * rows] = pore_ref[...].astype(jnp.bfloat16)
     out_ref[2 * rows] = flag_rows(active_ref, cols).astype(jnp.bfloat16)
+    heat_out[...] = heat_ref[...]
+    pore_out[...] = pore_ref[...]
+    choose, taken, again, _ = mask_at(ranks)
+
+    def put(row, holds):
+        mask_ref[row] = jnp.full((SUB, LANES), jnp.where(holds, 1.0, 0.0), jnp.float32)
+
+    for i in range(2):
+        for k in range(ranks):
+            for s in range(4):
+                here = slot_ref[i, k] == s
+                put(choose(i, k, s), here)
+                put(taken(i, k, s), here & (k < count_ref[i]))
+    for k in range(ranks):
+        for r in range(ranks):
+            put(again(k, r), (slot_ref[1, k] == slot_ref[0, r]) & (r < count_ref[0]))
+
+
+def inner(axis):
+    at = lax.axis_index(axis)
+    return jnp.where((at > 0) & (at < lax.axis_size(axis) - 1), 1.0, 0.0).astype(jnp.float32)
 
 
 def x_parts(own_ref, near_ref, far_ref):
@@ -69,8 +93,8 @@
 
 
 def step(
-    active_ref, slot_ref, heat_ref, pore_ref, xn_ref, xf_ref, yn_ref, yf_ref,
-    heat_out, pore_out, send_ref, wide, hs, qa, qb, vs, ks, vz, wz, ms,
+    own_ref, mask_ref, heat_ref, pore_ref, xn_ref, xf_ref, yn_ref, yf_ref,
+    heat_out, pore_out, send_ref, later_ref, wide, hs, qa, qb, vs, ks, vz, wz, ms,
 ):
     rows, cols = heat_ref.shape[0], heat_ref.shape[1]
     tx, ty = rows // 2, cols // 2
@@ -85,17 +109,28 @@
     odd = lax.rem(lax.axis_index("gy"), 2)
     edge = width - DEEP
     y_parts = (
-        (pl.ds(pl.multiple_of(edge - edge * odd, DEEP), DEEP), yn_ref),
-        (pl.ds(pl.multiple_of(edge * odd, DEEP), DEEP), yf_ref),
+        (pl.ds(pl.multiple_of(edge - edge * odd, DEEP), DEEP), yn_ref, None),
+        (pl.ds(pl.multiple_of(edge * odd, DEEP), DEEP), yf_ref, inner("gy")),
     )
     own = pl.ds(DEEP, cols)
-
-    for i, part in x_parts(None, xn_ref, xf_ref):
-        mid = flag_rows(active_ref, cols) if part is None else part[2 * rows].astype(f32)
-        wide[i, own, :] = mid
-    for at, part in y_parts:
+    x_open = inner("gx")
+    odd_x = lax.rem(lax.axis_index("gx"), 2)
+    row_open = (
+        jnp.where(odd_x == 0, x_open, 1.0),
+        None,
+        jnp.where(odd_x == 1, x_open, 1.0),
+    )
+
+    def scaled(v, *by):
+        for s in by:
+            v = v if s is None else v * s
+        return v
+
+    for (i, part), far in zip(x_parts(own_ref, xn_ref, xf_ref), (None, None, x_open)):
+        wide[i, own, :] = scaled(part[2 * rows].astype(f32), far)
+    for at, part, far in y_parts:
         for i in range(3):
-            wide[i, at, :] = part[6 * rows + i].astype(f32)
+            wide[i, at, :] = scaled(part[6 * rows + i].astype(f32), far, row_open[i])
     for i in range(3):
         for j in span:
             f = wide[i, pl.ds(j, SUB, stride=n), :]
@@ -103,14 +138,18 @@
             ms[2 * i, j] = jnp.where(low_half, f, r)
             ms[2 * i + 1, j] = jnp.where(low_half, r, f)
 
-    for field, own_ref, into in ((0, heat_ref, hs), (1, pore_ref, qa)):
-        for i, part in x_parts(None, xn_ref, xf_ref):
+    for field, home_ref, into in ((0, heat_ref, hs), (1, pore_ref, qa)):
+        for (i, part), far in zip(x_parts(None, xn_ref, xf_ref), (None, None, x_open)):
             for r in range(rows):
-                mid = own_ref[r] if part is None else part[field * rows + r].astype(f32)
+                if part is None:
+                    mid = home_ref[r]
+                else:
+                    mid = scaled(part[field * rows + r].astype(f32), far)
                 wide[i * rows + r, own, :] = mid
-        for at, part in y_parts:
+        for at, part, far in y_parts:
             for x in range(total):
-                wide[x, at, :] = part[field * total + x].astype(f32)
+                v = part[field * total + x].astype(f32)
+                wide[x, at, :] = scaled(v, far, row_open[x // rows])
         for x in range(total):
             for j in span:
                 v = wide[x, pl.ds(j, SUB, stride=n), :]
@@ -184,44 +223,66 @@
         for i in range(2):
             for k in range(2):
                 out[2 * i + k] = wide[i * tx : (i + 1) * tx, DEEP + k * ty : DEEP + (k + 1) * ty, :]
-    for k in range(slot_ref.shape[1]):
-        s = slot_ref[0, k]
-        send_ref[k, 0] = encode(heat_out[s], HEAT_SCALE, HEAT_SHIFT)
-        send_ref[k, 1] = encode(pore_out[s], PORE_SCALE, PORE_SHIFT)
-
-
-def resend(count_ref, slot_ref, heat_ref, pore_ref, got_ref, send_ref):
-    ranks = slot_ref.shape[1]
+    ranks = send_ref.shape[0]
+    choose = mask_at(ranks)[0]
+    shape = (tx, ty, LANES)
+    for field, src, scale, shift in (
+        (0, heat_out, HEAT_SCALE, HEAT_SHIFT),
+        (1, pore_out, PORE_SCALE, PORE_SHIFT),
+    ):
+        for i, out in ((0, send_ref), (1, later_ref)):
+            for k in range(ranks):
+                v = src[0]
+                for s in range(1, 4):
+                    v = jnp.where(held(mask_ref, choose(i, k, s), shape), src[s], v)
+                out[k, field] = encode(v, scale, shift)
+
+
+def held(mask_ref, row, shape):
+    m = mask_ref[row]
+    m = jnp.concatenate([m] * (shape[1] // SUB), axis=0)
+    return jnp.broadcast_to(m[None], shape) > 0.5
+
+
+def resend(mask_ref, got_ref, local_ref, send_ref):
+    ranks = got_ref.shape[0]
+    shape = got_ref.shape[2:]
+    again = mask_at(ranks)[2]
     for k in range(ranks):
-        s = slot_ref[1, k]
-        send_ref[k, 0] = encode(heat_ref[s], HEAT_SCALE, HEAT_SHIFT)
-        send_ref[k, 1] = encode(pore_ref[s], PORE_SCALE, PORE_SHIFT)
-        for r in range(ranks):
-
-            @pl.when((r < count_ref[0]) & (slot_ref[0, r] == s))
-            def _():
-                send_ref[k] = got_ref[r]
-
-
-def place(count_ref, slot_ref, heat_ref, pore_ref, first_ref, second_ref, heat_out, pore_out):
-    ranks = slot_ref.shape[1]
-    heat_out[...] = heat_ref[...]
-    pore_out[...] = pore_ref[...]
-    for i, got_ref in ((0, first_ref), (1, second_ref)):
-        for r in range(ranks):
-
-            @pl.when(r < count_ref[i])
-            def _():
-                s = slot_ref[i, r]
-                heat_out[s] = decode(got_ref[r, 0], HEAT_SCALE, HEAT_SHIFT)
-                pore_out[s] = decode(got_ref[r, 1], PORE_SCALE, PORE_SHIFT)
-
-
-def call(body, spec, outs, scratch=(), name=None, out_space=pltpu.VMEM):
+        for f in range(2):
+            v = local_ref[k, f].astype(jnp.int32)
+            for r in range(ranks):
+                v = jnp.where(
+                    held(mask_ref, again(k, r), shape), got_ref[r, f].astype(jnp.int32), v
+                )
+            send_ref[k, f] = v.astype(jnp.int16)
+
+
+def place(mask_ref, heat_ref, pore_ref, first_ref, second_ref, heat_out, pore_out):
+    ranks = first_ref.shape[0]
+    shape = first_ref.shape[2:]
+    taken = mask_at(ranks)[1]
+    for field, src, out, scale, shift in (
+        (0, heat_ref, heat_out, HEAT_SCALE, HEAT_SHIFT),
+        (1, pore_ref, pore_out, PORE_SCALE, PORE_SHIFT),
+    ):
+        came = [
+            (i, r, decode(got[r, field], scale, shift))
+            for i, got in ((0, first_ref), (1, second_ref))
+            for r in range(ranks)
+        ]
+        for s in range(4):
+            v = src[s]
+            for i, r, tile in came:
+                v = jnp.where(held(mask_ref, taken(i, r, s), shape), tile, v)
+            out[s] = v
+
+
+def call(body, spec, outs, scratch=(), out_space=pltpu.VMEM):
     def run(*args):
         space = {"s": pltpu.SMEM, "v": pltpu.VMEM, "V": pltpu.VMEM}
         args = [
-            pltpu.with_memory_space_constraint(a, pltpu.VMEM) if c == "V" else a
+            pltpu.with_memory_space_constraint(a, pltpu.VMEM if c == "V" else pltpu.HBM)
             for c, a in zip(spec, args)
         ]
         shapes = [
@@ -235,7 +296,6 @@
             out_shape=shapes,
             scratch_shapes=list(scratch),
             compiler_params=pltpu.CompilerParams(vmem_limit_bytes=VMEM_LIMIT),
-            name=name,
         )(*args)
 
     return run
@@ -243,10 +303,10 @@
 
 def exchange(near, far, axis):
     n = lax.axis_size(axis)
-    near_pairs = [(i, i ^ 1) for i in range(n) if i ^ 1 < n]
-    far_pairs = [(i, ((i + 1) ^ 1) - 1) for i in range(1, n) if ((i + 1) ^ 1) - 1 < n]
+    near_pairs = [(i, i ^ 1) for i in range(n)]
+    far_pairs = [(0, 0), (n - 1, n - 1)] + [(i, ((i + 1) ^ 1) - 1) for i in range(1, n - 1)]
+    near = lax.ppermute(near, axis, near_pairs)
     far = lax.ppermute(far, axis, far_pairs)
-    near = lax.ppermute(near, axis, near_pairs)
     return near, far
 
 
@@ -264,29 +324,29 @@
     f32, bf16, i16 = jnp.float32, jnp.bfloat16, jnp.int16
 
     block = ((rows, cols, depth), f32)
-    own, enthalpy, porosity = call(
-        pack_x, "svv", [((2 * rows + 1, cols, depth), bf16), block, block], name="pack_x"
-    )(active, enthalpy, porosity)
+    masks = ((mask_at(ranks)[3], SUB, LANES), f32)
+    own, enthalpy, porosity, masks = call(
+        pack_x, "sssvv", [((2 * rows + 1, cols, depth), bf16), block, block, masks]
+    )(active, count, slots, enthalpy, porosity)
     x_near, x_far = exchange(own, own, "gx")
     side = ((6 * rows + 3, DEEP, depth), bf16)
-    near, far = call(pack_y, "VVV", [side, side], name="pack_y")(own, x_near, x_far)
+    near, far = call(pack_y, "VVV", [side, side])(own, x_near, x_far)
     y_near, y_far = exchange(near, far, "gy")
     total, width = rows + 2 * DEEP, cols + 2 * DEEP
     tiles = ((4, tx, ty, depth), f32)
     parcel = ((ranks, 2, tx, ty, depth), i16)
     split = pltpu.VMEM((total, width // SUB, SUB, depth), f32)
-    heat, pore, first = call(
-        step, "ssVVVVVV", [tiles, tiles, parcel],
+    heat, pore, first, later = call(
+        step, "VVVVVVVV", [tiles, tiles, parcel, parcel],
         [pltpu.VMEM((total, width, depth), f32)]
         + [split] * 7
         + [pltpu.VMEM((total // tx, width // SUB, SUB, depth), f32)],
-        name="step",
-    )(active, slots, enthalpy, porosity, x_near, x_far, y_near, y_far)
+    )(own, masks, enthalpy, porosity, x_near, x_far, y_near, y_far)
     first = swap(first, "gx")
-    (second,) = call(resend, "ssVVV", [parcel], name="resend")(count, slots, heat, pore, first)
+    (second,) = call(resend, "VVV", [parcel])(masks, first, later)
     second = swap(second, "gy")
-    heat, pore = call(place, "ssVVVV", [tiles, tiles], name="place", out_space=None)(
-        count, slots, heat, pore, first, second
+    heat, pore = call(place, "VVVVV", [tiles, tiles], out_space=None)(
+        masks, heat, pore, first, second
     )
     return heat[None, None], pore[None, None]
 
@@ -300,6 +360,7 @@
         P("gx", "gy", None, None),
     )
     out = P("gx", "gy", None, None, None, None)
+
     return jax.shard_map(
         per_device, mesh=mesh, in_specs=placed, out_specs=(out, out), check_vma=False
     )

time: 38.2 us -> 33.1 us (0.87)
  local copies, waits for them, and re-layouts: 3.81 us -> 0 us
  Pallas kernels: 6.59 us -> 5.4 us
    unnamed x10 -> x0, local copies, waits for them, and re-layouts: 3.81 us -> none
    pallas_call x5, Pallas kernels: 6.59 us -> 5.4 us  [run(): pl.pallas_call(body, in_specs=[pl.BlockSpec(memory_space=space[c]) for c...]
where the time goes in v3:
time: 33.1 us; the launch traced here: 32.9 us
  starting transfers between devices  17 us (51%)
  waiting for transfers between devices  9.8 us (30%)
  Pallas kernels  5.4 us (16%)
  between operations  0.68 us (2%)
    ppermute x2, starting transfers between devices, swap(): return lax.ppermute(value, axis, [(i, (i + n // 2) % n) for i in range(n)])  9.7 us
    ppermute x2, starting transfers between devices, exchange(): near = lax.ppermute(near, axis, near_pairs)  6 us
    ppermute x2, waiting for transfers between devices, swap(): return lax.ppermute(value, axis, [(i, (i + n // 2) % n) for i in range(n)])  5.78 us
    pallas_call x5, Pallas kernels, run(): pl.pallas_call(body, in_specs=[pl.BlockSpec(memory_space=space[c]) for c...  5.4 us
    ppermute x2, waiting for transfers between devices, exchange(): near = lax.ppermute(near, axis, near_pairs)  4.01 us
    ppermute x2, starting transfers between devices, exchange(): far = lax.ppermute(far, axis, far_pairs)  1.34 us
  transfers between devices with their start and end apart: 6, of which 4 were waited for; matrix products, arithmetic and copies ran while one was open for 0% of the time, Pallas kernels for 0%

profile of v3, /device:TPU:0, one launch (start us, length us, event | category | flops | bytes accessed | tf_op | source)
XLA Modules:
  0.0 32.9 jit_solution(4821092854248235011)
XLA Ops:
  0.6 1.0 %shard_map.68 = (bf16[17,32,128]{2,1,0:T(8,128)(2,1)S(1)}, f32[8,32,128]{2,1,0:T(8,128)S(1)}, f32[8,32,128]{2,1,0:T(8,128)S(1)}, f32[36,8,128]{2,1,0:T(8,128)S(1)}) custom-call(s32[2,2]{1,0:T(2,128)} %active_ref.1, s32[2]{0:T(128)} %bitcast.5, s32[2,2]{1,0:T(2,128)} %bitcast.4, f32[8,32,128]{2,1,0:T(8,128)} %heat_ref.1, f32[8,32,128]{2,1,0:T(8,128)} %pore_ref.1), custom_call_target="tpu_custom_call" | custom-call | tf_op jit(solution)/shard_map/pallas_call | solution.py:292
  1.7 0.7 %collective-permute-start.1 = (bf16[17,32,128]{2,1,0:T(8,128)(2,1)S(1)}, bf16[17,32,128]{2,1,0:T(8,128)(2,1)S(1)}, u32[]{:S(2)}, u32[]{:S(2)}) collective-permute-start(bf16[17,32,128]{2,1,0:T(8,128)(2,1)S(1)} %get-tuple-element.15.own_ref), channel_id=1, source_target_pairs={{0,0},{24,24},{8,16},{16,8},{1,1},{25,25},{9,17},{17,9},{2,2},{26,... | collective-permute-start | bytes 417800 | tf_op jit(solution)/shard_map/ppermute | solution.py:309
  2.3 5.9 %collective-permute-start = (bf16[17,32,128]{2,1,0:T(8,128)(2,1)S(1)}, bf16[17,32,128]{2,1,0:T(8,128)(2,1)S(1)}, u32[]{:S(2)}, u32[]{:S(2)}) collective-permute-start(bf16[17,32,128]{2,1,0:T(8,128)(2,1)S(1)} %get-tuple-element.15.own_ref), channel_id=1, source_target_pairs={{0,8},{8,0},{16,24},{24,16},{1,9},{9,1},{17,25},{25,17},{2,10},{10... | collective-permute-start | bytes 417800 | tf_op jit(solution)/shard_map/ppermute | solution.py:308
  8.3 0.0 collective-permute-done.1.far_ref.xf_ref
  8.3 3.4 %collective-permute-done.near_ref.xn_ref = bf16[17,32,128]{2,1,0:T(8,128)(2,1)S(1)} collective-permute-done((bf16[17,32,128]{2,1,0:T(8,128)(2,1)S(1)}, bf16[17,32,128]{2,1,0:T(8,128)(2,1)S(1)}, u32[]{:S(2)}, u32[]{:S(2)}) %collective-permute-start) | collective-permute-done | bytes 139296 | tf_op jit(solution)/shard_map/ppermute | solution.py:308
  11.7 0.1 collective-permute-start.2
  11.8 0.7 %collective-permute-start.3 = (bf16[51,8,128]{2,1,0:T(8,128)(2,1)S(1)}, bf16[51,8,128]{2,1,0:T(8,128)(2,1)S(1)}, u32[]{:S(2)}, u32[]{:S(2)}) collective-permute-start(bf16[51,8,128]{2,1,0:T(8,128)(2,1)S(1)} %get-tuple-element.19), channel_id=1, source_target_pairs={{0,0},{7,7},{1,2},{2,1},{3,4},{4,3},{5,6},{6,5},{8,8},{15,15},{9,1... | collective-permute-start | bytes 313352 | tf_op jit(solution)/shard_map/ppermute | solution.py:309
  12.5 0.6 %collective-permute-done.2.yn_ref = bf16[51,8,128]{2,1,0:T(8,128)(2,1)S(1)} collective-permute-done((bf16[51,8,128]{2,1,0:T(8,128)(2,1)S(1)}, bf16[51,8,128]{2,1,0:T(8,128)(2,1)S(1)}, u32[]{:S(2)}, u32[]{:S(2)}) %collective-permute-start.2) | collective-permute-done | bytes 104480 | tf_op jit(solution)/shard_map/ppermute | solution.py:308
  13.1 0.0 collective-permute-done.3.yf_ref
  13.1 3.6 %shard_map.70 = (f32[4,4,16,128]{3,2,1,0:T(8,128)S(1)}, f32[4,4,16,128]{3,2,1,0:T(8,128)S(1)}, s16[2,2,4,16,128]{4,3,2,1,0:T(8,128)(2,1)S(1)}, s16[2,2,4,16,128]{4,3,2,1,0:T(8,128)(2,1)S(1)}) custom-call(bf16[17,32,128]{2,1,0:T(8,128)(2,1)S(1)} %get-tuple-element.15.own_ref, f32[36,8,128]{2,1,0:T(8,128)S(1)} %get-tuple-element.14.mask_ref, ...), custom_call_target="tpu_custom_call" | custom-call | tf_op jit(solution)/shard_map/pallas_call | solution.py:292
  16.7 1.7 %collective-permute-start.4 = (s16[2,2,4,16,128]{4,3,2,1,0:T(8,128)(2,1)S(1)}, s16[2,2,4,16,128]{4,3,2,1,0:T(8,128)(2,1)S(1)}, u32[]{:S(2)}, u32[]{:S(2)}) collective-permute-start(s16[2,2,4,16,128]{4,3,2,1,0:T(8,128)(2,1)S(1)} %get-tuple-element.22), channel_id=1, source_target_pairs={{0,16},{8,24},{16,0},{24,8},{1,17},{9,25},{17,1},{25,9},{2,18},{10... | collective-permute-start | bytes 196616 | tf_op jit(solution)/shard_map/ppermute | solution.py:315
  18.4 3.5 %collective-permute-done.4.got_ref.first_ref = s16[2,2,4,16,128]{4,3,2,1,0:T(8,128)(2,1)S(1)} collective-permute-done((s16[2,2,4,16,128]{4,3,2,1,0:T(8,128)(2,1)S(1)}, s16[2,2,4,16,128]{4,3,2,1,0:T(8,128)(2,1)S(1)}, u32[]{:S(2)}, u32[]{:S(2)}) %collective-permute-start.4) | collective-permute-done | bytes 65568 | tf_op jit(solution)/shard_map/ppermute | solution.py:315
  21.9 8.0 %collective-permute-start.5 = (s16[2,2,4,16,128]{4,3,2,1,0:T(8,128)(2,1)S(1)}, s16[2,2,4,16,128]{4,3,2,1,0:T(8,128)(2,1)S(1)}, u32[]{:S(2)}, u32[]{:S(2)}) collective-permute-start(s16[2,2,4,16,128]{4,3,2,1,0:T(8,128)(2,1)S(1)} %shard_map.71), channel_id=1, source_target_pairs={{0,4},{1,5},{2,6},{3,7},{4,0},{5,1},{6,2},{7,3},{8,12},{9,13},{10,... | collective-permute-start | bytes 196616 | tf_op jit(solution)/shard_map/ppermute | solution.py:315
  29.9 2.2 %collective-permute-done.5.second_ref = s16[2,2,4,16,128]{4,3,2,1,0:T(8,128)(2,1)S(1)} collective-permute-done((s16[2,2,4,16,128]{4,3,2,1,0:T(8,128)(2,1)S(1)}, s16[2,2,4,16,128]{4,3,2,1,0:T(8,128)(2,1)S(1)}, u32[]{:S(2)}, u32[]{:S(2)}) %collective-permute-start.5) | collective-permute-done | bytes 65568 | tf_op jit(solution)/shard_map/ppermute | solution.py:315
  32.2 0.7 %shard_map.72 = (f32[4,4,16,128]{3,2,1,0:T(8,128)}, f32[4,4,16,128]{3,2,1,0:T(8,128)}) custom-call(f32[36,8,128]{2,1,0:T(8,128)S(1)} %get-tuple-element.14.mask_ref, f32[4,4,16,128]{3,2,1,0:T(8,128)S(1)} %get-tuple-element.20.heat_ref, f32[4,4,16,128]{3,2,1,0:T(8,128)S(1)} %get-tuple-element.21.pore_ref, ...), custom_call_target="tpu_custom_call" | custom-call | tf_op jit(solution)/shard_map/pallas_call | solution.py:292
  (2 shorter events, 0.1 us)
Async XLA Ops:
  1.7 6.6 %collective-permute-start.1 = (bf16[17,32,128]{2,1,0:T(8,128)(2,1)S(1)}, bf16[17,32,128]{2,1,0:T(8,128)(2,1)S(1)}, u32[]{:S(2)}, u32[]{:S(2)}) collective-permute-start(bf16[17,32,128]{2,1,0:T(8,128)(2,1)S(1)} %get-tuple-element.15.own_ref), channel_id=1, source_target_pairs={{0,0},{24,24},{8,16},{16,8},{1,1},{25,25},{9,17},{17,9},{2,2},{26,... | collective-permute-start | bytes 417800 | tf_op jit(solution)/shard_map/ppermute | solution.py:309
  2.3 9.3 %collective-permute-start = (bf16[17,32,128]{2,1,0:T(8,128)(2,1)S(1)}, bf16[17,32,128]{2,1,0:T(8,128)(2,1)S(1)}, u32[]{:S(2)}, u32[]{:S(2)}) collective-permute-start(bf16[17,32,128]{2,1,0:T(8,128)(2,1)S(1)} %get-tuple-element.15.own_ref), channel_id=1, source_target_pairs={{0,8},{8,0},{16,24},{24,16},{1,9},{9,1},{17,25},{25,17},{2,10},{10... | collective-permute-start | bytes 417800 | tf_op jit(solution)/shard_map/ppermute | solution.py:308
  11.7 1.4 %collective-permute-start.2 = (bf16[51,8,128]{2,1,0:T(8,128)(2,1)S(1)}, bf16[51,8,128]{2,1,0:T(8,128)(2,1)S(1)}, u32[]{:S(2)}, u32[]{:S(2)}) collective-permute-start(bf16[51,8,128]{2,1,0:T(8,128)(2,1)S(1)} %get-tuple-element.18), channel_id=1, source_target_pairs={{0,1},{1,0},{2,3},{3,2},{4,5},{5,4},{6,7},{7,6},{8,9},{9,8},{10,11... | collective-permute-start | bytes 313352 | tf_op jit(solution)/shard_map/ppermute | solution.py:308
  11.8 1.3 %collective-permute-start.3 = (bf16[51,8,128]{2,1,0:T(8,128)(2,1)S(1)}, bf16[51,8,128]{2,1,0:T(8,128)(2,1)S(1)}, u32[]{:S(2)}, u32[]{:S(2)}) collective-permute-start(bf16[51,8,128]{2,1,0:T(8,128)(2,1)S(1)} %get-tuple-element.19), channel_id=1, source_target_pairs={{0,0},{7,7},{1,2},{2,1},{3,4},{4,3},{5,6},{6,5},{8,8},{15,15},{9,1... | collective-permute-start | bytes 313352 | tf_op jit(solution)/shard_map/ppermute | solution.py:309
  16.7 5.2 %collective-permute-start.4 = (s16[2,2,4,16,128]{4,3,2,1,0:T(8,128)(2,1)S(1)}, s16[2,2,4,16,128]{4,3,2,1,0:T(8,128)(2,1)S(1)}, u32[]{:S(2)}, u32[]{:S(2)}) collective-permute-start(s16[2,2,4,16,128]{4,3,2,1,0:T(8,128)(2,1)S(1)} %get-tuple-element.22), channel_id=1, source_target_pairs={{0,16},{8,24},{16,0},{24,8},{1,17},{9,25},{17,1},{25,9},{2,18},{10... | collective-permute-start | bytes 196616 | tf_op jit(solution)/shard_map/ppermute | solution.py:315
  21.9 10.3 %collective-permute-start.5 = (s16[2,2,4,16,128]{4,3,2,1,0:T(8,128)(2,1)S(1)}, s16[2,2,4,16,128]{4,3,2,1,0:T(8,128)(2,1)S(1)}, u32[]{:S(2)}, u32[]{:S(2)}) collective-permute-start(s16[2,2,4,16,128]{4,3,2,1,0:T(8,128)(2,1)S(1)} %shard_map.71), channel_id=1, source_target_pairs={{0,4},{1,5},{2,6},{3,7},{4,0},{5,1},{6,2},{7,3},{8,12},{9,13},{10,... | collective-permute-start | bytes 196616 | tf_op jit(solution)/shard_map/ppermute | solution.py:315

commit v4 on v3

--- a/solution.py
+++ b/solution.py
@@ -69,24 +69,25 @@
             put(again(k, r), (slot_ref[1, k] == slot_ref[0, r]) & (r < count_ref[0]))
 
 
-def inner(axis):
+def inside(axis, below):
     at = lax.axis_index(axis)
-    return jnp.where((at > 0) & (at < lax.axis_size(axis) - 1), 1.0, 0.0).astype(jnp.float32)
-
-
-def x_parts(own_ref, near_ref, far_ref):
-    odd = lax.rem(lax.axis_index("gx"), 2)
-    return ((2 - 2 * odd, near_ref), (1, own_ref), (2 * odd, far_ref))
-
-
-def pack_y(own_ref, near_ref, far_ref, near_out, far_out):
+    has = at < lax.axis_size(axis) - 1 if below else at > 0
+    return jnp.where(has, 1.0, 0.0).astype(jnp.float32)
+
+
+def x_parts(own_ref, first_ref, second_ref):
+    odd = lax.rem(lax.axis_index("gx") + lax.axis_index("gy"), 2)
+    return ((2 - 2 * odd, first_ref), (1, own_ref), (2 * odd, second_ref))
+
+
+def pack_y(own_ref, first_ref, second_ref, near_out, far_out):
     rows = (own_ref.shape[0] - 1) // 2
     cols = own_ref.shape[1]
     odd = lax.rem(lax.axis_index("gy"), 2)
     edge = cols - DEEP
     for out_ref, start in ((near_out, edge - edge * odd), (far_out, edge * odd)):
         at = pl.ds(pl.multiple_of(start, DEEP), DEEP)
-        for i, part in x_parts(own_ref, near_ref, far_ref):
+        for i, part in x_parts(own_ref, first_ref, second_ref):
             for f in range(2):
                 out_ref[pl.ds((3 * f + i) * rows, rows)] = part[pl.ds(f * rows, rows), at, :]
             out_ref[6 * rows + i] = part[2 * rows, at, :]
@@ -110,49 +111,41 @@
     edge = width - DEEP
     y_parts = (
         (pl.ds(pl.multiple_of(edge - edge * odd, DEEP), DEEP), yn_ref, None),
-        (pl.ds(pl.multiple_of(edge * odd, DEEP), DEEP), yf_ref, inner("gy")),
+        (
+            pl.ds(pl.multiple_of(edge * odd, DEEP), DEEP),
+            yf_ref,
+            jnp.where(odd == 1, inside("gy", True), inside("gy", False)),
+        ),
     )
     own = pl.ds(DEEP, cols)
-    x_open = inner("gx")
-    odd_x = lax.rem(lax.axis_index("gx"), 2)
-    row_open = (
-        jnp.where(odd_x == 0, x_open, 1.0),
-        None,
-        jnp.where(odd_x == 1, x_open, 1.0),
-    )
-
-    def scaled(v, *by):
-        for s in by:
-            v = v if s is None else v * s
-        return v
-
-    for (i, part), far in zip(x_parts(own_ref, xn_ref, xf_ref), (None, None, x_open)):
-        wide[i, own, :] = scaled(part[2 * rows].astype(f32), far)
+    row_open = (inside("gx", False), None, inside("gx", True))
+
+    def scaled(v, by):
+        return v if by is None else v * by
+
+    for i, part in x_parts(own_ref, xn_ref, xf_ref):
+        wide[i, own, :] = part[2 * rows].astype(f32)
     for at, part, far in y_parts:
         for i in range(3):
-            wide[i, at, :] = scaled(part[6 * rows + i].astype(f32), far, row_open[i])
+            wide[i, at, :] = scaled(part[6 * rows + i].astype(f32), far)
     for i in range(3):
         for j in span:
-            f = wide[i, pl.ds(j, SUB, stride=n), :]
+            f = scaled(wide[i, pl.ds(j, SUB, stride=n), :], row_open[i])
             r = pltpu.roll(f, LANES // 2, 1)
             ms[2 * i, j] = jnp.where(low_half, f, r)
             ms[2 * i + 1, j] = jnp.where(low_half, r, f)
 
     for field, home_ref, into in ((0, heat_ref, hs), (1, pore_ref, qa)):
-        for (i, part), far in zip(x_parts(None, xn_ref, xf_ref), (None, None, x_open)):
+        for i, part in x_parts(None, xn_ref, xf_ref):
             for r in range(rows):
-                if part is None:
-                    mid = home_ref[r]
-                else:
-                    mid = scaled(part[field * rows + r].astype(f32), far)
+                mid = home_ref[r] if part is None else part[field * rows + r].astype(f32)
                 wide[i * rows + r, own, :] = mid
         for at, part, far in y_parts:
             for x in range(total):
-                v = part[field * total + x].astype(f32)
-                wide[x, at, :] = scaled(v, far, row_open[x // rows])
+                wide[x, at, :] = scaled(part[field * total + x].astype(f32), far)
         for x in range(total):
             for j in span:
-                v = wide[x, pl.ds(j, SUB, stride=n), :]
+                v = scaled(wide[x, pl.ds(j, SUB, stride=n), :], row_open[x // rows])
                 into[x, j] = 2.0 * v - 2.0 if field == 0 else v
 
     def beside(x, j, v, w):
@@ -301,12 +294,41 @@
     return run
 
 
-def exchange(near, far, axis):
-    n = lax.axis_size(axis)
-    near_pairs = [(i, i ^ 1) for i in range(n)]
-    far_pairs = [(0, 0), (n - 1, n - 1)] + [(i, ((i + 1) ^ 1) - 1) for i in range(1, n - 1)]
-    near = lax.ppermute(near, axis, near_pairs)
-    far = lax.ppermute(far, axis, far_pairs)
+def permute(value, partner):
+    nx, ny = lax.axis_size("gx"), lax.axis_size("gy")
+    pairs = []
+    for x in range(nx):
+        for y in range(ny):
+            u, v = partner(x, y)
+            pairs.append((x * ny + y, u * ny + v))
+    return lax.ppermute(value, ("gx", "gy"), pairs)
+
+
+def exchange_x(value):
+    nx, ny = lax.axis_size("gx"), lax.axis_size("gy")
+
+    def partner(x, y, near):
+        if near:
+            return x ^ 1, y
+        if 0 < x < nx - 1:
+            return ((x + 1) ^ 1) - 1, y
+        return (x, y ^ 2) if ny % 4 == 0 else (x, y)
+
+    first = permute(value, lambda x, y: partner(x, y, y % 2 == 0))
+    second = permute(value, lambda x, y: partner(x, y, y % 2 == 1))
+    return first, second
+
+
+def exchange_y(near, far):
+    ny = lax.axis_size("gy")
+
+    def partner(x, y):
+        if 0 < y < ny - 1:
+            return x, ((y + 1) ^ 1) - 1
+        return x ^ 1, y
+
+    far = permute(far, partner)
+    near = permute(near, lambda x, y: (x, y ^ 1))
     return near, far
 
 
@@ -328,10 +350,10 @@
     own, enthalpy, porosity, masks = call(
         pack_x, "sssvv", [((2 * rows + 1, cols, depth), bf16), block, block, masks]
     )(active, count, slots, enthalpy, porosity)
-    x_near, x_far = exchange(own, own, "gx")
+    x_near, x_far = exchange_x(own)
     side = ((6 * rows + 3, DEEP, depth), bf16)
     near, far = call(pack_y, "VVV", [side, side])(own, x_near, x_far)
-    y_near, y_far = exchange(near, far, "gy")
+    y_near, y_far = exchange_y(near, far)
     total, width = rows + 2 * DEEP, cols + 2 * DEEP
     tiles = ((4, tx, ty, depth), f32)
     parcel = ((ranks, 2, tx, ty, depth), i16)

time: 33.1 us -> 30.3 us (0.915)
  starting transfers between devices: 17 us -> 9.97 us
  waiting for transfers between devices: 9.8 us -> 14.2 us
    ppermute x2, starting transfers between devices: 9.7 us -> 3.48 us  [swap(): return lax.ppermute(value, axis, [(i, (i + n // 2) % n) for i in range(n)])]
    ppermute x4, waiting for transfers between devices: 4.02 us -> 6.41 us  [permute(): return lax.ppermute(value, ('gx', 'gy'), pairs)]
    ppermute x2, waiting for transfers between devices: 5.78 us -> 7.81 us  [swap(): return lax.ppermute(value, axis, [(i, (i + n // 2) % n) for i in range(n)])]
    ppermute x4, starting transfers between devices: 7.34 us -> 6.49 us  [permute(): return lax.ppermute(value, ('gx', 'gy'), pairs)]
  transfers between devices with their start and end apart: 6 -> 6, of which waited for: 4 -> 5; matrix products, arithmetic and copies ran while one was open for 0% -> 0% of each run, Pallas kernels for 0% -> 0%
where the time goes in v4:
time: 30.3 us; the launch traced here: 30.2 us
  waiting for transfers between devices  14.2 us (47%)
  starting transfers between devices  9.97 us (33%)
  Pallas kernels  5.34 us (18%)
  between operations  0.67 us (2%)
    ppermute x2, waiting for transfers between devices, swap(): return lax.ppermute(value, axis, [(i, (i + n // 2) % n) for i in range(n)])  7.81 us
    ppermute x4, starting transfers between devices, permute(): return lax.ppermute(value, ('gx', 'gy'), pairs)  6.49 us
    ppermute x4, waiting for transfers between devices, permute(): return lax.ppermute(value, ('gx', 'gy'), pairs)  6.41 us
    pallas_call x5, Pallas kernels, run(): pl.pallas_call(body, in_specs=[pl.BlockSpec(memory_space=space[c]) for c...  5.34 us
    ppermute x2, starting transfers between devices, swap(): return lax.ppermute(value, axis, [(i, (i + n // 2) % n) for i in range(n)])  3.48 us
  transfers between devices with their start and end apart: 6, of which 5 were waited for; matrix products, arithmetic and copies ran while one was open for 0% of the time, Pallas kernels for 0%

profile of v4, /device:TPU:0, one launch (start us, length us, event | category | flops | bytes accessed | tf_op | source)
XLA Modules:
  0.0 30.2 jit_solution(918782094648662045)
XLA Ops:
  0.6 1.0 %shard_map.68 = (bf16[17,32,128]{2,1,0:T(8,128)(2,1)S(1)}, f32[8,32,128]{2,1,0:T(8,128)S(1)}, f32[8,32,128]{2,1,0:T(8,128)S(1)}, f32[36,8,128]{2,1,0:T(8,128)S(1)}) custom-call(s32[2,2]{1,0:T(2,128)} %active_ref.1, s32[2]{0:T(128)} %bitcast.5, s32[2,2]{1,0:T(2,128)} %bitcast.4, f32[8,32,128]{2,1,0:T(8,128)} %heat_ref.1, f32[8,32,128]{2,1,0:T(8,128)} %pore_ref.1), custom_call_target="tpu_custom_call" | custom-call | tf_op jit(solution)/shard_map/pallas_call | solution.py:285
  1.7 3.0 %collective-permute-start.1 = (bf16[17,32,128]{2,1,0:T(8,128)(2,1)S(1)}, bf16[17,32,128]{2,1,0:T(8,128)(2,1)S(1)}, u32[]{:S(2)}, u32[]{:S(2)}) collective-permute-start(bf16[17,32,128]{2,1,0:T(8,128)(2,1)S(1)} %get-tuple-element.15.own_ref), channel_id=1, source_target_pairs={{0,2},{1,9},{2,0},{3,11},{4,6},{5,13},{6,4},{7,15},{8,16},{9,1},{1... | collective-permute-start | bytes 417800 | tf_op jit(solution)/shard_map/ppermute | solution.py:304
  4.7 1.7 %collective-permute-start = (bf16[17,32,128]{2,1,0:T(8,128)(2,1)S(1)}, bf16[17,32,128]{2,1,0:T(8,128)(2,1)S(1)}, u32[]{:S(2)}, u32[]{:S(2)}) collective-permute-start(bf16[17,32,128]{2,1,0:T(8,128)(2,1)S(1)} %get-tuple-element.15.own_ref), channel_id=1, source_target_pairs={{0,8},{1,3},{2,10},{3,1},{4,12},{5,7},{6,14},{7,5},{8,0},{9,17},{1... | collective-permute-start | bytes 417800 | tf_op jit(solution)/shard_map/ppermute | solution.py:304
  6.4 2.2 %collective-permute-done.1.second_ref.xf_ref = bf16[17,32,128]{2,1,0:T(8,128)(2,1)S(1)} collective-permute-done((bf16[17,32,128]{2,1,0:T(8,128)(2,1)S(1)}, bf16[17,32,128]{2,1,0:T(8,128)(2,1)S(1)}, u32[]{:S(2)}, u32[]{:S(2)}) %collective-permute-start.1) | collective-permute-done | bytes 139296 | tf_op jit(solution)/shard_map/ppermute | solution.py:304
  8.6 1.2 %collective-permute-done.first_ref.xn_ref = bf16[17,32,128]{2,1,0:T(8,128)(2,1)S(1)} collective-permute-done((bf16[17,32,128]{2,1,0:T(8,128)(2,1)S(1)}, bf16[17,32,128]{2,1,0:T(8,128)(2,1)S(1)}, u32[]{:S(2)}, u32[]{:S(2)}) %collective-permute-start) | collective-permute-done | bytes 139296 | tf_op jit(solution)/shard_map/ppermute | solution.py:304
  9.8 0.1 collective-permute-start.2
  9.9 1.7 %collective-permute-start.3 = (bf16[51,8,128]{2,1,0:T(8,128)(2,1)S(1)}, bf16[51,8,128]{2,1,0:T(8,128)(2,1)S(1)}, u32[]{:S(2)}, u32[]{:S(2)}) collective-permute-start(bf16[51,8,128]{2,1,0:T(8,128)(2,1)S(1)} %get-tuple-element.19), channel_id=1, source_target_pairs={{0,8},{1,2},{2,1},{3,4},{4,3},{5,6},{6,5},{7,15},{8,0},{9,10},{10,... | collective-permute-start | bytes 313352 | tf_op jit(solution)/shard_map/ppermute | solution.py:304
  11.6 0.0 collective-permute-done.2.yn_ref
  11.6 3.0 %collective-permute-done.3.yf_ref = bf16[51,8,128]{2,1,0:T(8,128)(2,1)S(1)} collective-permute-done((bf16[51,8,128]{2,1,0:T(8,128)(2,1)S(1)}, bf16[51,8,128]{2,1,0:T(8,128)(2,1)S(1)}, u32[]{:S(2)}, u32[]{:S(2)}) %collective-permute-start.3) | collective-permute-done | bytes 104480 | tf_op jit(solution)/shard_map/ppermute | solution.py:304
  14.6 3.5 %shard_map.70 = (f32[4,4,16,128]{3,2,1,0:T(8,128)S(1)}, f32[4,4,16,128]{3,2,1,0:T(8,128)S(1)}, s16[2,2,4,16,128]{4,3,2,1,0:T(8,128)(2,1)S(1)}, s16[2,2,4,16,128]{4,3,2,1,0:T(8,128)(2,1)S(1)}) custom-call(bf16[17,32,128]{2,1,0:T(8,128)(2,1)S(1)} %get-tuple-element.15.own_ref, f32[36,8,128]{2,1,0:T(8,128)S(1)} %get-tuple-element.14.mask_ref, ...), custom_call_target="tpu_custom_call" | custom-call | tf_op jit(solution)/shard_map/pallas_call | solution.py:285
  18.1 2.5 %collective-permute-start.4 = (s16[2,2,4,16,128]{4,3,2,1,0:T(8,128)(2,1)S(1)}, s16[2,2,4,16,128]{4,3,2,1,0:T(8,128)(2,1)S(1)}, u32[]{:S(2)}, u32[]{:S(2)}) collective-permute-start(s16[2,2,4,16,128]{4,3,2,1,0:T(8,128)(2,1)S(1)} %get-tuple-element.22), channel_id=1, source_target_pairs={{0,16},{8,24},{16,0},{24,8},{1,17},{9,25},{17,1},{25,9},{2,18},{10... | collective-permute-start | bytes 196616 | tf_op jit(solution)/shard_map/ppermute | solution.py:337
  20.7 4.4 %collective-permute-done.4.got_ref.first_ref = s16[2,2,4,16,128]{4,3,2,1,0:T(8,128)(2,1)S(1)} collective-permute-done((s16[2,2,4,16,128]{4,3,2,1,0:T(8,128)(2,1)S(1)}, s16[2,2,4,16,128]{4,3,2,1,0:T(8,128)(2,1)S(1)}, u32[]{:S(2)}, u32[]{:S(2)}) %collective-permute-start.4) | collective-permute-done | bytes 65568 | tf_op jit(solution)/shard_map/ppermute | solution.py:337
  25.1 1.0 %collective-permute-start.5 = (s16[2,2,4,16,128]{4,3,2,1,0:T(8,128)(2,1)S(1)}, s16[2,2,4,16,128]{4,3,2,1,0:T(8,128)(2,1)S(1)}, u32[]{:S(2)}, u32[]{:S(2)}) collective-permute-start(s16[2,2,4,16,128]{4,3,2,1,0:T(8,128)(2,1)S(1)} %shard_map.71), channel_id=1, source_target_pairs={{0,4},{1,5},{2,6},{3,7},{4,0},{5,1},{6,2},{7,3},{8,12},{9,13},{10,... | collective-permute-start | bytes 196616 | tf_op jit(solution)/shard_map/ppermute | solution.py:337
  26.1 3.4 %collective-permute-done.5.second_ref = s16[2,2,4,16,128]{4,3,2,1,0:T(8,128)(2,1)S(1)} collective-permute-done((s16[2,2,4,16,128]{4,3,2,1,0:T(8,128)(2,1)S(1)}, s16[2,2,4,16,128]{4,3,2,1,0:T(8,128)(2,1)S(1)}, u32[]{:S(2)}, u32[]{:S(2)}) %collective-permute-start.5) | collective-permute-done | bytes 65568 | tf_op jit(solution)/shard_map/ppermute | solution.py:337
  29.5 0.7 %shard_map.72 = (f32[4,4,16,128]{3,2,1,0:T(8,128)}, f32[4,4,16,128]{3,2,1,0:T(8,128)}) custom-call(f32[36,8,128]{2,1,0:T(8,128)S(1)} %get-tuple-element.14.mask_ref, f32[4,4,16,128]{3,2,1,0:T(8,128)S(1)} %get-tuple-element.20.heat_ref, f32[4,4,16,128]{3,2,1,0:T(8,128)S(1)} %get-tuple-element.21.pore_ref, ...), custom_call_target="tpu_custom_call" | custom-call | tf_op jit(solution)/shard_map/pallas_call | solution.py:285
  (2 shorter events, 0.1 us)
Async XLA Ops:
  1.7 6.9 %collective-permute-start.1 = (bf16[17,32,128]{2,1,0:T(8,128)(2,1)S(1)}, bf16[17,32,128]{2,1,0:T(8,128)(2,1)S(1)}, u32[]{:S(2)}, u32[]{:S(2)}) collective-permute-start(bf16[17,32,128]{2,1,0:T(8,128)(2,1)S(1)} %get-tuple-element.15.own_ref), channel_id=1, source_target_pairs={{0,2},{1,9},{2,0},{3,11},{4,6},{5,13},{6,4},{7,15},{8,16},{9,1},{1... | collective-permute-start | bytes 417800 | tf_op jit(solution)/shard_map/ppermute | solution.py:304
  4.7 5.1 %collective-permute-start = (bf16[17,32,128]{2,1,0:T(8,128)(2,1)S(1)}, bf16[17,32,128]{2,1,0:T(8,128)(2,1)S(1)}, u32[]{:S(2)}, u32[]{:S(2)}) collective-permute-start(bf16[17,32,128]{2,1,0:T(8,128)(2,1)S(1)} %get-tuple-element.15.own_ref), channel_id=1, source_target_pairs={{0,8},{1,3},{2,10},{3,1},{4,12},{5,7},{6,14},{7,5},{8,0},{9,17},{1... | collective-permute-start | bytes 417800 | tf_op jit(solution)/shard_map/ppermute | solution.py:304
  9.8 1.8 %collective-permute-start.2 = (bf16[51,8,128]{2,1,0:T(8,128)(2,1)S(1)}, bf16[51,8,128]{2,1,0:T(8,128)(2,1)S(1)}, u32[]{:S(2)}, u32[]{:S(2)}) collective-permute-start(bf16[51,8,128]{2,1,0:T(8,128)(2,1)S(1)} %get-tuple-element.18), channel_id=1, source_target_pairs={{0,1},{1,0},{2,3},{3,2},{4,5},{5,4},{6,7},{7,6},{8,9},{9,8},{10,11... | collective-permute-start | bytes 313352 | tf_op jit(solution)/shard_map/ppermute | solution.py:304
  9.9 4.7 %collective-permute-start.3 = (bf16[51,8,128]{2,1,0:T(8,128)(2,1)S(1)}, bf16[51,8,128]{2,1,0:T(8,128)(2,1)S(1)}, u32[]{:S(2)}, u32[]{:S(2)}) collective-permute-start(bf16[51,8,128]{2,1,0:T(8,128)(2,1)S(1)} %get-tuple-element.19), channel_id=1, source_target_pairs={{0,8},{1,2},{2,1},{3,4},{4,3},{5,6},{6,5},{7,15},{8,0},{9,10},{10,... | collective-permute-start | bytes 313352 | tf_op jit(solution)/shard_map/ppermute | solution.py:304
  18.1 7.0 %collective-permute-start.4 = (s16[2,2,4,16,128]{4,3,2,1,0:T(8,128)(2,1)S(1)}, s16[2,2,4,16,128]{4,3,2,1,0:T(8,128)(2,1)S(1)}, u32[]{:S(2)}, u32[]{:S(2)}) collective-permute-start(s16[2,2,4,16,128]{4,3,2,1,0:T(8,128)(2,1)S(1)} %get-tuple-element.22), channel_id=1, source_target_pairs={{0,16},{8,24},{16,0},{24,8},{1,17},{9,25},{17,1},{25,9},{2,18},{10... | collective-permute-start | bytes 196616 | tf_op jit(solution)/shard_map/ppermute | solution.py:337
  25.1 4.3 %collective-permute-start.5 = (s16[2,2,4,16,128]{4,3,2,1,0:T(8,128)(2,1)S(1)}, s16[2,2,4,16,128]{4,3,2,1,0:T(8,128)(2,1)S(1)}, u32[]{:S(2)}, u32[]{:S(2)}) collective-permute-start(s16[2,2,4,16,128]{4,3,2,1,0:T(8,128)(2,1)S(1)} %shard_map.71), channel_id=1, source_target_pairs={{0,4},{1,5},{2,6},{3,7},{4,0},{5,1},{6,2},{7,3},{8,12},{9,13},{10,... | collective-permute-start | bytes 196616 | tf_op jit(solution)/shard_map/ppermute | solution.py:337

commit v5 on v4

--- a/solution.py
+++ b/solution.py
@@ -83,14 +83,47 @@
 def pack_y(own_ref, first_ref, second_ref, near_out, far_out):
     rows = (own_ref.shape[0] - 1) // 2
     cols = own_ref.shape[1]
+    side = 2 * rows
     odd = lax.rem(lax.axis_index("gy"), 2)
     edge = cols - DEEP
-    for out_ref, start in ((near_out, edge - edge * odd), (far_out, edge * odd)):
+    sub = lax.broadcasted_iota(jnp.int32, (DEEP, LANES), 0)
+    sides = ((near_out, edge - edge * odd, odd == 0), (far_out, edge * odd, odd == 1))
+    for out_ref, start, right in sides:
         at = pl.ds(pl.multiple_of(start, DEEP), DEEP)
+        flags = jnp.zeros((DEEP, LANES), jnp.float32)
         for i, part in x_parts(own_ref, first_ref, second_ref):
+            flags = jnp.where(sub == i, part[2 * rows, at, :].astype(jnp.float32), flags)
             for f in range(2):
-                out_ref[pl.ds((3 * f + i) * rows, rows)] = part[pl.ds(f * rows, rows), at, :]
-            out_ref[6 * rows + i] = part[2 * rows, at, :]
+                if part is own_ref:
+                    out_ref[pl.ds(f * side, rows)] = part[pl.ds(f * rows, rows), at, :]
+                    continue
+                for d in range(1, rows // 2 + 1):
+                    a, b = (
+                        part[f * rows + jnp.where(i == 0, rows - e, e - 1), at, :].astype(jnp.float32)
+                        for e in (d, rows - d)
+                    )
+                    if d < rows - d:
+                        a = jnp.where(
+                            right,
+                            jnp.where(sub >= d, a, pltpu.roll(b, d, 0)),
+                            jnp.where(sub < DEEP - d, a, pltpu.roll(b, DEEP - d, 0)),
+                        )
+                    out_ref[f * side + rows + (i // 2) * (rows // 2) + d - 1] = a.astype(jnp.bfloat16)
+        out_ref[2 * side] = flags.astype(jnp.bfloat16)
+
+
+def edge_row(part, field, x, rows, right):
+    side = 2 * rows
+    if rows <= x < 2 * rows:
+        return part[field * side + x - rows].astype(jnp.float32)
+    d = rows - x if x < rows else x - 2 * rows + 1
+    at = field * side + rows + (0 if x < rows else rows // 2) - 1
+    if d <= rows // 2:
+        return part[at + d].astype(jnp.float32)
+    if d == rows:
+        return part[at + rows // 2].astype(jnp.float32)
+    v = part[at + rows - d].astype(jnp.float32)
+    return jnp.where(right, pltpu.roll(v, d, 0), pltpu.roll(v, DEEP - d, 0))
 
 
 def step(
@@ -110,11 +143,12 @@
     odd = lax.rem(lax.axis_index("gy"), 2)
     edge = width - DEEP
     y_parts = (
-        (pl.ds(pl.multiple_of(edge - edge * odd, DEEP), DEEP), yn_ref, None),
+        (pl.ds(pl.multiple_of(edge - edge * odd, DEEP), DEEP), yn_ref, None, odd == 1),
         (
             pl.ds(pl.multiple_of(edge * odd, DEEP), DEEP),
             yf_ref,
             jnp.where(odd == 1, inside("gy", True), inside("gy", False)),
+            odd == 0,
         ),
     )
     own = pl.ds(DEEP, cols)
@@ -125,9 +159,10 @@
 
     for i, part in x_parts(own_ref, xn_ref, xf_ref):
         wide[i, own, :] = part[2 * rows].astype(f32)
-    for at, part, far in y_parts:
+    for at, part, far, _ in y_parts:
+        marks = scaled(part[4 * rows].astype(f32), far)
         for i in range(3):
-            wide[i, at, :] = scaled(part[6 * rows + i].astype(f32), far)
+            wide[i, at, :] = jnp.broadcast_to(marks[i : i + 1], (DEEP, LANES))
     for i in range(3):
         for j in span:
             f = scaled(wide[i, pl.ds(j, SUB, stride=n), :], row_open[i])
@@ -140,9 +175,9 @@
             for r in range(rows):
                 mid = home_ref[r] if part is None else part[field * rows + r].astype(f32)
                 wide[i * rows + r, own, :] = mid
-        for at, part, far in y_parts:
+        for at, part, far, right in y_parts:
             for x in range(total):
-                wide[x, at, :] = scaled(part[field * total + x].astype(f32), far)
+                wide[x, at, :] = scaled(edge_row(part, field, x, rows, right), far)
         for x in range(total):
             for j in span:
                 v = scaled(wide[x, pl.ds(j, SUB, stride=n), :], row_open[x // rows])
@@ -187,7 +222,8 @@
                 v = h - 0.4 * t
                 ks[x, j] = k
                 vs[x, j] = v
-                beside(x, j, v, k)
+                if lo < x < hi - 1:
+                    beside(x, j, v, k)
         along_depth(vs, lo + 1, hi - 1)
 
         def warm(x, j, v, w, acc):
@@ -199,7 +235,8 @@
                 g = hs[x, j]
                 rate = 1.0 + jnp.tanh(2.5 * g - jnp.tanh(g))
                 ks[x, j] = rate
-                beside(x, j, q[x, j], rate)
+                if lo + 1 < x < hi - 2:
+                    beside(x, j, q[x, j], rate)
         along_depth(q, lo + 2, hi - 2)
 
         def fill(x, j, v, w, acc, q_next=q_next):
@@ -351,7 +388,7 @@
         pack_x, "sssvv", [((2 * rows + 1, cols, depth), bf16), block, block, masks]
     )(active, count, slots, enthalpy, porosity)
     x_near, x_far = exchange_x(own)
-    side = ((6 * rows + 3, DEEP, depth), bf16)
+    side = ((4 * rows + 1, DEEP, depth), bf16)
     near, far = call(pack_y, "VVV", [side, side])(own, x_near, x_far)
     y_near, y_far = exchange_y(near, far)
     total, width = rows + 2 * DEEP, cols + 2 * DEEP

time: 30.3 us -> 29.7 us (0.980)
  waiting for transfers between devices: 14.2 us -> 13.3 us
    ppermute x2, waiting for transfers between devices: 7.81 us -> 7.27 us  [swap(): return lax.ppermute(value, axis, [(i, (i + n // 2) % n) for i in range(n)])]
    ppermute x4, waiting for transfers between devices: 6.41 us -> 6.02 us  [permute(): return lax.ppermute(value, ('gx', 'gy'), pairs)]
where the time goes in v5:
time: 29.7 us; the launch traced here: 29.5 us
  waiting for transfers between devices  13.3 us (45%)
  starting transfers between devices  10.2 us (34%)
  Pallas kernels  5.37 us (18%)
  between operations  0.67 us (2%)
    ppermute x2, waiting for transfers between devices, swap(): return lax.ppermute(value, axis, [(i, (i + n // 2) % n) for i in range(n)])  7.27 us
    ppermute x4, starting transfers between devices, permute(): return lax.ppermute(value, ('gx', 'gy'), pairs)  6.49 us
    ppermute x4, waiting for transfers between devices, permute(): return lax.ppermute(value, ('gx', 'gy'), pairs)  6.02 us
    pallas_call x5, Pallas kernels, run(): pl.pallas_call(body, in_specs=[pl.BlockSpec(memory_space=space[c]) for c...  5.37 us
    ppermute x2, starting transfers between devices, swap(): return lax.ppermute(value, axis, [(i, (i + n // 2) % n) for i in range(n)])  3.69 us
  transfers between devices with their start and end apart: 6, of which 5 were waited for; matrix products, arithmetic and copies ran while one was open for 0% of the time, Pallas kernels for 0%

profile of v5, /device:TPU:0, one launch (start us, length us, event | category | flops | bytes accessed | tf_op | source)
XLA Modules:
  0.0 29.5 jit_solution(2802384789952825148)
XLA Ops:
  0.6 1.0 %shard_map.68 = (bf16[17,32,128]{2,1,0:T(8,128)(2,1)S(1)}, f32[8,32,128]{2,1,0:T(8,128)S(1)}, f32[8,32,128]{2,1,0:T(8,128)S(1)}, f32[36,8,128]{2,1,0:T(8,128)S(1)}) custom-call(s32[2,2]{1,0:T(2,128)} %active_ref.1, s32[2]{0:T(128)} %bitcast.5, s32[2,2]{1,0:T(2,128)} %bitcast.4, f32[8,32,128]{2,1,0:T(8,128)} %heat_ref.1, f32[8,32,128]{2,1,0:T(8,128)} %pore_ref.1), custom_call_target="tpu_custom_call" | custom-call | tf_op jit(solution)/shard_map/pallas_call | solution.py:322
  1.7 3.0 %collective-permute-start.1 = (bf16[17,32,128]{2,1,0:T(8,128)(2,1)S(1)}, bf16[17,32,128]{2,1,0:T(8,128)(2,1)S(1)}, u32[]{:S(2)}, u32[]{:S(2)}) collective-permute-start(bf16[17,32,128]{2,1,0:T(8,128)(2,1)S(1)} %get-tuple-element.15.own_ref), channel_id=1, source_target_pairs={{0,2},{1,9},{2,0},{3,11},{4,6},{5,13},{6,4},{7,15},{8,16},{9,1},{1... | collective-permute-start | bytes 417800 | tf_op jit(solution)/shard_map/ppermute | solution.py:341
  4.7 1.7 %collective-permute-start = (bf16[17,32,128]{2,1,0:T(8,128)(2,1)S(1)}, bf16[17,32,128]{2,1,0:T(8,128)(2,1)S(1)}, u32[]{:S(2)}, u32[]{:S(2)}) collective-permute-start(bf16[17,32,128]{2,1,0:T(8,128)(2,1)S(1)} %get-tuple-element.15.own_ref), channel_id=1, source_target_pairs={{0,8},{1,3},{2,10},{3,1},{4,12},{5,7},{6,14},{7,5},{8,0},{9,17},{1... | collective-permute-start | bytes 417800 | tf_op jit(solution)/shard_map/ppermute | solution.py:341
  6.4 2.2 %collective-permute-done.1.second_ref.xf_ref = bf16[17,32,128]{2,1,0:T(8,128)(2,1)S(1)} collective-permute-done((bf16[17,32,128]{2,1,0:T(8,128)(2,1)S(1)}, bf16[17,32,128]{2,1,0:T(8,128)(2,1)S(1)}, u32[]{:S(2)}, u32[]{:S(2)}) %collective-permute-start.1) | collective-permute-done | bytes 139296 | tf_op jit(solution)/shard_map/ppermute | solution.py:341
  8.6 1.2 %collective-permute-done.first_ref.xn_ref = bf16[17,32,128]{2,1,0:T(8,128)(2,1)S(1)} collective-permute-done((bf16[17,32,128]{2,1,0:T(8,128)(2,1)S(1)}, bf16[17,32,128]{2,1,0:T(8,128)(2,1)S(1)}, u32[]{:S(2)}, u32[]{:S(2)}) %collective-permute-start) | collective-permute-done | bytes 139296 | tf_op jit(solution)/shard_map/ppermute | solution.py:341
  9.7 0.1 shard_map.69
  9.8 0.1 collective-permute-start.2
  9.9 1.7 %collective-permute-start.3 = (bf16[33,8,128]{2,1,0:T(8,128)(2,1)S(1)}, bf16[33,8,128]{2,1,0:T(8,128)(2,1)S(1)}, u32[]{:S(2)}, u32[]{:S(2)}) collective-permute-start(bf16[33,8,128]{2,1,0:T(8,128)(2,1)S(1)} %get-tuple-element.19), channel_id=1, source_target_pairs={{0,8},{1,2},{2,1},{3,4},{4,3},{5,6},{6,5},{7,15},{8,0},{9,10},{10,... | collective-permute-start | bytes 202760 | tf_op jit(solution)/shard_map/ppermute | solution.py:341
  11.6 0.0 collective-permute-done.2.yn_ref
  11.6 2.6 %collective-permute-done.3.yf_ref = bf16[33,8,128]{2,1,0:T(8,128)(2,1)S(1)} collective-permute-done((bf16[33,8,128]{2,1,0:T(8,128)(2,1)S(1)}, bf16[33,8,128]{2,1,0:T(8,128)(2,1)S(1)}, u32[]{:S(2)}, u32[]{:S(2)}) %collective-permute-start.3) | collective-permute-done | bytes 67616 | tf_op jit(solution)/shard_map/ppermute | solution.py:341
  14.3 3.5 %shard_map.70 = (f32[4,4,16,128]{3,2,1,0:T(8,128)S(1)}, f32[4,4,16,128]{3,2,1,0:T(8,128)S(1)}, s16[2,2,4,16,128]{4,3,2,1,0:T(8,128)(2,1)S(1)}, s16[2,2,4,16,128]{4,3,2,1,0:T(8,128)(2,1)S(1)}) custom-call(bf16[17,32,128]{2,1,0:T(8,128)(2,1)S(1)} %get-tuple-element.15.own_ref, f32[36,8,128]{2,1,0:T(8,128)S(1)} %get-tuple-element.14.mask_ref, ...), custom_call_target="tpu_custom_call" | custom-call | tf_op jit(solution)/shard_map/pallas_call | solution.py:322
  17.8 2.5 %collective-permute-start.4 = (s16[2,2,4,16,128]{4,3,2,1,0:T(8,128)(2,1)S(1)}, s16[2,2,4,16,128]{4,3,2,1,0:T(8,128)(2,1)S(1)}, u32[]{:S(2)}, u32[]{:S(2)}) collective-permute-start(s16[2,2,4,16,128]{4,3,2,1,0:T(8,128)(2,1)S(1)} %get-tuple-element.22), channel_id=1, source_target_pairs={{0,16},{8,24},{16,0},{24,8},{1,17},{9,25},{17,1},{25,9},{2,18},{10... | collective-permute-start | bytes 196616 | tf_op jit(solution)/shard_map/ppermute | solution.py:374
  20.3 4.1 %collective-permute-done.4.got_ref.first_ref = s16[2,2,4,16,128]{4,3,2,1,0:T(8,128)(2,1)S(1)} collective-permute-done((s16[2,2,4,16,128]{4,3,2,1,0:T(8,128)(2,1)S(1)}, s16[2,2,4,16,128]{4,3,2,1,0:T(8,128)(2,1)S(1)}, u32[]{:S(2)}, u32[]{:S(2)}) %collective-permute-start.4) | collective-permute-done | bytes 65568 | tf_op jit(solution)/shard_map/ppermute | solution.py:374
  24.4 1.2 %collective-permute-start.5 = (s16[2,2,4,16,128]{4,3,2,1,0:T(8,128)(2,1)S(1)}, s16[2,2,4,16,128]{4,3,2,1,0:T(8,128)(2,1)S(1)}, u32[]{:S(2)}, u32[]{:S(2)}) collective-permute-start(s16[2,2,4,16,128]{4,3,2,1,0:T(8,128)(2,1)S(1)} %shard_map.71), channel_id=1, source_target_pairs={{0,4},{1,5},{2,6},{3,7},{4,0},{5,1},{6,2},{7,3},{8,12},{9,13},{10,... | collective-permute-start | bytes 196616 | tf_op jit(solution)/shard_map/ppermute | solution.py:374
  25.6 3.2 %collective-permute-done.5.second_ref = s16[2,2,4,16,128]{4,3,2,1,0:T(8,128)(2,1)S(1)} collective-permute-done((s16[2,2,4,16,128]{4,3,2,1,0:T(8,128)(2,1)S(1)}, s16[2,2,4,16,128]{4,3,2,1,0:T(8,128)(2,1)S(1)}, u32[]{:S(2)}, u32[]{:S(2)}) %collective-permute-start.5) | collective-permute-done | bytes 65568 | tf_op jit(solution)/shard_map/ppermute | solution.py:374
  28.8 0.7 %shard_map.72 = (f32[4,4,16,128]{3,2,1,0:T(8,128)}, f32[4,4,16,128]{3,2,1,0:T(8,128)}) custom-call(f32[36,8,128]{2,1,0:T(8,128)S(1)} %get-tuple-element.14.mask_ref, f32[4,4,16,128]{3,2,1,0:T(8,128)S(1)} %get-tuple-element.20.heat_ref, f32[4,4,16,128]{3,2,1,0:T(8,128)S(1)} %get-tuple-element.21.pore_ref, ...), custom_call_target="tpu_custom_call" | custom-call | tf_op jit(solution)/shard_map/pallas_call | solution.py:322
  (1 shorter events, 0.0 us)
Async XLA Ops:
  1.7 6.9 %collective-permute-start.1 = (bf16[17,32,128]{2,1,0:T(8,128)(2,1)S(1)}, bf16[17,32,128]{2,1,0:T(8,128)(2,1)S(1)}, u32[]{:S(2)}, u32[]{:S(2)}) collective-permute-start(bf16[17,32,128]{2,1,0:T(8,128)(2,1)S(1)} %get-tuple-element.15.own_ref), channel_id=1, source_target_pairs={{0,2},{1,9},{2,0},{3,11},{4,6},{5,13},{6,4},{7,15},{8,16},{9,1},{1... | collective-permute-start | bytes 417800 | tf_op jit(solution)/shard_map/ppermute | solution.py:341
  4.7 5.1 %collective-permute-start = (bf16[17,32,128]{2,1,0:T(8,128)(2,1)S(1)}, bf16[17,32,128]{2,1,0:T(8,128)(2,1)S(1)}, u32[]{:S(2)}, u32[]{:S(2)}) collective-permute-start(bf16[17,32,128]{2,1,0:T(8,128)(2,1)S(1)} %get-tuple-element.15.own_ref), channel_id=1, source_target_pairs={{0,8},{1,3},{2,10},{3,1},{4,12},{5,7},{6,14},{7,5},{8,0},{9,17},{1... | collective-permute-start | bytes 417800 | tf_op jit(solution)/shard_map/ppermute | solution.py:341
  9.8 1.8 %collective-permute-start.2 = (bf16[33,8,128]{2,1,0:T(8,128)(2,1)S(1)}, bf16[33,8,128]{2,1,0:T(8,128)(2,1)S(1)}, u32[]{:S(2)}, u32[]{:S(2)}) collective-permute-start(bf16[33,8,128]{2,1,0:T(8,128)(2,1)S(1)} %get-tuple-element.18), channel_id=1, source_target_pairs={{0,1},{1,0},{2,3},{3,2},{4,5},{5,4},{6,7},{7,6},{8,9},{9,8},{10,11... | collective-permute-start | bytes 202760 | tf_op jit(solution)/shard_map/ppermute | solution.py:341
  9.9 4.4 %collective-permute-start.3 = (bf16[33,8,128]{2,1,0:T(8,128)(2,1)S(1)}, bf16[33,8,128]{2,1,0:T(8,128)(2,1)S(1)}, u32[]{:S(2)}, u32[]{:S(2)}) collective-permute-start(bf16[33,8,128]{2,1,0:T(8,128)(2,1)S(1)} %get-tuple-element.19), channel_id=1, source_target_pairs={{0,8},{1,2},{2,1},{3,4},{4,3},{5,6},{6,5},{7,15},{8,0},{9,10},{10,... | collective-permute-start | bytes 202760 | tf_op jit(solution)/shard_map/ppermute | solution.py:341
  17.8 6.6 %collective-permute-start.4 = (s16[2,2,4,16,128]{4,3,2,1,0:T(8,128)(2,1)S(1)}, s16[2,2,4,16,128]{4,3,2,1,0:T(8,128)(2,1)S(1)}, u32[]{:S(2)}, u32[]{:S(2)}) collective-permute-start(s16[2,2,4,16,128]{4,3,2,1,0:T(8,128)(2,1)S(1)} %get-tuple-element.22), channel_id=1, source_target_pairs={{0,16},{8,24},{16,0},{24,8},{1,17},{9,25},{17,1},{25,9},{2,18},{10... | collective-permute-start | bytes 196616 | tf_op jit(solution)/shard_map/ppermute | solution.py:374
  24.4 4.3 %collective-permute-start.5 = (s16[2,2,4,16,128]{4,3,2,1,0:T(8,128)(2,1)S(1)}, s16[2,2,4,16,128]{4,3,2,1,0:T(8,128)(2,1)S(1)}, u32[]{:S(2)}, u32[]{:S(2)}) collective-permute-start(s16[2,2,4,16,128]{4,3,2,1,0:T(8,128)(2,1)S(1)} %shard_map.71), channel_id=1, source_target_pairs={{0,4},{1,5},{2,6},{3,7},{4,0},{5,1},{6,2},{7,3},{8,12},{9,13},{10,... | collective-permute-start | bytes 196616 | tf_op jit(solution)/shard_map/ppermute | solution.py:374

commit v6 on v5

--- a/solution.py
+++ b/solution.py
@@ -126,133 +126,239 @@
     return jnp.where(right, pltpu.roll(v, d, 0), pltpu.roll(v, DEEP - d, 0))
 
 
-def step(
-    own_ref, mask_ref, heat_ref, pore_ref, xn_ref, xf_ref, yn_ref, yf_ref,
-    heat_out, pore_out, send_ref, later_ref, wide, hs, qa, qb, vs, ks, vz, wz, ms,
+def along_depth(v, w, lane_open):
+    f = (w + pltpu.roll(w, LANES - 1, 1)) * (pltpu.roll(v, LANES - 1, 1) - v)
+    f = jnp.where(lane_open, f, 0.0)
+    return f - pltpu.roll(f, 1, 1)
+
+
+def flux_sum(val, wgt, lo, hi):
+    n = len(val[lo])
+    span = range(n)
+    lane_open = lax.broadcasted_iota(jnp.int32, (SUB, LANES), 1) < LANES - 1
+    depth = {c: [along_depth(val[c][j], wgt[c][j], lane_open) for j in span] for c in range(lo, hi)}
+
+    def toward(c):
+        return [(wgt[c][j] + wgt[c + 1][j]) * (val[c + 1][j] - val[c][j]) for j in span]
+
+    out = {}
+    last = toward(lo - 1)
+    for c in range(lo, hi):
+        v, w = val[c], wgt[c]
+        ahead = toward(c)
+        down = [(w[j] + w[j + 1]) * (v[j + 1] - v[j]) for j in range(n - 1)]
+        down.append(
+            (w[n - 1] + pltpu.roll(w[0], SUB - 1, 0)) * (pltpu.roll(v[0], SUB - 1, 0) - v[n - 1])
+        )
+        up = [pltpu.roll(down[-1], 1, 0)] + down[:-1]
+        out[c] = [(ahead[j] - last[j]) + (down[j] - up[j]) + depth[c][j] for j in span]
+        last = ahead
+    return out
+
+
+def conduct(h, q, mask, lo, hi):
+    temp, cond = {}, {}
+    for c in range(lo - 1, hi + 1):
+        t = [jnp.tanh(v) for v in h[c]]
+        temp[c] = [v - 0.4 * u for v, u in zip(h[c], t)]
+        cond[c] = [(1.0 - v) * (1.0 - v) * (u + 7.0 / 3.0) for v, u in zip(q[c], t)]
+    acc = flux_sum(temp, cond, lo, hi)
+    return {
+        c: [v + m * a for v, m, a in zip(h[c], mask(c, 0), acc[c])] for c in range(lo, hi)
+    }
+
+
+def consolidate(h, q, mask, lo, hi):
+    rate = {
+        c: [1.0 + jnp.tanh(2.5 * v - jnp.tanh(v)) for v in h[c]] for c in range(lo - 1, hi + 1)
+    }
+    acc = flux_sum(q, rate, lo, hi)
+    return {
+        c: [
+            v + m * (a - 4.0 * r * v)
+            for v, m, a, r in zip(q[c], mask(c, 1), acc[c], rate[c])
+        ]
+        for c in range(lo, hi)
+    }
+
+
+def tile_rows(marks, i, tx, n, out):
+    low = lax.broadcasted_iota(jnp.int32, (SUB, LANES), 1) < LANES // 2
+    sub = lax.broadcasted_iota(jnp.int32, (SUB, LANES), 0)
+    other = pltpu.roll(marks, LANES // 2, 1)
+    for h, flag in ((0, jnp.where(low, marks, other)), (1, jnp.where(low, other, marks))):
+        first = (2 * i + h) * tx
+        for j in range(n):
+            x = sub * n + j
+            out[j] = jnp.where((x >= first) & (x < first + tx), flag, out[j])
+    return out
+
+
+def scalings(flags):
+    return ([0.0225 * f for f in flags], [0.0375 * f for f in flags])
+
+
+def inner(
+    own_ref, heat_ref, pore_ref, xa_ref, xb_ref,
+    heat_edge, pore_edge, heat_save, pore_save, heat_mid, pore_mid, flag_out, wide,
 ):
     rows, cols = heat_ref.shape[0], heat_ref.shape[1]
-    tx, ty = rows // 2, cols // 2
     total = rows + 2 * DEEP
     width = cols + 2 * DEEP
-    n = width // SUB
-    span = range(n)
-    lane = lax.broadcasted_iota(jnp.int32, (SUB, LANES), 1)
-    lane_open = lane < LANES - 1
-    low_half = lane < LANES // 2
+    n = total // SUB
+    tx, ty = rows // 2, cols // 2
+    f32 = jnp.float32
+    opens = []
+    parts = x_parts(own_ref, xa_ref, xb_ref)
+    for i, part in parts:
+        opens.append(jnp.where(i == 0, inside("gx", False), inside("gx", True)))
+
+    flags = []
+    for k in range(2):
+        f = [jnp.zeros((SUB, LANES), f32) for _ in range(n)]
+        for (i, part), has in zip(parts, opens):
+            marks = part[2 * rows, pl.ds(k * ty, SUB), :].astype(f32)
+            f = tile_rows(marks if part is own_ref else marks * has, i, tx, n, f)
+        for j in range(n):
+            flag_out[k, j] = f[j]
+        flags.append(scalings(f))
+
+    def mask(c, kind):
+        return flags[0 if c < DEEP + ty else 1][kind]
+
+    h, q = {}, {}
+    for field, home, state in ((0, heat_ref, h), (1, pore_ref, q)):
+        for (i, part), has in zip(parts, opens):
+            for r in range(rows):
+                if part is own_ref:
+                    v = home[r]
+                else:
+                    v = part[field * rows + r].astype(f32) * has
+                at = pl.multiple_of((i * rows + r) * cols, SUB)
+                wide[field, pl.ds(at, cols), :] = 2.0 * v - 2.0 if field == 0 else v
+        for c in range(cols):
+            state[DEEP + c] = [
+                wide[field, pl.ds(j * cols + c, SUB, stride=n * cols), :] for j in range(n)
+            ]
+
+    for p in range(PAIRS):
+        lo, hi = DEEP + 2 * p + 1, width - DEEP - 2 * p - 1
+        for side, c in ((0, lo), (1, hi - 1)):
+            for j in range(n):
+                heat_save[p, side, j] = h[c][j]
+        h.update(conduct(h, q, mask, lo, hi))
+        lo, hi = lo + 1, hi - 1
+        for side, c in ((0, lo), (1, hi - 1)):
+            for j in range(n):
+                pore_save[p, side, j] = q[c][j]
+        q.update(consolidate(h, q, mask, lo, hi))
+
+    for field, state, edge, mid in ((0, h, heat_edge, heat_mid), (1, q, pore_edge, pore_mid)):
+        for c in range(DEEP + 1):
+            for j in range(n):
+                edge[0, c, j] = state[DEEP + c][j]
+                edge[1, c, j] = state[width - DEEP - 1 - c][j]
+        for c in range(DEEP, cols - DEEP):
+            for j in range(n):
+                v = state[DEEP + c][j]
+                wide[field, pl.ds(j * cols + c, SUB, stride=n * cols), :] = (
+                    0.5 * v + 1.0 if field == 0 else v
+                )
+        for r in range(rows):
+            mid[r] = wide[field, pl.ds((DEEP + r) * cols + DEEP, cols - 2 * DEEP), :]
+
+
+def edges(
+    mask_ref, heat_edge, pore_edge, heat_save, pore_save, heat_mid, pore_mid, flag_ref, yn_ref, yf_ref,
+    heat_out, pore_out, send_ref, later_ref, wide, block,
+):
+    rows, cols = heat_mid.shape[0], heat_mid.shape[1] + 2 * DEEP
+    total = rows + 2 * DEEP
+    width = cols + 2 * DEEP
+    n = total // SUB
+    tx, ty = rows // 2, cols // 2
     f32 = jnp.float32
     odd = lax.rem(lax.axis_index("gy"), 2)
-    edge = width - DEEP
-    y_parts = (
-        (pl.ds(pl.multiple_of(edge - edge * odd, DEEP), DEEP), yn_ref, None, odd == 1),
-        (
-            pl.ds(pl.multiple_of(edge * odd, DEEP), DEEP),
-            yf_ref,
-            jnp.where(odd == 1, inside("gy", True), inside("gy", False)),
-            odd == 0,
-        ),
-    )
-    own = pl.ds(DEEP, cols)
     row_open = (inside("gx", False), None, inside("gx", True))
-
-    def scaled(v, by):
-        return v if by is None else v * by
-
-    for i, part in x_parts(own_ref, xn_ref, xf_ref):
-        wide[i, own, :] = part[2 * rows].astype(f32)
-    for at, part, far, _ in y_parts:
-        marks = scaled(part[4 * rows].astype(f32), far)
+    far_open = jnp.where(odd == 1, inside("gy", True), inside("gy", False))
+    parts = ((1 - odd, yn_ref, None, odd == 1), (odd, yf_ref, far_open, odd == 0))
+
+    def scaled(v, *by):
+        for s in by:
+            v = v if s is None else v * s
+        return v
+
+    halves = []
+    for at, part, has, _ in parts:
+        marks = scaled(part[4 * rows].astype(f32), has)
+        f = [jnp.zeros((SUB, LANES), f32) for _ in range(n)]
         for i in range(3):
-            wide[i, at, :] = jnp.broadcast_to(marks[i : i + 1], (DEEP, LANES))
-    for i in range(3):
-        for j in span:
-            f = scaled(wide[i, pl.ds(j, SUB, stride=n), :], row_open[i])
-            r = pltpu.roll(f, LANES // 2, 1)
-            ms[2 * i, j] = jnp.where(low_half, f, r)
-            ms[2 * i + 1, j] = jnp.where(low_half, r, f)
-
-    for field, home_ref, into in ((0, heat_ref, hs), (1, pore_ref, qa)):
-        for i, part in x_parts(None, xn_ref, xf_ref):
-            for r in range(rows):
-                mid = home_ref[r] if part is None else part[field * rows + r].astype(f32)
-                wide[i * rows + r, own, :] = mid
-        for at, part, far, right in y_parts:
+            f = tile_rows(
+                jnp.broadcast_to(scaled(marks[i : i + 1], row_open[i]), (SUB, LANES)), i, tx, n, f
+            )
+        halves.append(f)
+    near, far = halves
+    left = [jnp.where(odd == 1, a, b) for a, b in zip(near, far)]
+    right = [jnp.where(odd == 1, b, a) for a, b in zip(near, far)]
+    flags = [
+        scalings(f)
+        for f in (left, *([flag_ref[k, j] for j in range(n)] for k in range(2)), right)
+    ]
+
+    def mask(c, kind):
+        return flags[0 if c < DEEP else 1 if c < DEEP + ty else 2 if c < DEEP + cols else 3][kind]
+
+    pair = 2 * DEEP
+    h, q = {}, {}
+    for field, edge, state in ((0, heat_edge, h), (1, pore_edge, q)):
+        for at, part, has, right_end in parts:
             for x in range(total):
-                wide[x, at, :] = scaled(edge_row(part, field, x, rows, right), far)
-        for x in range(total):
-            for j in span:
-                v = scaled(wide[x, pl.ds(j, SUB, stride=n), :], row_open[x // rows])
-                into[x, j] = 2.0 * v - 2.0 if field == 0 else v
-
-    def beside(x, j, v, w):
-        vz[x, j] = pltpu.roll(v, LANES - 1, 1)
-        wz[x, j] = pltpu.roll(w, LANES - 1, 1)
-
-    def along_depth(val, lo, hi):
-        for x in range(lo, hi):
-            for j in span:
-                f = (ks[x, j] + wz[x, j]) * (vz[x, j] - val[x, j])
-                f = jnp.where(lane_open, f, 0.0)
-                vz[x, j] = f - pltpu.roll(f, 1, 1)
-
-    def across(val, lo, hi, finish):
-        prev = [(ks[lo - 1, j] + ks[lo, j]) * (val[lo, j] - val[lo - 1, j]) for j in span]
-        for x in range(lo, hi):
-            v = [val[x, j] for j in span]
-            w = [ks[x, j] for j in span]
-            down = [(w[j] + ks[x + 1, j]) * (val[x + 1, j] - v[j]) for j in span]
-            flux = [(w[j] + w[j + 1]) * (v[j + 1] - v[j]) for j in range(n - 1)]
-            flux.append(
-                (w[n - 1] + pltpu.roll(w[0], SUB - 1, 0)) * (pltpu.roll(v[0], SUB - 1, 0) - v[n - 1])
-            )
-            left = [pltpu.roll(flux[-1], 1, 0)] + flux[:-1]
-            for j in span:
-                acc = (down[j] - prev[j]) + (flux[j] - left[j]) + vz[x, j]
-                finish(x, j, v[j], w[j], acc)
-            prev = down
-
-    q, q_next = qa, qb
+                v = scaled(edge_row(part, field, x, rows, right_end), has, row_open[x // rows])
+                into = pl.multiple_of(x * pair + at * DEEP, SUB)
+                wide[field, pl.ds(into, DEEP), :] = 2.0 * v - 2.0 if field == 0 else v
+        for c in range(DEEP):
+            for first, halo in ((0, c), (DEEP, width - DEEP + c)):
+                state[halo] = [
+                    wide[field, pl.ds(j * pair + first + c, SUB, stride=n * pair), :]
+                    for j in range(n)
+                ]
+        for c in range(DEEP + 1):
+            state[DEEP + c] = [edge[0, c, j] for j in range(n)]
+            state[width - DEEP - 1 - c] = [edge[1, c, j] for j in range(n)]
+
     for p in range(PAIRS):
-        lo, hi = 2 * p, total - 2 * p
-        for x in range(lo, hi):
-            for j in span:
-                h = hs[x, j]
-                t = jnp.tanh(h)
-                solid = 1.0 - q[x, j]
-                k = solid * solid * (t + 7.0 / 3.0)
-                v = h - 0.4 * t
-                ks[x, j] = k
-                vs[x, j] = v
-                if lo < x < hi - 1:
-                    beside(x, j, v, k)
-        along_depth(vs, lo + 1, hi - 1)
-
-        def warm(x, j, v, w, acc):
-            hs[x, j] = hs[x, j] + (0.0225 * ms[x // tx, j]) * acc
-
-        across(vs, lo + 1, hi - 1, warm)
-        for x in range(lo + 1, hi - 1):
-            for j in span:
-                g = hs[x, j]
-                rate = 1.0 + jnp.tanh(2.5 * g - jnp.tanh(g))
-                ks[x, j] = rate
-                if lo + 1 < x < hi - 2:
-                    beside(x, j, q[x, j], rate)
-        along_depth(q, lo + 2, hi - 2)
-
-        def fill(x, j, v, w, acc, q_next=q_next):
-            q_next[x, j] = v + (0.0375 * ms[x // tx, j]) * (acc - 4.0 * w * v)
-
-        across(q, lo + 2, hi - 2, fill)
-        q, q_next = q_next, q
-
-    for src, out, field in ((hs, heat_out, 0), (q, pore_out, 1)):
+        lo = 2 * p + 1
+        hi = width - lo
+        new = {}
+        for side, a, b, c in ((0, lo, lo + DEEP, lo + DEEP), (1, hi - DEEP, hi, hi - DEEP - 1)):
+            then = dict(h)
+            then[c] = [heat_save[p, side, j] for j in range(n)]
+            new.update(conduct(then, q, mask, a, b))
+        h.update(new)
+        lo, hi = lo + 1, hi - 1
+        new = {}
+        for side, a, b, c in ((0, lo, lo + DEEP, lo + DEEP), (1, hi - DEEP, hi, hi - DEEP - 1)):
+            then = dict(q)
+            then[c] = [pore_save[p, side, j] for j in range(n)]
+            new.update(consolidate(h, then, mask, a, b))
+        q.update(new)
+
+    for field, state, mid, out in ((0, h, heat_mid, heat_out), (1, q, pore_mid, pore_out)):
+        for c in range(DEEP):
+            for first, own in ((0, DEEP + c), (DEEP, width - pair + c)):
+                for j in range(n):
+                    v = state[own][j]
+                    wide[field, pl.ds(j * pair + first + c, SUB, stride=n * pair), :] = (
+                        0.5 * v + 1.0 if field == 0 else v
+                    )
         for r in range(rows):
-            for j in span:
-                v = src[DEEP + r, j]
-                wide[r, pl.ds(j, SUB, stride=n), :] = 0.5 * v + 1.0 if field == 0 else v
+            row = (DEEP + r) * pair
+            block[field, r, 0:DEEP] = wide[field, pl.ds(row, DEEP), :]
+            block[field, r, DEEP : cols - DEEP] = mid[r]
+            block[field, r, cols - DEEP :] = wide[field, pl.ds(row + DEEP, DEEP), :]
         for i in range(2):
             for k in range(2):
-                out[2 * i + k] = wide[i * tx : (i + 1) * tx, DEEP + k * ty : DEEP + (k + 1) * ty, :]
+                out[2 * i + k] = block[field, i * tx : (i + 1) * tx, k * ty : (k + 1) * ty, :]
     ranks = send_ref.shape[0]
     choose = mask_at(ranks)[0]
     shape = (tx, ty, LANES)
@@ -391,16 +497,25 @@
     side = ((4 * rows + 1, DEEP, depth), bf16)
     near, far = call(pack_y, "VVV", [side, side])(own, x_near, x_far)
     y_near, y_far = exchange_y(near, far)
-    total, width = rows + 2 * DEEP, cols + 2 * DEEP
+    total = rows + 2 * DEEP
+    n = total // SUB
     tiles = ((4, tx, ty, depth), f32)
     parcel = ((ranks, 2, tx, ty, depth), i16)
-    split = pltpu.VMEM((total, width // SUB, SUB, depth), f32)
+    edge = ((2, DEEP + 1, n, SUB, depth), f32)
+    save = ((PAIRS, 2, n, SUB, depth), f32)
+    mid = ((rows, cols - 2 * DEEP, depth), f32)
+    flag = ((2, n, SUB, depth), f32)
+    state = call(
+        inner, "VVVVV", [edge, edge, save, save, mid, mid, flag],
+        [pltpu.VMEM((2, total * cols, depth), f32)],
+    )(own, enthalpy, porosity, x_near, x_far)
     heat, pore, first, later = call(
-        step, "VVVVVVVV", [tiles, tiles, parcel, parcel],
-        [pltpu.VMEM((total, width, depth), f32)]
-        + [split] * 7
-        + [pltpu.VMEM((total // tx, width // SUB, SUB, depth), f32)],
-    )(own, masks, enthalpy, porosity, x_near, x_far, y_near, y_far)
+        edges, "V" * 10, [tiles, tiles, parcel, parcel],
+        [
+            pltpu.VMEM((2, total * 2 * DEEP, depth), f32),
+            pltpu.VMEM((2, rows, cols, depth), f32),
+        ],
+    )(masks, *state, y_near, y_far)
     first = swap(first, "gx")
     (second,) = call(resend, "VVV", [parcel])(masks, first, later)
     second = swap(second, "gy")

time: 29.7 us -> 75.4 us (2.54)
  Pallas kernels: 5.37 us -> 54 us
  waiting for transfers between devices: 13.3 us -> 10.1 us
    pallas_call x5 -> x6, Pallas kernels: 5.37 us -> 54 us  [run(): pl.pallas_call(body, in_specs=[pl.BlockSpec(memory_space=space[c]) for c...]
    ppermute x4, waiting for transfers between devices: 6.02 us -> 3.57 us  [permute(): return lax.ppermute(value, ('gx', 'gy'), pairs)]
  transfers between devices with their start and end apart: 6 -> 6, of which waited for: 5 -> 4; matrix products, arithmetic and copies ran while one was open for 0% -> 0% of each run, Pallas kernels for 0% -> 48%
where the time goes in v6:
time: 75.4 us; the launch traced here: 75.3 us
  Pallas kernels  54 us (72%)
  starting transfers between devices  10.5 us (14%)
  waiting for transfers between devices  10.1 us (13%)
    pallas_call x6, Pallas kernels, run(): pl.pallas_call(body, in_specs=[pl.BlockSpec(memory_space=space[c]) for c...  54 us
    ppermute x2, waiting for transfers between devices, swap(): return lax.ppermute(value, axis, [(i, (i + n // 2) % n) for i in range(n)])  6.56 us
    ppermute x4, starting transfers between devices, permute(): return lax.ppermute(value, ('gx', 'gy'), pairs)  6.11 us
    ppermute x2, starting transfers between devices, swap(): return lax.ppermute(value, axis, [(i, (i + n // 2) % n) for i in range(n)])  4.4 us
    ppermute x4, waiting for transfers between devices, permute(): return lax.ppermute(value, ('gx', 'gy'), pairs)  3.57 us
  transfers between devices with their start and end apart: 6, of which 4 were waited for; matrix products, arithmetic and copies ran while one was open for 0% of the time, Pallas kernels for 48%

profile of v6, /device:TPU:0, one launch (start us, length us, event | category | flops | bytes accessed | tf_op | source)
XLA Modules:
  0.0 75.3 jit_solution(11251153905345551305)
XLA Ops:
  0.6 1.0 %shard_map.68 = (bf16[17,32,128]{2,1,0:T(8,128)(2,1)S(1)}, f32[8,32,128]{2,1,0:T(8,128)S(1)}, f32[8,32,128]{2,1,0:T(8,128)S(1)}, f32[36,8,128]{2,1,0:T(8,128)S(1)}) custom-call(s32[2,2]{1,0:T(2,128)} %active_ref.1, s32[2]{0:T(128)} %bitcast.5, s32[2,2]{1,0:T(2,128)} %bitcast.4, f32[8,32,128]{2,1,0:T(8,128)} %heat_ref.1, f32[8,32,128]{2,1,0:T(8,128)} %pore_ref.1), custom_call_target="tpu_custom_call" | custom-call | tf_op jit(solution)/shard_map/pallas_call | solution.py:428
  1.7 3.1 %collective-permute-start = (bf16[17,32,128]{2,1,0:T(8,128)(2,1)S(1)}, bf16[17,32,128]{2,1,0:T(8,128)(2,1)S(1)}, u32[]{:S(2)}, u32[]{:S(2)}) collective-permute-start(bf16[17,32,128]{2,1,0:T(8,128)(2,1)S(1)} %get-tuple-element.22.own_ref), channel_id=1, source_target_pairs={{0,8},{1,3},{2,10},{3,1},{4,12},{5,7},{6,14},{7,5},{8,0},{9,17},{1... | collective-permute-start | bytes 417800 | tf_op jit(solution)/shard_map/ppermute | solution.py:447
  4.8 1.5 %collective-permute-start.1 = (bf16[17,32,128]{2,1,0:T(8,128)(2,1)S(1)}, bf16[17,32,128]{2,1,0:T(8,128)(2,1)S(1)}, u32[]{:S(2)}, u32[]{:S(2)}) collective-permute-start(bf16[17,32,128]{2,1,0:T(8,128)(2,1)S(1)} %get-tuple-element.22.own_ref), channel_id=1, source_target_pairs={{0,2},{1,9},{2,0},{3,11},{4,6},{5,13},{6,4},{7,15},{8,16},{9,1},{1... | collective-permute-start | bytes 417800 | tf_op jit(solution)/shard_map/ppermute | solution.py:447
  6.3 2.5 %collective-permute-done.xa_ref.first_ref = bf16[17,32,128]{2,1,0:T(8,128)(2,1)S(1)} collective-permute-done((bf16[17,32,128]{2,1,0:T(8,128)(2,1)S(1)}, bf16[17,32,128]{2,1,0:T(8,128)(2,1)S(1)}, u32[]{:S(2)}, u32[]{:S(2)}) %collective-permute-start) | collective-permute-done | bytes 139296 | tf_op jit(solution)/shard_map/ppermute | solution.py:447
  8.8 1.0 %collective-permute-done.1.xb_ref.second_ref = bf16[17,32,128]{2,1,0:T(8,128)(2,1)S(1)} collective-permute-done((bf16[17,32,128]{2,1,0:T(8,128)(2,1)S(1)}, bf16[17,32,128]{2,1,0:T(8,128)(2,1)S(1)}, u32[]{:S(2)}, u32[]{:S(2)}) %collective-permute-start.1) | collective-permute-done | bytes 139296 | tf_op jit(solution)/shard_map/ppermute | solution.py:447
  9.8 0.1 shard_map.70
  9.9 0.1 collective-permute-start.2
  10.0 1.4 %collective-permute-start.3 = (bf16[33,8,128]{2,1,0:T(8,128)(2,1)S(1)}, bf16[33,8,128]{2,1,0:T(8,128)(2,1)S(1)}, u32[]{:S(2)}, u32[]{:S(2)}) collective-permute-start(bf16[33,8,128]{2,1,0:T(8,128)(2,1)S(1)} %get-tuple-element.33), channel_id=1, source_target_pairs={{0,8},{1,2},{2,1},{3,4},{4,3},{5,6},{6,5},{7,15},{8,0},{9,10},{10,... | collective-permute-start | bytes 202760 | tf_op jit(solution)/shard_map/ppermute | solution.py:447
  11.4 36.0 %shard_map.69 = (f32[2,9,3,8,128]{4,3,2,1,0:T(8,128)S(1)}, f32[2,9,3,8,128]{4,3,2,1,0:T(8,128)S(1)}, f32[4,2,3,8,128]{4,3,2,1,0:T(8,128)S(1)}, f32[4,2,3,8,128]{...) custom-call(bf16[17,32,128]{2,1,0:T(8,128)(2,1)S(1)} %get-tuple-element.2, ...), custom_call_target="tpu_custom_call" | custom-call | tf_op jit(solution)/shard_map/pallas_call | solution.py:428
  47.4 0.0 collective-permute-done.2.yn_ref
  47.4 0.0 collective-permute-done.3.yf_ref
  47.5 16.1 %shard_map.71 = (f32[4,4,16,128]{3,2,1,0:T(8,128)S(1)}, f32[4,4,16,128]{3,2,1,0:T(8,128)S(1)}, s16[2,2,4,16,128]{4,3,2,1,0:T(8,128)(2,1)S(1)}, s16[2,2,4,16,128]{4,3,2,1,0:T(8,128)(2,1)S(1)}) custom-call(f32[36,8,128]{2,1,0:T(8,128)S(1)} %get-tuple-element.21.mask_ref, f32[2,9,3,8,128]{4,3,2,1,0:T(8,128)S(1)} %get-tuple-element.25.heat_edge, ...), custom_call_target="tpu_custom_call" | custom-call | tf_op jit(solution)/shard_map/pallas_call | solution.py:428
  63.6 2.7 %collective-permute-start.4 = (s16[2,2,4,16,128]{4,3,2,1,0:T(8,128)(2,1)S(1)}, s16[2,2,4,16,128]{4,3,2,1,0:T(8,128)(2,1)S(1)}, u32[]{:S(2)}, u32[]{:S(2)}) collective-permute-start(s16[2,2,4,16,128]{4,3,2,1,0:T(8,128)(2,1)S(1)} %get-tuple-element.36), channel_id=1, source_target_pairs={{0,16},{8,24},{16,0},{24,8},{1,17},{9,25},{17,1},{25,9},{2,18},{10... | collective-permute-start | bytes 196616 | tf_op jit(solution)/shard_map/ppermute | solution.py:480
  66.3 3.9 %collective-permute-done.4.got_ref.first_ref = s16[2,2,4,16,128]{4,3,2,1,0:T(8,128)(2,1)S(1)} collective-permute-done((s16[2,2,4,16,128]{4,3,2,1,0:T(8,128)(2,1)S(1)}, s16[2,2,4,16,128]{4,3,2,1,0:T(8,128)(2,1)S(1)}, u32[]{:S(2)}, u32[]{:S(2)}) %collective-permute-start.4) | collective-permute-done | bytes 65568 | tf_op jit(solution)/shard_map/ppermute | solution.py:480
  70.2 1.7 %collective-permute-start.5 = (s16[2,2,4,16,128]{4,3,2,1,0:T(8,128)(2,1)S(1)}, s16[2,2,4,16,128]{4,3,2,1,0:T(8,128)(2,1)S(1)}, u32[]{:S(2)}, u32[]{:S(2)}) collective-permute-start(s16[2,2,4,16,128]{4,3,2,1,0:T(8,128)(2,1)S(1)} %shard_map.72), channel_id=1, source_target_pairs={{0,4},{1,5},{2,6},{3,7},{4,0},{5,1},{6,2},{7,3},{8,12},{9,13},{10,... | collective-permute-start | bytes 196616 | tf_op jit(solution)/shard_map/ppermute | solution.py:480
  71.9 2.7 %collective-permute-done.5.second_ref = s16[2,2,4,16,128]{4,3,2,1,0:T(8,128)(2,1)S(1)} collective-permute-done((s16[2,2,4,16,128]{4,3,2,1,0:T(8,128)(2,1)S(1)}, s16[2,2,4,16,128]{4,3,2,1,0:T(8,128)(2,1)S(1)}, u32[]{:S(2)}, u32[]{:S(2)}) %collective-permute-start.5) | collective-permute-done | bytes 65568 | tf_op jit(solution)/shard_map/ppermute | solution.py:480
  74.6 0.7 shard_map.73
  (1 shorter events, 0.0 us)
Async XLA Ops:
  1.7 7.1 %collective-permute-start = (bf16[17,32,128]{2,1,0:T(8,128)(2,1)S(1)}, bf16[17,32,128]{2,1,0:T(8,128)(2,1)S(1)}, u32[]{:S(2)}, u32[]{:S(2)}) collective-permute-start(bf16[17,32,128]{2,1,0:T(8,128)(2,1)S(1)} %get-tuple-element.22.own_ref), channel_id=1, source_target_pairs={{0,8},{1,3},{2,10},{3,1},{4,12},{5,7},{6,14},{7,5},{8,0},{9,17},{1... | collective-permute-start | bytes 417800 | tf_op jit(solution)/shard_map/ppermute | solution.py:447
  4.8 5.1 %collective-permute-start.1 = (bf16[17,32,128]{2,1,0:T(8,128)(2,1)S(1)}, bf16[17,32,128]{2,1,0:T(8,128)(2,1)S(1)}, u32[]{:S(2)}, u32[]{:S(2)}) collective-permute-start(bf16[17,32,128]{2,1,0:T(8,128)(2,1)S(1)} %get-tuple-element.22.own_ref), channel_id=1, source_target_pairs={{0,2},{1,9},{2,0},{3,11},{4,6},{5,13},{6,4},{7,15},{8,16},{9,1},{1... | collective-permute-start | bytes 417800 | tf_op jit(solution)/shard_map/ppermute | solution.py:447
  9.9 37.5 %collective-permute-start.2 = (bf16[33,8,128]{2,1,0:T(8,128)(2,1)S(1)}, bf16[33,8,128]{2,1,0:T(8,128)(2,1)S(1)}, u32[]{:S(2)}, u32[]{:S(2)}) collective-permute-start(bf16[33,8,128]{2,1,0:T(8,128)(2,1)S(1)} %get-tuple-element.32), channel_id=1, source_target_pairs={{0,1},{1,0},{2,3},{3,2},{4,5},{5,4},{6,7},{7,6},{8,9},{9,8},{10,11... | collective-permute-start | bytes 202760 | tf_op jit(solution)/shard_map/ppermute | solution.py:447
  10.0 37.5 %collective-permute-start.3 = (bf16[33,8,128]{2,1,0:T(8,128)(2,1)S(1)}, bf16[33,8,128]{2,1,0:T(8,128)(2,1)S(1)}, u32[]{:S(2)}, u32[]{:S(2)}) collective-permute-start(bf16[33,8,128]{2,1,0:T(8,128)(2,1)S(1)} %get-tuple-element.33), channel_id=1, source_target_pairs={{0,8},{1,2},{2,1},{3,4},{4,3},{5,6},{6,5},{7,15},{8,0},{9,10},{10,... | collective-permute-start | bytes 202760 | tf_op jit(solution)/shard_map/ppermute | solution.py:447
  63.6 6.6 %collective-permute-start.4 = (s16[2,2,4,16,128]{4,3,2,1,0:T(8,128)(2,1)S(1)}, s16[2,2,4,16,128]{4,3,2,1,0:T(8,128)(2,1)S(1)}, u32[]{:S(2)}, u32[]{:S(2)}) collective-permute-start(s16[2,2,4,16,128]{4,3,2,1,0:T(8,128)(2,1)S(1)} %get-tuple-element.36), channel_id=1, source_target_pairs={{0,16},{8,24},{16,0},{24,8},{1,17},{9,25},{17,1},{25,9},{2,18},{10... | collective-permute-start | bytes 196616 | tf_op jit(solution)/shard_map/ppermute | solution.py:480
  70.2 4.3 %collective-permute-start.5 = (s16[2,2,4,16,128]{4,3,2,1,0:T(8,128)(2,1)S(1)}, s16[2,2,4,16,128]{4,3,2,1,0:T(8,128)(2,1)S(1)}, u32[]{:S(2)}, u32[]{:S(2)}) collective-permute-start(s16[2,2,4,16,128]{4,3,2,1,0:T(8,128)(2,1)S(1)} %shard_map.72), channel_id=1, source_target_pairs={{0,4},{1,5},{2,6},{3,7},{4,0},{5,1},{6,2},{7,3},{8,12},{9,13},{10,... | collective-permute-start | bytes 196616 | tf_op jit(solution)/shard_map/ppermute | solution.py:480

commit v7 on v6

--- a/solution.py
+++ b/solution.py
@@ -126,17 +126,19 @@
     return jnp.where(right, pltpu.roll(v, d, 0), pltpu.roll(v, DEEP - d, 0))
 
 
-def along_depth(v, w, lane_open):
-    f = (w + pltpu.roll(w, LANES - 1, 1)) * (pltpu.roll(v, LANES - 1, 1) - v)
-    f = jnp.where(lane_open, f, 0.0)
-    return f - pltpu.roll(f, 1, 1)
-
-
 def flux_sum(val, wgt, lo, hi):
     n = len(val[lo])
     span = range(n)
     lane_open = lax.broadcasted_iota(jnp.int32, (SUB, LANES), 1) < LANES - 1
-    depth = {c: [along_depth(val[c][j], wgt[c][j], lane_open) for j in span] for c in range(lo, hi)}
+    each = [(c, j) for c in range(lo, hi) for j in span]
+    deeper = [
+        (pltpu.roll(val[c][j], LANES - 1, 1), pltpu.roll(wgt[c][j], LANES - 1, 1)) for c, j in each
+    ]
+    depth = {}
+    for (c, j), (v, w) in zip(each, deeper):
+        depth[c, j] = jnp.where(lane_open, (wgt[c][j] + w) * (v - val[c][j]), 0.0)
+    for at in each:
+        depth[at] = depth[at] - pltpu.roll(depth[at], 1, 1)
 
     def toward(c):
         return [(wgt[c][j] + wgt[c + 1][j]) * (val[c + 1][j] - val[c][j]) for j in span]
@@ -151,7 +153,7 @@
             (w[n - 1] + pltpu.roll(w[0], SUB - 1, 0)) * (pltpu.roll(v[0], SUB - 1, 0) - v[n - 1])
         )
         up = [pltpu.roll(down[-1], 1, 0)] + down[:-1]
-        out[c] = [(ahead[j] - last[j]) + (down[j] - up[j]) + depth[c][j] for j in span]
+        out[c] = [(ahead[j] - last[j]) + (down[j] - up[j]) + depth[c, j] for j in span]
         last = ahead
     return out
 

time: 75.4 us -> 29.2 us (0.39)
  Pallas kernels: 54 us -> 7.67 us
    pallas_call x6, Pallas kernels: 54 us -> 7.67 us  [run(): pl.pallas_call(body, in_specs=[pl.BlockSpec(memory_space=space[c]) for c...]
  transfers between devices with their start and end apart: 6 -> 6, of which waited for: 4 -> 4; matrix products, arithmetic and copies ran while one was open for 0% -> 0% of each run, Pallas kernels for 48% -> 11%
where the time goes in v7:
time: 29.2 us; the launch traced here: 29 us
  starting transfers between devices  10.5 us (36%)
  waiting for transfers between devices  10.1 us (35%)
  Pallas kernels  7.67 us (26%)
  between operations  0.69 us (2%)
    pallas_call x6, Pallas kernels, run(): pl.pallas_call(body, in_specs=[pl.BlockSpec(memory_space=space[c]) for c...  7.67 us
    ppermute x2, waiting for transfers between devices, swap(): return lax.ppermute(value, axis, [(i, (i + n // 2) % n) for i in range(n)])  6.56 us
    ppermute x4, starting transfers between devices, permute(): return lax.ppermute(value, ('gx', 'gy'), pairs)  6.11 us
    ppermute x2, starting transfers between devices, swap(): return lax.ppermute(value, axis, [(i, (i + n // 2) % n) for i in range(n)])  4.4 us
    ppermute x4, waiting for transfers between devices, permute(): return lax.ppermute(value, ('gx', 'gy'), pairs)  3.57 us
  transfers between devices with their start and end apart: 6, of which 4 were waited for; matrix products, arithmetic and copies ran while one was open for 0% of the time, Pallas kernels for 11%

profile of v7, /device:TPU:0, one launch (start us, length us, event | category | flops | bytes accessed | tf_op | source)
XLA Modules:
  0.0 29.0 jit_solution(12629924591704613691)
XLA Ops:
  0.6 1.0 %shard_map.68 = (bf16[17,32,128]{2,1,0:T(8,128)(2,1)S(1)}, f32[8,32,128]{2,1,0:T(8,128)S(1)}, f32[8,32,128]{2,1,0:T(8,128)S(1)}, f32[36,8,128]{2,1,0:T(8,128)S(1)}) custom-call(s32[2,2]{1,0:T(2,128)} %active_ref.1, s32[2]{0:T(128)} %bitcast.5, s32[2,2]{1,0:T(2,128)} %bitcast.4, f32[8,32,128]{2,1,0:T(8,128)} %heat_ref.1, f32[8,32,128]{2,1,0:T(8,128)} %pore_ref.1), custom_call_target="tpu_custom_call" | custom-call | tf_op jit(solution)/shard_map/pallas_call | solution.py:430
  1.7 3.1 %collective-permute-start = (bf16[17,32,128]{2,1,0:T(8,128)(2,1)S(1)}, bf16[17,32,128]{2,1,0:T(8,128)(2,1)S(1)}, u32[]{:S(2)}, u32[]{:S(2)}) collective-permute-start(bf16[17,32,128]{2,1,0:T(8,128)(2,1)S(1)} %get-tuple-element.22.own_ref), channel_id=1, source_target_pairs={{0,8},{1,3},{2,10},{3,1},{4,12},{5,7},{6,14},{7,5},{8,0},{9,17},{1... | collective-permute-start | bytes 417800 | tf_op jit(solution)/shard_map/ppermute | solution.py:449
  4.8 1.5 %collective-permute-start.1 = (bf16[17,32,128]{2,1,0:T(8,128)(2,1)S(1)}, bf16[17,32,128]{2,1,0:T(8,128)(2,1)S(1)}, u32[]{:S(2)}, u32[]{:S(2)}) collective-permute-start(bf16[17,32,128]{2,1,0:T(8,128)(2,1)S(1)} %get-tuple-element.22.own_ref), channel_id=1, source_target_pairs={{0,2},{1,9},{2,0},{3,11},{4,6},{5,13},{6,4},{7,15},{8,16},{9,1},{1... | collective-permute-start | bytes 417800 | tf_op jit(solution)/shard_map/ppermute | solution.py:449
  6.3 2.5 %collective-permute-done.xa_ref.first_ref = bf16[17,32,128]{2,1,0:T(8,128)(2,1)S(1)} collective-permute-done((bf16[17,32,128]{2,1,0:T(8,128)(2,1)S(1)}, bf16[17,32,128]{2,1,0:T(8,128)(2,1)S(1)}, u32[]{:S(2)}, u32[]{:S(2)}) %collective-permute-start) | collective-permute-done | bytes 139296 | tf_op jit(solution)/shard_map/ppermute | solution.py:449
  8.8 1.0 %collective-permute-done.1.xb_ref.second_ref = bf16[17,32,128]{2,1,0:T(8,128)(2,1)S(1)} collective-permute-done((bf16[17,32,128]{2,1,0:T(8,128)(2,1)S(1)}, bf16[17,32,128]{2,1,0:T(8,128)(2,1)S(1)}, u32[]{:S(2)}, u32[]{:S(2)}) %collective-permute-start.1) | collective-permute-done | bytes 139296 | tf_op jit(solution)/shard_map/ppermute | solution.py:449
  9.8 0.1 shard_map.70
  9.9 0.1 collective-permute-start.2
  10.0 1.4 %collective-permute-start.3 = (bf16[33,8,128]{2,1,0:T(8,128)(2,1)S(1)}, bf16[33,8,128]{2,1,0:T(8,128)(2,1)S(1)}, u32[]{:S(2)}, u32[]{:S(2)}) collective-permute-start(bf16[33,8,128]{2,1,0:T(8,128)(2,1)S(1)} %get-tuple-element.33), channel_id=1, source_target_pairs={{0,8},{1,2},{2,1},{3,4},{4,3},{5,6},{6,5},{7,15},{8,0},{9,10},{10,... | collective-permute-start | bytes 202760 | tf_op jit(solution)/shard_map/ppermute | solution.py:449
  11.4 3.3 %shard_map.69 = (f32[2,9,3,8,128]{4,3,2,1,0:T(8,128)S(1)}, f32[2,9,3,8,128]{4,3,2,1,0:T(8,128)S(1)}, f32[4,2,3,8,128]{4,3,2,1,0:T(8,128)S(1)}, f32[4,2,3,8,128]{...) custom-call(bf16[17,32,128]{2,1,0:T(8,128)(2,1)S(1)} %get-tuple-element.2, ...), custom_call_target="tpu_custom_call" | custom-call | tf_op jit(solution)/shard_map/pallas_call | solution.py:430
  14.7 0.0 collective-permute-done.2.yn_ref
  14.7 0.0 collective-permute-done.3.yf_ref
  14.7 2.5 %shard_map.71 = (f32[4,4,16,128]{3,2,1,0:T(8,128)S(1)}, f32[4,4,16,128]{3,2,1,0:T(8,128)S(1)}, s16[2,2,4,16,128]{4,3,2,1,0:T(8,128)(2,1)S(1)}, s16[2,2,4,16,128]{4,3,2,1,0:T(8,128)(2,1)S(1)}) custom-call(f32[36,8,128]{2,1,0:T(8,128)S(1)} %get-tuple-element.21.mask_ref, f32[2,9,3,8,128]{4,3,2,1,0:T(8,128)S(1)} %get-tuple-element.25.heat_edge, ...), custom_call_target="tpu_custom_call" | custom-call | tf_op jit(solution)/shard_map/pallas_call | solution.py:430
  17.3 2.7 %collective-permute-start.4 = (s16[2,2,4,16,128]{4,3,2,1,0:T(8,128)(2,1)S(1)}, s16[2,2,4,16,128]{4,3,2,1,0:T(8,128)(2,1)S(1)}, u32[]{:S(2)}, u32[]{:S(2)}) collective-permute-start(s16[2,2,4,16,128]{4,3,2,1,0:T(8,128)(2,1)S(1)} %get-tuple-element.36), channel_id=1, source_target_pairs={{0,16},{8,24},{16,0},{24,8},{1,17},{9,25},{17,1},{25,9},{2,18},{10... | collective-permute-start | bytes 196616 | tf_op jit(solution)/shard_map/ppermute | solution.py:482
  20.0 3.9 %collective-permute-done.4.got_ref.first_ref = s16[2,2,4,16,128]{4,3,2,1,0:T(8,128)(2,1)S(1)} collective-permute-done((s16[2,2,4,16,128]{4,3,2,1,0:T(8,128)(2,1)S(1)}, s16[2,2,4,16,128]{4,3,2,1,0:T(8,128)(2,1)S(1)}, u32[]{:S(2)}, u32[]{:S(2)}) %collective-permute-start.4) | collective-permute-done | bytes 65568 | tf_op jit(solution)/shard_map/ppermute | solution.py:482
  23.9 1.7 %collective-permute-start.5 = (s16[2,2,4,16,128]{4,3,2,1,0:T(8,128)(2,1)S(1)}, s16[2,2,4,16,128]{4,3,2,1,0:T(8,128)(2,1)S(1)}, u32[]{:S(2)}, u32[]{:S(2)}) collective-permute-start(s16[2,2,4,16,128]{4,3,2,1,0:T(8,128)(2,1)S(1)} %shard_map.72), channel_id=1, source_target_pairs={{0,4},{1,5},{2,6},{3,7},{4,0},{5,1},{6,2},{7,3},{8,12},{9,13},{10,... | collective-permute-start | bytes 196616 | tf_op jit(solution)/shard_map/ppermute | solution.py:482
  25.6 2.7 %collective-permute-done.5.second_ref = s16[2,2,4,16,128]{4,3,2,1,0:T(8,128)(2,1)S(1)} collective-permute-done((s16[2,2,4,16,128]{4,3,2,1,0:T(8,128)(2,1)S(1)}, s16[2,2,4,16,128]{4,3,2,1,0:T(8,128)(2,1)S(1)}, u32[]{:S(2)}, u32[]{:S(2)}) %collective-permute-start.5) | collective-permute-done | bytes 65568 | tf_op jit(solution)/shard_map/ppermute | solution.py:482
  28.3 0.7 %shard_map.73 = (f32[4,4,16,128]{3,2,1,0:T(8,128)}, f32[4,4,16,128]{3,2,1,0:T(8,128)}) custom-call(f32[36,8,128]{2,1,0:T(8,128)S(1)} %get-tuple-element.21.mask_ref, f32[4,4,16,128]{3,2,1,0:T(8,128)S(1)} %get-tuple-element.34.heat_ref, f32[4,4,16,128]{3,2,1,0:T(8,128)S(1)} %get-tuple-element.35.pore_ref, ...), custom_call_target="tpu_custom_call" | custom-call | tf_op jit(solution)/shard_map/pallas_call | solution.py:430
  (1 shorter events, 0.0 us)
Async XLA Ops:
  1.7 7.1 %collective-permute-start = (bf16[17,32,128]{2,1,0:T(8,128)(2,1)S(1)}, bf16[17,32,128]{2,1,0:T(8,128)(2,1)S(1)}, u32[]{:S(2)}, u32[]{:S(2)}) collective-permute-start(bf16[17,32,128]{2,1,0:T(8,128)(2,1)S(1)} %get-tuple-element.22.own_ref), channel_id=1, source_target_pairs={{0,8},{1,3},{2,10},{3,1},{4,12},{5,7},{6,14},{7,5},{8,0},{9,17},{1... | collective-permute-start | bytes 417800 | tf_op jit(solution)/shard_map/ppermute | solution.py:449
  4.8 5.1 %collective-permute-start.1 = (bf16[17,32,128]{2,1,0:T(8,128)(2,1)S(1)}, bf16[17,32,128]{2,1,0:T(8,128)(2,1)S(1)}, u32[]{:S(2)}, u32[]{:S(2)}) collective-permute-start(bf16[17,32,128]{2,1,0:T(8,128)(2,1)S(1)} %get-tuple-element.22.own_ref), channel_id=1, source_target_pairs={{0,2},{1,9},{2,0},{3,11},{4,6},{5,13},{6,4},{7,15},{8,16},{9,1},{1... | collective-permute-start | bytes 417800 | tf_op jit(solution)/shard_map/ppermute | solution.py:449
  9.9 4.8 %collective-permute-start.2 = (bf16[33,8,128]{2,1,0:T(8,128)(2,1)S(1)}, bf16[33,8,128]{2,1,0:T(8,128)(2,1)S(1)}, u32[]{:S(2)}, u32[]{:S(2)}) collective-permute-start(bf16[33,8,128]{2,1,0:T(8,128)(2,1)S(1)} %get-tuple-element.32), channel_id=1, source_target_pairs={{0,1},{1,0},{2,3},{3,2},{4,5},{5,4},{6,7},{7,6},{8,9},{9,8},{10,11... | collective-permute-start | bytes 202760 | tf_op jit(solution)/shard_map/ppermute | solution.py:449
  10.0 4.7 %collective-permute-start.3 = (bf16[33,8,128]{2,1,0:T(8,128)(2,1)S(1)}, bf16[33,8,128]{2,1,0:T(8,128)(2,1)S(1)}, u32[]{:S(2)}, u32[]{:S(2)}) collective-permute-start(bf16[33,8,128]{2,1,0:T(8,128)(2,1)S(1)} %get-tuple-element.33), channel_id=1, source_target_pairs={{0,8},{1,2},{2,1},{3,4},{4,3},{5,6},{6,5},{7,15},{8,0},{9,10},{10,... | collective-permute-start | bytes 202760 | tf_op jit(solution)/shard_map/ppermute | solution.py:449
  17.3 6.6 %collective-permute-start.4 = (s16[2,2,4,16,128]{4,3,2,1,0:T(8,128)(2,1)S(1)}, s16[2,2,4,16,128]{4,3,2,1,0:T(8,128)(2,1)S(1)}, u32[]{:S(2)}, u32[]{:S(2)}) collective-permute-start(s16[2,2,4,16,128]{4,3,2,1,0:T(8,128)(2,1)S(1)} %get-tuple-element.36), channel_id=1, source_target_pairs={{0,16},{8,24},{16,0},{24,8},{1,17},{9,25},{17,1},{25,9},{2,18},{10... | collective-permute-start | bytes 196616 | tf_op jit(solution)/shard_map/ppermute | solution.py:482
  23.9 4.3 %collective-permute-start.5 = (s16[2,2,4,16,128]{4,3,2,1,0:T(8,128)(2,1)S(1)}, s16[2,2,4,16,128]{4,3,2,1,0:T(8,128)(2,1)S(1)}, u32[]{:S(2)}, u32[]{:S(2)}) collective-permute-start(s16[2,2,4,16,128]{4,3,2,1,0:T(8,128)(2,1)S(1)} %shard_map.72), channel_id=1, source_target_pairs={{0,4},{1,5},{2,6},{3,7},{4,0},{5,1},{6,2},{7,3},{8,12},{9,13},{10,... | collective-permute-start | bytes 196616 | tf_op jit(solution)/shard_map/ppermute | solution.py:482

commit v8 on v6

--- a/solution.py
+++ b/solution.py
@@ -126,60 +126,81 @@
     return jnp.where(right, pltpu.roll(v, d, 0), pltpu.roll(v, DEEP - d, 0))
 
 
-def along_depth(v, w, lane_open):
-    f = (w + pltpu.roll(w, LANES - 1, 1)) * (pltpu.roll(v, LANES - 1, 1) - v)
-    f = jnp.where(lane_open, f, 0.0)
-    return f - pltpu.roll(f, 1, 1)
-
-
-def flux_sum(val, wgt, lo, hi):
-    n = len(val[lo])
-    span = range(n)
+def flux_sums(parts):
     lane_open = lax.broadcasted_iota(jnp.int32, (SUB, LANES), 1) < LANES - 1
-    depth = {c: [along_depth(val[c][j], wgt[c][j], lane_open) for j in span] for c in range(lo, hi)}
-
-    def toward(c):
-        return [(wgt[c][j] + wgt[c + 1][j]) * (val[c + 1][j] - val[c][j]) for j in span]
-
-    out = {}
-    last = toward(lo - 1)
-    for c in range(lo, hi):
-        v, w = val[c], wgt[c]
-        ahead = toward(c)
-        down = [(w[j] + w[j + 1]) * (v[j + 1] - v[j]) for j in range(n - 1)]
-        down.append(
-            (w[n - 1] + pltpu.roll(w[0], SUB - 1, 0)) * (pltpu.roll(v[0], SUB - 1, 0) - v[n - 1])
+    depths = []
+    for val, wgt, lo, hi in parts:
+        depths.append(
+            {
+                (c, j): (pltpu.roll(v, LANES - 1, 1), pltpu.roll(w, LANES - 1, 1))
+                for c in range(lo, hi)
+                for j, (v, w) in enumerate(zip(val[c], wgt[c]))
+            }
         )
-        up = [pltpu.roll(down[-1], 1, 0)] + down[:-1]
-        out[c] = [(ahead[j] - last[j]) + (down[j] - up[j]) + depth[c][j] for j in span]
-        last = ahead
-    return out
-
-
-def conduct(h, q, mask, lo, hi):
-    temp, cond = {}, {}
-    for c in range(lo - 1, hi + 1):
-        t = [jnp.tanh(v) for v in h[c]]
-        temp[c] = [v - 0.4 * u for v, u in zip(h[c], t)]
-        cond[c] = [(1.0 - v) * (1.0 - v) * (u + 7.0 / 3.0) for v, u in zip(q[c], t)]
-    acc = flux_sum(temp, cond, lo, hi)
-    return {
-        c: [v + m * a for v, m, a in zip(h[c], mask(c, 0), acc[c])] for c in range(lo, hi)
-    }
-
-
-def consolidate(h, q, mask, lo, hi):
-    rate = {
-        c: [1.0 + jnp.tanh(2.5 * v - jnp.tanh(v)) for v in h[c]] for c in range(lo - 1, hi + 1)
-    }
-    acc = flux_sum(q, rate, lo, hi)
-    return {
-        c: [
-            v + m * (a - 4.0 * r * v)
-            for v, m, a, r in zip(q[c], mask(c, 1), acc[c], rate[c])
-        ]
-        for c in range(lo, hi)
-    }
+    for (val, wgt, _, _), depth in zip(parts, depths):
+        for (c, j), (v, w) in depth.items():
+            depth[c, j] = jnp.where(lane_open, (wgt[c][j] + w) * (v - val[c][j]), 0.0)
+    for depth in depths:
+        for at, f in depth.items():
+            depth[at] = f - pltpu.roll(f, 1, 1)
+
+    sums = []
+    for (val, wgt, lo, hi), depth in zip(parts, depths):
+        n = len(val[lo])
+        span = range(n)
+
+        def toward(c):
+            return [(wgt[c][j] + wgt[c + 1][j]) * (val[c + 1][j] - val[c][j]) for j in span]
+
+        out = {}
+        last = toward(lo - 1)
+        for c in range(lo, hi):
+            v, w = val[c], wgt[c]
+            ahead = toward(c)
+            down = [(w[j] + w[j + 1]) * (v[j + 1] - v[j]) for j in range(n - 1)]
+            down.append(
+                (w[n - 1] + pltpu.roll(w[0], SUB - 1, 0))
+                * (pltpu.roll(v[0], SUB - 1, 0) - v[n - 1])
+            )
+            up = [pltpu.roll(down[-1], 1, 0)] + down[:-1]
+            out[c] = [(ahead[j] - last[j]) + (down[j] - up[j]) + depth[c, j] for j in span]
+            last = ahead
+        sums.append(out)
+    return sums
+
+
+def conduct(parts, mask):
+    fluxes = []
+    for h, q, lo, hi in parts:
+        temp, cond = {}, {}
+        for c in range(lo - 1, hi + 1):
+            t = [jnp.tanh(v) for v in h[c]]
+            temp[c] = [2.5 * v - u for v, u in zip(h[c], t)]
+            cond[c] = [(1.0 - v) * (1.0 - v) * (u + 7.0 / 3.0) for v, u in zip(q[c], t)]
+        fluxes.append((temp, cond, lo, hi))
+    new = {}
+    for (h, q, lo, hi), acc in zip(parts, flux_sums(fluxes)):
+        for c in range(lo, hi):
+            new[c] = [v + m * a for v, m, a in zip(h[c], mask(c, 0), acc[c])]
+    return new
+
+
+def consolidate(parts, mask):
+    fluxes = []
+    for h, q, lo, hi in parts:
+        rate = {
+            c: [1.0 + jnp.tanh(2.5 * v - jnp.tanh(v)) for v in h[c]]
+            for c in range(lo - 1, hi + 1)
+        }
+        fluxes.append((q, rate, lo, hi))
+    new = {}
+    for (q, rate, lo, hi), acc in zip(fluxes, flux_sums(fluxes)):
+        for c in range(lo, hi):
+            new[c] = [
+                v + m * (a - 4.0 * r * v)
+                for v, m, a, r in zip(q[c], mask(c, 1), acc[c], rate[c])
+            ]
+    return new
 
 
 def tile_rows(marks, i, tx, n, out):
@@ -195,12 +216,21 @@
 
 
 def scalings(flags):
-    return ([0.0225 * f for f in flags], [0.0375 * f for f in flags])
+    return ([0.009 * f for f in flags], [0.0375 * f for f in flags])
+
+
+def back(columns, wide, turn, rows, total, heat):
+    for c, column in enumerate(columns):
+        n = len(column)
+        for j, v in enumerate(column):
+            wide[pl.ds(c * total + j, SUB, stride=n), :] = 0.5 * v + 1.0 if heat else v
+    for c in range(len(columns)):
+        turn[pl.ds(c * rows, rows), :] = wide[pl.ds(c * total + DEEP, rows), :]
 
 
 def inner(
     own_ref, heat_ref, pore_ref, xa_ref, xb_ref,
-    heat_edge, pore_edge, heat_save, pore_save, heat_mid, pore_mid, flag_out, wide,
+    heat_edge, pore_edge, heat_save, pore_save, heat_mid, pore_mid, flag_out, wide, turn,
 ):
     rows, cols = heat_ref.shape[0], heat_ref.shape[1]
     total = rows + 2 * DEEP
@@ -234,11 +264,14 @@
                     v = home[r]
                 else:
                     v = part[field * rows + r].astype(f32) * has
-                at = pl.multiple_of((i * rows + r) * cols, SUB)
-                wide[field, pl.ds(at, cols), :] = 2.0 * v - 2.0 if field == 0 else v
+                v = 2.0 * v - 2.0 if field == 0 else v
+                for g in range(0, cols, SUB):
+                    at = pl.multiple_of(g * total + (i * rows + r) * SUB, SUB)
+                    wide[field, pl.ds(at, SUB), :] = v[g : g + SUB]
         for c in range(cols):
+            at = c // SUB * SUB * total + c % SUB
             state[DEEP + c] = [
-                wide[field, pl.ds(j * cols + c, SUB, stride=n * cols), :] for j in range(n)
+                wide[field, pl.ds(at + j * SUB, SUB, stride=n * SUB), :] for j in range(n)
             ]
 
     for p in range(PAIRS):
@@ -246,31 +279,30 @@
         for side, c in ((0, lo), (1, hi - 1)):
             for j in range(n):
                 heat_save[p, side, j] = h[c][j]
-        h.update(conduct(h, q, mask, lo, hi))
+        h.update(conduct([(h, q, lo, hi)], mask))
         lo, hi = lo + 1, hi - 1
         for side, c in ((0, lo), (1, hi - 1)):
             for j in range(n):
                 pore_save[p, side, j] = q[c][j]
-        q.update(consolidate(h, q, mask, lo, hi))
+        q.update(consolidate([(h, q, lo, hi)], mask))
 
     for field, state, edge, mid in ((0, h, heat_edge, heat_mid), (1, q, pore_edge, pore_mid)):
         for c in range(DEEP + 1):
             for j in range(n):
                 edge[0, c, j] = state[DEEP + c][j]
                 edge[1, c, j] = state[width - DEEP - 1 - c][j]
-        for c in range(DEEP, cols - DEEP):
-            for j in range(n):
-                v = state[DEEP + c][j]
-                wide[field, pl.ds(j * cols + c, SUB, stride=n * cols), :] = (
-                    0.5 * v + 1.0 if field == 0 else v
-                )
+        back(
+            [state[c] for c in range(2 * DEEP, width - 2 * DEEP)], wide.at[field], turn.at[field],
+            rows, total, field == 0,
+        )
         for r in range(rows):
-            mid[r] = wide[field, pl.ds((DEEP + r) * cols + DEEP, cols - 2 * DEEP), :]
+            for g in range(0, cols - 2 * DEEP, SUB):
+                mid[r, g : g + SUB] = turn[field, pl.ds(g * rows + r, SUB, stride=rows), :]
 
 
 def edges(
     mask_ref, heat_edge, pore_edge, heat_save, pore_save, heat_mid, pore_mid, flag_ref, yn_ref, yf_ref,
-    heat_out, pore_out, send_ref, later_ref, wide, block,
+    heat_out, pore_out, send_ref, later_ref, wide, turn, block,
 ):
     rows, cols = heat_mid.shape[0], heat_mid.shape[1] + 2 * DEEP
     total = rows + 2 * DEEP
@@ -314,12 +346,12 @@
         for at, part, has, right_end in parts:
             for x in range(total):
                 v = scaled(edge_row(part, field, x, rows, right_end), has, row_open[x // rows])
-                into = pl.multiple_of(x * pair + at * DEEP, SUB)
+                into = pl.multiple_of(at * DEEP * total + x * DEEP, SUB)
                 wide[field, pl.ds(into, DEEP), :] = 2.0 * v - 2.0 if field == 0 else v
         for c in range(DEEP):
             for first, halo in ((0, c), (DEEP, width - DEEP + c)):
                 state[halo] = [
-                    wide[field, pl.ds(j * pair + first + c, SUB, stride=n * pair), :]
+                    wide[field, pl.ds(first * total + j * DEEP + c, SUB, stride=n * DEEP), :]
                     for j in range(n)
                 ]
         for c in range(DEEP + 1):
@@ -329,33 +361,29 @@
     for p in range(PAIRS):
         lo = 2 * p + 1
         hi = width - lo
-        new = {}
+        parts = []
         for side, a, b, c in ((0, lo, lo + DEEP, lo + DEEP), (1, hi - DEEP, hi, hi - DEEP - 1)):
             then = dict(h)
             then[c] = [heat_save[p, side, j] for j in range(n)]
-            new.update(conduct(then, q, mask, a, b))
-        h.update(new)
+            parts.append((then, q, a, b))
+        h.update(conduct(parts, mask))
         lo, hi = lo + 1, hi - 1
-        new = {}
+        parts = []
         for side, a, b, c in ((0, lo, lo + DEEP, lo + DEEP), (1, hi - DEEP, hi, hi - DEEP - 1)):
             then = dict(q)
             then[c] = [pore_save[p, side, j] for j in range(n)]
-            new.update(consolidate(h, then, mask, a, b))
-        q.update(new)
+            parts.append((h, then, a, b))
+        q.update(consolidate(parts, mask))
 
     for field, state, mid, out in ((0, h, heat_mid, heat_out), (1, q, pore_mid, pore_out)):
-        for c in range(DEEP):
-            for first, own in ((0, DEEP + c), (DEEP, width - pair + c)):
-                for j in range(n):
-                    v = state[own][j]
-                    wide[field, pl.ds(j * pair + first + c, SUB, stride=n * pair), :] = (
-                        0.5 * v + 1.0 if field == 0 else v
-                    )
+        ends = [*range(DEEP, pair), *range(width - pair, width - DEEP)]
+        back([state[c] for c in ends], wide.at[field], turn.at[field], rows, total, field == 0)
         for r in range(rows):
-            row = (DEEP + r) * pair
-            block[field, r, 0:DEEP] = wide[field, pl.ds(row, DEEP), :]
+            block[field, r, 0:DEEP] = turn[field, pl.ds(r, DEEP, stride=rows), :]
             block[field, r, DEEP : cols - DEEP] = mid[r]
-            block[field, r, cols - DEEP :] = wide[field, pl.ds(row + DEEP, DEEP), :]
+            block[field, r, cols - DEEP :] = turn[
+                field, pl.ds(DEEP * rows + r, DEEP, stride=rows), :
+            ]
         for i in range(2):
             for k in range(2):
                 out[2 * i + k] = block[field, i * tx : (i + 1) * tx, k * ty : (k + 1) * ty, :]
@@ -507,12 +535,16 @@
     flag = ((2, n, SUB, depth), f32)
     state = call(
         inner, "VVVVV", [edge, edge, save, save, mid, mid, flag],
-        [pltpu.VMEM((2, total * cols, depth), f32)],
+        [
+            pltpu.VMEM((2, total * cols, depth), f32),
+            pltpu.VMEM((2, rows * (cols - 2 * DEEP), depth), f32),
+        ],
     )(own, enthalpy, porosity, x_near, x_far)
     heat, pore, first, later = call(
         edges, "V" * 10, [tiles, tiles, parcel, parcel],
         [
             pltpu.VMEM((2, total * 2 * DEEP, depth), f32),
+            pltpu.VMEM((2, rows * 2 * DEEP, depth), f32),
             pltpu.VMEM((2, rows, cols, depth), f32),
         ],
     )(masks, *state, y_near, y_far)

time: 75.4 us -> 28.3 us (0.38)
  Pallas kernels: 54 us -> 6.56 us
  waiting for transfers between devices: 10.1 us -> 11.3 us
  starting transfers between devices: 10.5 us -> 9.65 us
    pallas_call x6, Pallas kernels: 54 us -> 6.56 us  [run(): pl.pallas_call(body, in_specs=[pl.BlockSpec(memory_space=space[c]) for c...]
    ppermute x2, starting transfers between devices: 4.4 us -> 3.54 us  [swap(): return lax.ppermute(value, axis, [(i, (i + n // 2) % n) for i in range(n)])]
    ppermute x2, waiting for transfers between devices: 6.56 us -> 7.43 us  [swap(): return lax.ppermute(value, axis, [(i, (i + n // 2) % n) for i in range(n)])]
  transfers between devices with their start and end apart: 6 -> 6, of which waited for: 4 -> 5; matrix products, arithmetic and copies ran while one was open for 0% -> 0% of each run, Pallas kernels for 48% -> 9%
where the time goes in v8:
time: 28.3 us; the launch traced here: 28.1 us
  waiting for transfers between devices  11.3 us (40%)
  starting transfers between devices  9.65 us (34%)
  Pallas kernels  6.56 us (23%)
  between operations  0.68 us (2%)
    ppermute x2, waiting for transfers between devices, swap(): return lax.ppermute(value, axis, [(i, (i + n // 2) % n) for i in range(n)])  7.43 us
    pallas_call x6, Pallas kernels, run(): pl.pallas_call(body, in_specs=[pl.BlockSpec(memory_space=space[c]) for c...  6.56 us
    ppermute x4, starting transfers between devices, permute(): return lax.ppermute(value, ('gx', 'gy'), pairs)  6.11 us
    ppermute x4, waiting for transfers between devices, permute(): return lax.ppermute(value, ('gx', 'gy'), pairs)  3.83 us
    ppermute x2, starting transfers between devices, swap(): return lax.ppermute(value, axis, [(i, (i + n // 2) % n) for i in range(n)])  3.54 us
  transfers between devices with their start and end apart: 6, of which 5 were waited for; matrix products, arithmetic and copies ran while one was open for 0% of the time, Pallas kernels for 9%

profile of v8, /device:TPU:0, one launch (start us, length us, event | category | flops | bytes accessed | tf_op | source)
XLA Modules:
  0.0 28.1 jit_solution(4685361649333886816)
XLA Ops:
  0.6 1.0 %shard_map.68 = (bf16[17,32,128]{2,1,0:T(8,128)(2,1)S(1)}, f32[8,32,128]{2,1,0:T(8,128)S(1)}, f32[8,32,128]{2,1,0:T(8,128)S(1)}, f32[36,8,128]{2,1,0:T(8,128)S(1)}) custom-call(s32[2,2]{1,0:T(2,128)} %active_ref.1, s32[2]{0:T(128)} %bitcast.5, s32[2,2]{1,0:T(2,128)} %bitcast.4, f32[8,32,128]{2,1,0:T(8,128)} %heat_ref.1, f32[8,32,128]{2,1,0:T(8,128)} %pore_ref.1), custom_call_target="tpu_custom_call" | custom-call | tf_op jit(solution)/shard_map/pallas_call | solution.py:456
  1.7 3.1 %collective-permute-start = (bf16[17,32,128]{2,1,0:T(8,128)(2,1)S(1)}, bf16[17,32,128]{2,1,0:T(8,128)(2,1)S(1)}, u32[]{:S(2)}, u32[]{:S(2)}) collective-permute-start(bf16[17,32,128]{2,1,0:T(8,128)(2,1)S(1)} %get-tuple-element.22.own_ref), channel_id=1, source_target_pairs={{0,8},{1,3},{2,10},{3,1},{4,12},{5,7},{6,14},{7,5},{8,0},{9,17},{1... | collective-permute-start | bytes 417800 | tf_op jit(solution)/shard_map/ppermute | solution.py:475
  4.8 1.5 %collective-permute-start.1 = (bf16[17,32,128]{2,1,0:T(8,128)(2,1)S(1)}, bf16[17,32,128]{2,1,0:T(8,128)(2,1)S(1)}, u32[]{:S(2)}, u32[]{:S(2)}) collective-permute-start(bf16[17,32,128]{2,1,0:T(8,128)(2,1)S(1)} %get-tuple-element.22.own_ref), channel_id=1, source_target_pairs={{0,2},{1,9},{2,0},{3,11},{4,6},{5,13},{6,4},{7,15},{8,16},{9,1},{1... | collective-permute-start | bytes 417800 | tf_op jit(solution)/shard_map/ppermute | solution.py:475
  6.3 2.5 %collective-permute-done.xa_ref.first_ref = bf16[17,32,128]{2,1,0:T(8,128)(2,1)S(1)} collective-permute-done((bf16[17,32,128]{2,1,0:T(8,128)(2,1)S(1)}, bf16[17,32,128]{2,1,0:T(8,128)(2,1)S(1)}, u32[]{:S(2)}, u32[]{:S(2)}) %collective-permute-start) | collective-permute-done | bytes 139296 | tf_op jit(solution)/shard_map/ppermute | solution.py:475
  8.8 1.0 %collective-permute-done.1.xb_ref.second_ref = bf16[17,32,128]{2,1,0:T(8,128)(2,1)S(1)} collective-permute-done((bf16[17,32,128]{2,1,0:T(8,128)(2,1)S(1)}, bf16[17,32,128]{2,1,0:T(8,128)(2,1)S(1)}, u32[]{:S(2)}, u32[]{:S(2)}) %collective-permute-start.1) | collective-permute-done | bytes 139296 | tf_op jit(solution)/shard_map/ppermute | solution.py:475
  9.8 0.1 shard_map.70
  9.9 0.1 collective-permute-start.2
  10.0 1.4 %collective-permute-start.3 = (bf16[33,8,128]{2,1,0:T(8,128)(2,1)S(1)}, bf16[33,8,128]{2,1,0:T(8,128)(2,1)S(1)}, u32[]{:S(2)}, u32[]{:S(2)}) collective-permute-start(bf16[33,8,128]{2,1,0:T(8,128)(2,1)S(1)} %get-tuple-element.33), channel_id=1, source_target_pairs={{0,8},{1,2},{2,1},{3,4},{4,3},{5,6},{6,5},{7,15},{8,0},{9,10},{10,... | collective-permute-start | bytes 202760 | tf_op jit(solution)/shard_map/ppermute | solution.py:475
  11.4 2.7 %shard_map.69 = (f32[2,9,3,8,128]{4,3,2,1,0:T(8,128)S(1)}, f32[2,9,3,8,128]{4,3,2,1,0:T(8,128)S(1)}, f32[4,2,3,8,128]{4,3,2,1,0:T(8,128)S(1)}, f32[4,2,3,8,128]{...) custom-call(bf16[17,32,128]{2,1,0:T(8,128)(2,1)S(1)} %get-tuple-element.2, ...), custom_call_target="tpu_custom_call" | custom-call | tf_op jit(solution)/shard_map/pallas_call | solution.py:456
  14.1 0.0 collective-permute-done.2.yn_ref
  14.1 0.3 collective-permute-done.3.yf_ref
  14.3 2.0 %shard_map.71 = (f32[4,4,16,128]{3,2,1,0:T(8,128)S(1)}, f32[4,4,16,128]{3,2,1,0:T(8,128)S(1)}, s16[2,2,4,16,128]{4,3,2,1,0:T(8,128)(2,1)S(1)}, s16[2,2,4,16,128]{4,3,2,1,0:T(8,128)(2,1)S(1)}) custom-call(f32[36,8,128]{2,1,0:T(8,128)S(1)} %get-tuple-element.21.mask_ref, f32[2,9,3,8,128]{4,3,2,1,0:T(8,128)S(1)} %get-tuple-element.25.heat_edge, ...), custom_call_target="tpu_custom_call" | custom-call | tf_op jit(solution)/shard_map/pallas_call | solution.py:456
  16.4 2.7 %collective-permute-start.4 = (s16[2,2,4,16,128]{4,3,2,1,0:T(8,128)(2,1)S(1)}, s16[2,2,4,16,128]{4,3,2,1,0:T(8,128)(2,1)S(1)}, u32[]{:S(2)}, u32[]{:S(2)}) collective-permute-start(s16[2,2,4,16,128]{4,3,2,1,0:T(8,128)(2,1)S(1)} %get-tuple-element.36), channel_id=1, source_target_pairs={{0,16},{8,24},{16,0},{24,8},{1,17},{9,25},{17,1},{25,9},{2,18},{10... | collective-permute-start | bytes 196616 | tf_op jit(solution)/shard_map/ppermute | solution.py:508
  19.1 4.0 %collective-permute-done.4.got_ref.first_ref = s16[2,2,4,16,128]{4,3,2,1,0:T(8,128)(2,1)S(1)} collective-permute-done((s16[2,2,4,16,128]{4,3,2,1,0:T(8,128)(2,1)S(1)}, s16[2,2,4,16,128]{4,3,2,1,0:T(8,128)(2,1)S(1)}, u32[]{:S(2)}, u32[]{:S(2)}) %collective-permute-start.4) | collective-permute-done | bytes 65568 | tf_op jit(solution)/shard_map/ppermute | solution.py:508
  23.1 0.9 %collective-permute-start.5 = (s16[2,2,4,16,128]{4,3,2,1,0:T(8,128)(2,1)S(1)}, s16[2,2,4,16,128]{4,3,2,1,0:T(8,128)(2,1)S(1)}, u32[]{:S(2)}, u32[]{:S(2)}) collective-permute-start(s16[2,2,4,16,128]{4,3,2,1,0:T(8,128)(2,1)S(1)} %shard_map.72), channel_id=1, source_target_pairs={{0,4},{1,5},{2,6},{3,7},{4,0},{5,1},{6,2},{7,3},{8,12},{9,13},{10,... | collective-permute-start | bytes 196616 | tf_op jit(solution)/shard_map/ppermute | solution.py:508
  23.9 3.4 %collective-permute-done.5.second_ref = s16[2,2,4,16,128]{4,3,2,1,0:T(8,128)(2,1)S(1)} collective-permute-done((s16[2,2,4,16,128]{4,3,2,1,0:T(8,128)(2,1)S(1)}, s16[2,2,4,16,128]{4,3,2,1,0:T(8,128)(2,1)S(1)}, u32[]{:S(2)}, u32[]{:S(2)}) %collective-permute-start.5) | collective-permute-done | bytes 65568 | tf_op jit(solution)/shard_map/ppermute | solution.py:508
  27.4 0.7 %shard_map.73 = (f32[4,4,16,128]{3,2,1,0:T(8,128)}, f32[4,4,16,128]{3,2,1,0:T(8,128)}) custom-call(f32[36,8,128]{2,1,0:T(8,128)S(1)} %get-tuple-element.21.mask_ref, f32[4,4,16,128]{3,2,1,0:T(8,128)S(1)} %get-tuple-element.34.heat_ref, f32[4,4,16,128]{3,2,1,0:T(8,128)S(1)} %get-tuple-element.35.pore_ref, ...), custom_call_target="tpu_custom_call" | custom-call | tf_op jit(solution)/shard_map/pallas_call | solution.py:456
  (1 shorter events, 0.0 us)
Async XLA Ops:
  1.7 7.1 %collective-permute-start = (bf16[17,32,128]{2,1,0:T(8,128)(2,1)S(1)}, bf16[17,32,128]{2,1,0:T(8,128)(2,1)S(1)}, u32[]{:S(2)}, u32[]{:S(2)}) collective-permute-start(bf16[17,32,128]{2,1,0:T(8,128)(2,1)S(1)} %get-tuple-element.22.own_ref), channel_id=1, source_target_pairs={{0,8},{1,3},{2,10},{3,1},{4,12},{5,7},{6,14},{7,5},{8,0},{9,17},{1... | collective-permute-start | bytes 417800 | tf_op jit(solution)/shard_map/ppermute | solution.py:475
  4.8 5.1 %collective-permute-start.1 = (bf16[17,32,128]{2,1,0:T(8,128)(2,1)S(1)}, bf16[17,32,128]{2,1,0:T(8,128)(2,1)S(1)}, u32[]{:S(2)}, u32[]{:S(2)}) collective-permute-start(bf16[17,32,128]{2,1,0:T(8,128)(2,1)S(1)} %get-tuple-element.22.own_ref), channel_id=1, source_target_pairs={{0,2},{1,9},{2,0},{3,11},{4,6},{5,13},{6,4},{7,15},{8,16},{9,1},{1... | collective-permute-start | bytes 417800 | tf_op jit(solution)/shard_map/ppermute | solution.py:475
  9.9 4.2 %collective-permute-start.2 = (bf16[33,8,128]{2,1,0:T(8,128)(2,1)S(1)}, bf16[33,8,128]{2,1,0:T(8,128)(2,1)S(1)}, u32[]{:S(2)}, u32[]{:S(2)}) collective-permute-start(bf16[33,8,128]{2,1,0:T(8,128)(2,1)S(1)} %get-tuple-element.32), channel_id=1, source_target_pairs={{0,1},{1,0},{2,3},{3,2},{4,5},{5,4},{6,7},{7,6},{8,9},{9,8},{10,11... | collective-permute-start | bytes 202760 | tf_op jit(solution)/shard_map/ppermute | solution.py:475
  10.0 4.4 %collective-permute-start.3 = (bf16[33,8,128]{2,1,0:T(8,128)(2,1)S(1)}, bf16[33,8,128]{2,1,0:T(8,128)(2,1)S(1)}, u32[]{:S(2)}, u32[]{:S(2)}) collective-permute-start(bf16[33,8,128]{2,1,0:T(8,128)(2,1)S(1)} %get-tuple-element.33), channel_id=1, source_target_pairs={{0,8},{1,2},{2,1},{3,4},{4,3},{5,6},{6,5},{7,15},{8,0},{9,10},{10,... | collective-permute-start | bytes 202760 | tf_op jit(solution)/shard_map/ppermute | solution.py:475
  16.4 6.6 %collective-permute-start.4 = (s16[2,2,4,16,128]{4,3,2,1,0:T(8,128)(2,1)S(1)}, s16[2,2,4,16,128]{4,3,2,1,0:T(8,128)(2,1)S(1)}, u32[]{:S(2)}, u32[]{:S(2)}) collective-permute-start(s16[2,2,4,16,128]{4,3,2,1,0:T(8,128)(2,1)S(1)} %get-tuple-element.36), channel_id=1, source_target_pairs={{0,16},{8,24},{16,0},{24,8},{1,17},{9,25},{17,1},{25,9},{2,18},{10... | collective-permute-start | bytes 196616 | tf_op jit(solution)/shard_map/ppermute | solution.py:508
  23.1 4.3 %collective-permute-start.5 = (s16[2,2,4,16,128]{4,3,2,1,0:T(8,128)(2,1)S(1)}, s16[2,2,4,16,128]{4,3,2,1,0:T(8,128)(2,1)S(1)}, u32[]{:S(2)}, u32[]{:S(2)}) collective-permute-start(s16[2,2,4,16,128]{4,3,2,1,0:T(8,128)(2,1)S(1)} %shard_map.72), channel_id=1, source_target_pairs={{0,4},{1,5},{2,6},{3,7},{4,0},{5,1},{6,2},{7,3},{8,12},{9,13},{10,... | collective-permute-start | bytes 196616 | tf_op jit(solution)/shard_map/ppermute | solution.py:508

commit v9 on v8

--- a/solution.py
+++ b/solution.py
@@ -8,6 +8,7 @@
 
 PAIRS = 4
 DEEP = 2 * PAIRS
+PARTS = 4
 SUB = 8
 LANES = 128
 VMEM_LIMIT = 16 * 2**20
@@ -44,15 +45,29 @@
 
 
 def pack_x(
-    active_ref, count_ref, slot_ref, heat_ref, pore_ref, out_ref, heat_out, pore_out, mask_ref
+    active_in, count_in, slot_in, heat_in, pore_in, out_ref, heat_ref, pore_ref, mask_ref,
+    active_ref, count_ref, slot_ref, sems,
 ):
     rows, cols = heat_ref.shape[0], heat_ref.shape[1]
     ranks = slot_ref.shape[1]
+    part = rows // PARTS
+    copies = []
+
+    def fetch(src, dst):
+        copies.append(pltpu.make_async_copy(src, dst, sems.at[len(copies)]))
+        copies[-1].start()
+
+    for src, dst in ((heat_in, heat_ref), (pore_in, pore_ref)):
+        for i in range(PARTS):
+            at = pl.ds(i * part, part)
+            fetch(src.at[at], dst.at[at])
+    for src, dst in ((active_in, active_ref), (count_in, count_ref), (slot_in, slot_ref)):
+        fetch(src, dst)
+    for copy in copies:
+        copy.wait()
     out_ref[0:rows] = heat_ref[...].astype(jnp.bfloat16)
     out_ref[rows : 2 * rows] = pore_ref[...].astype(jnp.bfloat16)
     out_ref[2 * rows] = flag_rows(active_ref, cols).astype(jnp.bfloat16)
-    heat_out[...] = heat_ref[...]
-    pore_out[...] = pore_ref[...]
     choose, taken, again, _ = mask_at(ranks)
 
     def put(row, holds):
@@ -422,10 +437,11 @@
             send_ref[k, f] = v.astype(jnp.int16)
 
 
-def place(mask_ref, heat_ref, pore_ref, first_ref, second_ref, heat_out, pore_out):
+def place(mask_ref, heat_ref, pore_ref, first_ref, second_ref, heat_out, pore_out, tiles, sems):
     ranks = first_ref.shape[0]
     shape = first_ref.shape[2:]
     taken = mask_at(ranks)[1]
+    copies = []
     for field, src, out, scale, shift in (
         (0, heat_ref, heat_out, HEAT_SCALE, HEAT_SHIFT),
         (1, pore_ref, pore_out, PORE_SCALE, PORE_SHIFT),
@@ -439,24 +455,30 @@
             v = src[s]
             for i, r, tile in came:
                 v = jnp.where(held(mask_ref, taken(i, r, s), shape), tile, v)
-            out[s] = v
+            tiles[field, s] = v
+            copies.append(
+                pltpu.make_async_copy(tiles.at[field, s], out.at[s], sems.at[2 * s + field])
+            )
+            copies[-1].start()
+    for copy in copies:
+        copy.wait()
 
 
 def call(body, spec, outs, scratch=(), out_space=pltpu.VMEM):
     def run(*args):
-        space = {"s": pltpu.SMEM, "v": pltpu.VMEM, "V": pltpu.VMEM}
+        space = {"h": pltpu.HBM, "V": pltpu.VMEM}
         args = [
             pltpu.with_memory_space_constraint(a, pltpu.VMEM if c == "V" else pltpu.HBM)
             for c, a in zip(spec, args)
         ]
         shapes = [
-            pltpu.VMEM(s, d) if out_space is not None else jax.ShapeDtypeStruct(s, d)
+            pltpu.VMEM(s, d) if out_space is pltpu.VMEM else jax.ShapeDtypeStruct(s, d)
             for s, d in outs
         ]
         return pl.pallas_call(
             body,
             in_specs=[pl.BlockSpec(memory_space=space[c]) for c in spec],
-            out_specs=[pl.BlockSpec(memory_space=pltpu.VMEM) for _ in outs],
+            out_specs=[pl.BlockSpec(memory_space=out_space) for _ in outs],
             out_shape=shapes,
             scratch_shapes=list(scratch),
             compiler_params=pltpu.CompilerParams(vmem_limit_bytes=VMEM_LIMIT),
@@ -519,7 +541,13 @@
     block = ((rows, cols, depth), f32)
     masks = ((mask_at(ranks)[3], SUB, LANES), f32)
     own, enthalpy, porosity, masks = call(
-        pack_x, "sssvv", [((2 * rows + 1, cols, depth), bf16), block, block, masks]
+        pack_x, "hhhhh", [((2 * rows + 1, cols, depth), bf16), block, block, masks],
+        [
+            pltpu.SMEM(active.shape, active.dtype),
+            pltpu.SMEM(count.shape, count.dtype),
+            pltpu.SMEM(slots.shape, slots.dtype),
+            pltpu.SemaphoreType.DMA((2 * PARTS + 3,)),
+        ],
     )(active, count, slots, enthalpy, porosity)
     x_near, x_far = exchange_x(own)
     side = ((4 * rows + 1, DEEP, depth), bf16)
@@ -551,7 +579,11 @@
     first = swap(first, "gx")
     (second,) = call(resend, "VVV", [parcel])(masks, first, later)
     second = swap(second, "gy")
-    heat, pore = call(place, "VVVVV", [tiles, tiles], out_space=None)(
+    heat, pore = call(
+        place, "VVVVV", [tiles, tiles],
+        [pltpu.VMEM((2, 4, tx, ty, depth), f32), pltpu.SemaphoreType.DMA((8,))],
+        out_space=pltpu.HBM,
+    )(
         masks, heat, pore, first, second
     )
     return heat[None, None], pore[None, None]

time: 28.3 us -> 28.4 us (level)
  no operation moved by 1% of the time
where the time goes in v9:
time: 28.4 us; the launch traced here: 28.2 us
  waiting for transfers between devices  11.3 us (40%)
  starting transfers between devices  9.65 us (34%)
  Pallas kernels  6.62 us (23%)
  between operations  0.68 us (2%)
    ppermute x2, waiting for transfers between devices, swap(): return lax.ppermute(value, axis, [(i, (i + n // 2) % n) for i in range(n)])  7.43 us
    pallas_call x6, Pallas kernels, run(): pl.pallas_call(body, in_specs=[pl.BlockSpec(memory_space=space[c]) for c...  6.62 us
    ppermute x4, starting transfers between devices, permute(): return lax.ppermute(value, ('gx', 'gy'), pairs)  6.11 us
    ppermute x4, waiting for transfers between devices, permute(): return lax.ppermute(value, ('gx', 'gy'), pairs)  3.83 us
    ppermute x2, starting transfers between devices, swap(): return lax.ppermute(value, axis, [(i, (i + n // 2) % n) for i in range(n)])  3.54 us
  transfers between devices with their start and end apart: 6, of which 5 were waited for; matrix products, arithmetic and copies ran while one was open for 0% of the time, Pallas kernels for 9%

profile of v9, /device:TPU:0, one launch (start us, length us, event | category | flops | bytes accessed | tf_op | source)
XLA Modules:
  0.0 28.2 jit_solution(17823411320568759115)
XLA Ops:
  0.6 1.0 %shard_map.68 = (bf16[17,32,128]{2,1,0:T(8,128)(2,1)S(1)}, f32[8,32,128]{2,1,0:T(8,128)S(1)}, f32[8,32,128]{2,1,0:T(8,128)S(1)}, f32[36,8,128]{2,1,0:T(8,128)S(1)}) custom-call(s32[2,2]{1,0:T(2,128)} %active_in.1, s32[2]{0:T(128)} %bitcast.5, s32[2,2]{1,0:T(2,128)} %bitcast.4, f32[8,32,128]{2,1,0:T(8,128)} %heat_in.1, f32[8,32,128]{2,1,0:T(8,128)} %pore_in.1), custom_call_target="tpu_custom_call" | custom-call | tf_op jit(solution)/shard_map/pallas_call | solution.py:478
  1.7 3.1 %collective-permute-start = (bf16[17,32,128]{2,1,0:T(8,128)(2,1)S(1)}, bf16[17,32,128]{2,1,0:T(8,128)(2,1)S(1)}, u32[]{:S(2)}, u32[]{:S(2)}) collective-permute-start(bf16[17,32,128]{2,1,0:T(8,128)(2,1)S(1)} %get-tuple-element.22.own_ref), channel_id=1, source_target_pairs={{0,8},{1,3},{2,10},{3,1},{4,12},{5,7},{6,14},{7,5},{8,0},{9,17},{1... | collective-permute-start | bytes 417800 | tf_op jit(solution)/shard_map/ppermute | solution.py:497
  4.8 1.5 %collective-permute-start.1 = (bf16[17,32,128]{2,1,0:T(8,128)(2,1)S(1)}, bf16[17,32,128]{2,1,0:T(8,128)(2,1)S(1)}, u32[]{:S(2)}, u32[]{:S(2)}) collective-permute-start(bf16[17,32,128]{2,1,0:T(8,128)(2,1)S(1)} %get-tuple-element.22.own_ref), channel_id=1, source_target_pairs={{0,2},{1,9},{2,0},{3,11},{4,6},{5,13},{6,4},{7,15},{8,16},{9,1},{1... | collective-permute-start | bytes 417800 | tf_op jit(solution)/shard_map/ppermute | solution.py:497
  6.3 2.5 %collective-permute-done.xa_ref.first_ref = bf16[17,32,128]{2,1,0:T(8,128)(2,1)S(1)} collective-permute-done((bf16[17,32,128]{2,1,0:T(8,128)(2,1)S(1)}, bf16[17,32,128]{2,1,0:T(8,128)(2,1)S(1)}, u32[]{:S(2)}, u32[]{:S(2)}) %collective-permute-start) | collective-permute-done | bytes 139296 | tf_op jit(solution)/shard_map/ppermute | solution.py:497
  8.8 1.0 %collective-permute-done.1.xb_ref.second_ref = bf16[17,32,128]{2,1,0:T(8,128)(2,1)S(1)} collective-permute-done((bf16[17,32,128]{2,1,0:T(8,128)(2,1)S(1)}, bf16[17,32,128]{2,1,0:T(8,128)(2,1)S(1)}, u32[]{:S(2)}, u32[]{:S(2)}) %collective-permute-start.1) | collective-permute-done | bytes 139296 | tf_op jit(solution)/shard_map/ppermute | solution.py:497
  9.8 0.1 shard_map.70
  9.9 0.1 collective-permute-start.2
  10.0 1.4 %collective-permute-start.3 = (bf16[33,8,128]{2,1,0:T(8,128)(2,1)S(1)}, bf16[33,8,128]{2,1,0:T(8,128)(2,1)S(1)}, u32[]{:S(2)}, u32[]{:S(2)}) collective-permute-start(bf16[33,8,128]{2,1,0:T(8,128)(2,1)S(1)} %get-tuple-element.33), channel_id=1, source_target_pairs={{0,8},{1,2},{2,1},{3,4},{4,3},{5,6},{6,5},{7,15},{8,0},{9,10},{10,... | collective-permute-start | bytes 202760 | tf_op jit(solution)/shard_map/ppermute | solution.py:497
  11.4 2.7 %shard_map.69 = (f32[2,9,3,8,128]{4,3,2,1,0:T(8,128)S(1)}, f32[2,9,3,8,128]{4,3,2,1,0:T(8,128)S(1)}, f32[4,2,3,8,128]{4,3,2,1,0:T(8,128)S(1)}, f32[4,2,3,8,128]{...) custom-call(bf16[17,32,128]{2,1,0:T(8,128)(2,1)S(1)} %get-tuple-element.2, ...), custom_call_target="tpu_custom_call" | custom-call | tf_op jit(solution)/shard_map/pallas_call | solution.py:478
  14.1 0.0 collective-permute-done.2.yn_ref
  14.1 0.3 collective-permute-done.3.yf_ref
  14.4 2.0 %shard_map.71 = (f32[4,4,16,128]{3,2,1,0:T(8,128)S(1)}, f32[4,4,16,128]{3,2,1,0:T(8,128)S(1)}, s16[2,2,4,16,128]{4,3,2,1,0:T(8,128)(2,1)S(1)}, s16[2,2,4,16,128]{4,3,2,1,0:T(8,128)(2,1)S(1)}) custom-call(f32[36,8,128]{2,1,0:T(8,128)S(1)} %get-tuple-element.21.mask_ref, f32[2,9,3,8,128]{4,3,2,1,0:T(8,128)S(1)} %get-tuple-element.25.heat_edge, ...), custom_call_target="tpu_custom_call" | custom-call | tf_op jit(solution)/shard_map/pallas_call | solution.py:478
  16.4 2.7 %collective-permute-start.4 = (s16[2,2,4,16,128]{4,3,2,1,0:T(8,128)(2,1)S(1)}, s16[2,2,4,16,128]{4,3,2,1,0:T(8,128)(2,1)S(1)}, u32[]{:S(2)}, u32[]{:S(2)}) collective-permute-start(s16[2,2,4,16,128]{4,3,2,1,0:T(8,128)(2,1)S(1)} %get-tuple-element.36), channel_id=1, source_target_pairs={{0,16},{8,24},{16,0},{24,8},{1,17},{9,25},{17,1},{25,9},{2,18},{10... | collective-permute-start | bytes 196616 | tf_op jit(solution)/shard_map/ppermute | solution.py:530
  19.1 4.0 %collective-permute-done.4.got_ref.first_ref = s16[2,2,4,16,128]{4,3,2,1,0:T(8,128)(2,1)S(1)} collective-permute-done((s16[2,2,4,16,128]{4,3,2,1,0:T(8,128)(2,1)S(1)}, s16[2,2,4,16,128]{4,3,2,1,0:T(8,128)(2,1)S(1)}, u32[]{:S(2)}, u32[]{:S(2)}) %collective-permute-start.4) | collective-permute-done | bytes 65568 | tf_op jit(solution)/shard_map/ppermute | solution.py:530
  23.1 0.9 %collective-permute-start.5 = (s16[2,2,4,16,128]{4,3,2,1,0:T(8,128)(2,1)S(1)}, s16[2,2,4,16,128]{4,3,2,1,0:T(8,128)(2,1)S(1)}, u32[]{:S(2)}, u32[]{:S(2)}) collective-permute-start(s16[2,2,4,16,128]{4,3,2,1,0:T(8,128)(2,1)S(1)} %shard_map.72), channel_id=1, source_target_pairs={{0,4},{1,5},{2,6},{3,7},{4,0},{5,1},{6,2},{7,3},{8,12},{9,13},{10,... | collective-permute-start | bytes 196616 | tf_op jit(solution)/shard_map/ppermute | solution.py:530
  24.0 3.4 %collective-permute-done.5.second_ref = s16[2,2,4,16,128]{4,3,2,1,0:T(8,128)(2,1)S(1)} collective-permute-done((s16[2,2,4,16,128]{4,3,2,1,0:T(8,128)(2,1)S(1)}, s16[2,2,4,16,128]{4,3,2,1,0:T(8,128)(2,1)S(1)}, u32[]{:S(2)}, u32[]{:S(2)}) %collective-permute-start.5) | collective-permute-done | bytes 65568 | tf_op jit(solution)/shard_map/ppermute | solution.py:530
  27.4 0.8 %shard_map.73 = (f32[4,4,16,128]{3,2,1,0:T(8,128)}, f32[4,4,16,128]{3,2,1,0:T(8,128)}) custom-call(f32[36,8,128]{2,1,0:T(8,128)S(1)} %get-tuple-element.21.mask_ref, f32[4,4,16,128]{3,2,1,0:T(8,128)S(1)} %get-tuple-element.34.heat_ref, f32[4,4,16,128]{3,2,1,0:T(8,128)S(1)} %get-tuple-element.35.pore_ref, ...), custom_call_target="tpu_custom_call" | custom-call | tf_op jit(solution)/shard_map/pallas_call | solution.py:478
  (1 shorter events, 0.0 us)
Async XLA Ops:
  1.7 7.1 %collective-permute-start = (bf16[17,32,128]{2,1,0:T(8,128)(2,1)S(1)}, bf16[17,32,128]{2,1,0:T(8,128)(2,1)S(1)}, u32[]{:S(2)}, u32[]{:S(2)}) collective-permute-start(bf16[17,32,128]{2,1,0:T(8,128)(2,1)S(1)} %get-tuple-element.22.own_ref), channel_id=1, source_target_pairs={{0,8},{1,3},{2,10},{3,1},{4,12},{5,7},{6,14},{7,5},{8,0},{9,17},{1... | collective-permute-start | bytes 417800 | tf_op jit(solution)/shard_map/ppermute | solution.py:497
  4.8 5.1 %collective-permute-start.1 = (bf16[17,32,128]{2,1,0:T(8,128)(2,1)S(1)}, bf16[17,32,128]{2,1,0:T(8,128)(2,1)S(1)}, u32[]{:S(2)}, u32[]{:S(2)}) collective-permute-start(bf16[17,32,128]{2,1,0:T(8,128)(2,1)S(1)} %get-tuple-element.22.own_ref), channel_id=1, source_target_pairs={{0,2},{1,9},{2,0},{3,11},{4,6},{5,13},{6,4},{7,15},{8,16},{9,1},{1... | collective-permute-start | bytes 417800 | tf_op jit(solution)/shard_map/ppermute | solution.py:497
  9.9 4.2 %collective-permute-start.2 = (bf16[33,8,128]{2,1,0:T(8,128)(2,1)S(1)}, bf16[33,8,128]{2,1,0:T(8,128)(2,1)S(1)}, u32[]{:S(2)}, u32[]{:S(2)}) collective-permute-start(bf16[33,8,128]{2,1,0:T(8,128)(2,1)S(1)} %get-tuple-element.32), channel_id=1, source_target_pairs={{0,1},{1,0},{2,3},{3,2},{4,5},{5,4},{6,7},{7,6},{8,9},{9,8},{10,11... | collective-permute-start | bytes 202760 | tf_op jit(solution)/shard_map/ppermute | solution.py:497
  10.0 4.4 %collective-permute-start.3 = (bf16[33,8,128]{2,1,0:T(8,128)(2,1)S(1)}, bf16[33,8,128]{2,1,0:T(8,128)(2,1)S(1)}, u32[]{:S(2)}, u32[]{:S(2)}) collective-permute-start(bf16[33,8,128]{2,1,0:T(8,128)(2,1)S(1)} %get-tuple-element.33), channel_id=1, source_target_pairs={{0,8},{1,2},{2,1},{3,4},{4,3},{5,6},{6,5},{7,15},{8,0},{9,10},{10,... | collective-permute-start | bytes 202760 | tf_op jit(solution)/shard_map/ppermute | solution.py:497
  16.4 6.6 %collective-permute-start.4 = (s16[2,2,4,16,128]{4,3,2,1,0:T(8,128)(2,1)S(1)}, s16[2,2,4,16,128]{4,3,2,1,0:T(8,128)(2,1)S(1)}, u32[]{:S(2)}, u32[]{:S(2)}) collective-permute-start(s16[2,2,4,16,128]{4,3,2,1,0:T(8,128)(2,1)S(1)} %get-tuple-element.36), channel_id=1, source_target_pairs={{0,16},{8,24},{16,0},{24,8},{1,17},{9,25},{17,1},{25,9},{2,18},{10... | collective-permute-start | bytes 196616 | tf_op jit(solution)/shard_map/ppermute | solution.py:530
  23.1 4.3 %collective-permute-start.5 = (s16[2,2,4,16,128]{4,3,2,1,0:T(8,128)(2,1)S(1)}, s16[2,2,4,16,128]{4,3,2,1,0:T(8,128)(2,1)S(1)}, u32[]{:S(2)}, u32[]{:S(2)}) collective-permute-start(s16[2,2,4,16,128]{4,3,2,1,0:T(8,128)(2,1)S(1)} %shard_map.72), channel_id=1, source_target_pairs={{0,4},{1,5},{2,6},{3,7},{4,0},{5,1},{6,2},{7,3},{8,12},{9,13},{10,... | collective-permute-start | bytes 196616 | tf_op jit(solution)/shard_map/ppermute | solution.py:530

commit v10 on v8

--- a/solution.py
+++ b/solution.py
@@ -8,6 +8,7 @@
 
 PAIRS = 4
 DEEP = 2 * PAIRS
+EARLY = PAIRS // 2
 SUB = 8
 LANES = 128
 VMEM_LIMIT = 16 * 2**20
@@ -126,23 +127,30 @@
     return jnp.where(right, pltpu.roll(v, d, 0), pltpu.roll(v, DEEP - d, 0))
 
 
-def flux_sums(parts):
-    lane_open = lax.broadcasted_iota(jnp.int32, (SUB, LANES), 1) < LANES - 1
+def flux_sums(parts, twice):
+    lane = lax.broadcasted_iota(jnp.int32, (SUB, LANES), 1)
     depths = []
     for val, wgt, lo, hi in parts:
         depths.append(
             {
-                (c, j): (pltpu.roll(v, LANES - 1, 1), pltpu.roll(w, LANES - 1, 1))
+                (c, j): [
+                    (pltpu.roll(v, by, 1), pltpu.roll(w, by, 1))
+                    for by in ((LANES - 1,) if twice else (LANES - 1, 1))
+                ]
                 for c in range(lo, hi)
                 for j, (v, w) in enumerate(zip(val[c], wgt[c]))
             }
         )
     for (val, wgt, _, _), depth in zip(parts, depths):
-        for (c, j), (v, w) in depth.items():
-            depth[c, j] = jnp.where(lane_open, (wgt[c][j] + w) * (v - val[c][j]), 0.0)
+        for (c, j), shifted in depth.items():
+            f = None
+            for (v, w), ok in zip(shifted, (lane < LANES - 1, lane > 0)):
+                g = jnp.where(ok, (wgt[c][j] + w) * (v - val[c][j]), 0.0)
+                f = g if f is None else f + g
+            depth[c, j] = f
     for depth in depths:
         for at, f in depth.items():
-            depth[at] = f - pltpu.roll(f, 1, 1)
+            depth[at] = f - pltpu.roll(f, 1, 1) if twice else f
 
     sums = []
     for (val, wgt, lo, hi), depth in zip(parts, depths):
@@ -169,38 +177,33 @@
     return sums
 
 
-def conduct(parts, mask):
+def advance(*parts, twice=True):
     fluxes = []
-    for h, q, lo, hi in parts:
-        temp, cond = {}, {}
+    for pore, h, q, lo, hi, _ in parts:
+        val, wgt = {}, {}
         for c in range(lo - 1, hi + 1):
             t = [jnp.tanh(v) for v in h[c]]
-            temp[c] = [2.5 * v - u for v, u in zip(h[c], t)]
-            cond[c] = [(1.0 - v) * (1.0 - v) * (u + 7.0 / 3.0) for v, u in zip(q[c], t)]
-        fluxes.append((temp, cond, lo, hi))
-    new = {}
-    for (h, q, lo, hi), acc in zip(parts, flux_sums(fluxes)):
+            temp = [2.5 * v - u for v, u in zip(h[c], t)]
+            if pore:
+                val[c] = q[c]
+                wgt[c] = [1.0 + jnp.tanh(v) for v in temp]
+            else:
+                val[c] = temp
+                wgt[c] = [(1.0 - v) * (1.0 - v) * (u + 7.0 / 3.0) for v, u in zip(q[c], t)]
+        fluxes.append((val, wgt, lo, hi))
+    results = []
+    for (pore, h, q, lo, hi, mask), (val, wgt, _, _), acc in zip(parts, fluxes, flux_sums(fluxes, twice)):
+        new = {}
         for c in range(lo, hi):
-            new[c] = [v + m * a for v, m, a in zip(h[c], mask(c, 0), acc[c])]
-    return new
-
-
-def consolidate(parts, mask):
-    fluxes = []
-    for h, q, lo, hi in parts:
-        rate = {
-            c: [1.0 + jnp.tanh(2.5 * v - jnp.tanh(v)) for v in h[c]]
-            for c in range(lo - 1, hi + 1)
-        }
-        fluxes.append((q, rate, lo, hi))
-    new = {}
-    for (q, rate, lo, hi), acc in zip(fluxes, flux_sums(fluxes)):
-        for c in range(lo, hi):
-            new[c] = [
-                v + m * (a - 4.0 * r * v)
-                for v, m, a, r in zip(q[c], mask(c, 1), acc[c], rate[c])
-            ]
-    return new
+            if pore:
+                new[c] = [
+                    v + m * (a - 4.0 * r * v)
+                    for v, m, a, r in zip(q[c], mask(c, 1), acc[c], wgt[c])
+                ]
+            else:
+                new[c] = [v + m * a for v, m, a in zip(h[c], mask(c, 0), acc[c])]
+        results.append(new)
+    return results
 
 
 def tile_rows(marks, i, tx, n, out):
@@ -230,7 +233,7 @@
 
 def inner(
     own_ref, heat_ref, pore_ref, xa_ref, xb_ref,
-    heat_edge, pore_edge, heat_save, pore_save, heat_mid, pore_mid, flag_out, wide, turn,
+    heat_out, pore_out, heat_save, pore_save, flag_out, wide,
 ):
     rows, cols = heat_ref.shape[0], heat_ref.shape[1]
     total = rows + 2 * DEEP
@@ -274,116 +277,203 @@
                 wide[field, pl.ds(at + j * SUB, SUB, stride=n * SUB), :] for j in range(n)
             ]
 
-    for p in range(PAIRS):
+    for p in range(EARLY):
         lo, hi = DEEP + 2 * p + 1, width - DEEP - 2 * p - 1
         for side, c in ((0, lo), (1, hi - 1)):
             for j in range(n):
                 heat_save[p, side, j] = h[c][j]
-        h.update(conduct([(h, q, lo, hi)], mask))
+        h.update(*advance((False, h, q, lo, hi, mask)))
         lo, hi = lo + 1, hi - 1
         for side, c in ((0, lo), (1, hi - 1)):
             for j in range(n):
                 pore_save[p, side, j] = q[c][j]
-        q.update(consolidate([(h, q, lo, hi)], mask))
-
-    for field, state, edge, mid in ((0, h, heat_edge, heat_mid), (1, q, pore_edge, pore_mid)):
-        for c in range(DEEP + 1):
+        q.update(*advance((True, h, q, lo, hi, mask)))
+    for state, out in ((h, heat_out), (q, pore_out)):
+        for c in range(cols):
             for j in range(n):
-                edge[0, c, j] = state[DEEP + c][j]
-                edge[1, c, j] = state[width - DEEP - 1 - c][j]
-        back(
-            [state[c] for c in range(2 * DEEP, width - 2 * DEEP)], wide.at[field], turn.at[field],
-            rows, total, field == 0,
-        )
-        for r in range(rows):
-            for g in range(0, cols - 2 * DEEP, SUB):
-                mid[r, g : g + SUB] = turn[field, pl.ds(g * rows + r, SUB, stride=rows), :]
-
-
-def edges(
-    mask_ref, heat_edge, pore_edge, heat_save, pore_save, heat_mid, pore_mid, flag_ref, yn_ref, yf_ref,
-    heat_out, pore_out, send_ref, later_ref, wide, turn, block,
-):
-    rows, cols = heat_mid.shape[0], heat_mid.shape[1] + 2 * DEEP
-    total = rows + 2 * DEEP
-    width = cols + 2 * DEEP
-    n = total // SUB
-    tx, ty = rows // 2, cols // 2
+                out[c, j] = state[DEEP + c][j]
+
+
+def halo(near, flag_ref, got_ref, wide, rows, n):
+    total = n * SUB
+    tx = rows // 2
     f32 = jnp.float32
     odd = lax.rem(lax.axis_index("gy"), 2)
+    side = 1 - odd if near else odd
+    left = side == 0
+    has = None if near else jnp.where(left, inside("gy", False), inside("gy", True))
     row_open = (inside("gx", False), None, inside("gx", True))
-    far_open = jnp.where(odd == 1, inside("gy", True), inside("gy", False))
-    parts = ((1 - odd, yn_ref, None, odd == 1), (odd, yf_ref, far_open, odd == 0))
 
     def scaled(v, *by):
         for s in by:
             v = v if s is None else v * s
         return v
 
-    halves = []
-    for at, part, has, _ in parts:
-        marks = scaled(part[4 * rows].astype(f32), has)
-        f = [jnp.zeros((SUB, LANES), f32) for _ in range(n)]
-        for i in range(3):
-            f = tile_rows(
-                jnp.broadcast_to(scaled(marks[i : i + 1], row_open[i]), (SUB, LANES)), i, tx, n, f
-            )
-        halves.append(f)
-    near, far = halves
-    left = [jnp.where(odd == 1, a, b) for a, b in zip(near, far)]
-    right = [jnp.where(odd == 1, b, a) for a, b in zip(near, far)]
-    flags = [
-        scalings(f)
-        for f in (left, *([flag_ref[k, j] for j in range(n)] for k in range(2)), right)
-    ]
+    marks = scaled(got_ref[4 * rows].astype(f32), has)
+    beyond = [jnp.zeros((SUB, LANES), f32) for _ in range(n)]
+    for i in range(3):
+        row = jnp.broadcast_to(scaled(marks[i : i + 1], row_open[i]), (SUB, LANES))
+        beyond = tile_rows(row, i, tx, n, beyond)
+    flags = [scalings(beyond), scalings([flag_ref[side, j] for j in range(n)])]
 
     def mask(c, kind):
-        return flags[0 if c < DEEP else 1 if c < DEEP + ty else 2 if c < DEEP + cols else 3][kind]
-
-    pair = 2 * DEEP
-    h, q = {}, {}
-    for field, edge, state in ((0, heat_edge, h), (1, pore_edge, q)):
-        for at, part, has, right_end in parts:
-            for x in range(total):
-                v = scaled(edge_row(part, field, x, rows, right_end), has, row_open[x // rows])
-                into = pl.multiple_of(at * DEEP * total + x * DEEP, SUB)
-                wide[field, pl.ds(into, DEEP), :] = 2.0 * v - 2.0 if field == 0 else v
+        return flags[0 if c < DEEP else 1][kind]
+
+    states = ({}, {})
+    for field, state in enumerate(states):
+        for x in range(total):
+            v = scaled(edge_row(got_ref, field, x, rows, left), has, row_open[x // rows])
+            wide[field, x * DEEP : (x + 1) * DEEP, :] = 2.0 * v - 2.0 if field == 0 else v
         for c in range(DEEP):
-            for first, halo in ((0, c), (DEEP, width - DEEP + c)):
-                state[halo] = [
-                    wide[field, pl.ds(first * total + j * DEEP + c, SUB, stride=n * DEEP), :]
-                    for j in range(n)
-                ]
+            state[c] = [
+                jnp.where(
+                    left,
+                    wide[field, pl.ds(j * DEEP + c, SUB, stride=n * DEEP), :],
+                    wide[field, pl.ds(j * DEEP + DEEP - 1 - c, SUB, stride=n * DEEP), :],
+                )
+                for j in range(n)
+            ]
+    return side, left, states, mask
+
+
+def strips(h, q, left, wide, turn, rows, n):
+    total = n * SUB
+    for field, state in ((0, h), (1, q)):
+        for c in range(DEEP):
+            for j, v in enumerate(state[DEEP + c]):
+                wide[field, pl.ds(c * total + j, SUB, stride=n), :] = (
+                    0.5 * v + 1.0 if field == 0 else v
+                )
+        for c in range(DEEP):
+            at = pl.multiple_of(jnp.where(left, c, DEEP - 1 - c) * rows, SUB)
+            turn[field, pl.ds(at, rows), :] = wide[field, pl.ds(c * total + DEEP, rows), :]
+
+
+def middle(
+    heat_in, pore_in, heat_save, pore_save, flag_ref, got_ref,
+    heat_strip, pore_strip, heat_mid, pore_mid, heat_edge, pore_edge, heat_kept, pore_kept,
+    wide, turn, wide_mid, turn_mid,
+):
+    rows, cols = heat_mid.shape[0], heat_in.shape[0]
+    n = heat_in.shape[1]
+    width = cols + 2 * DEEP
+    total = n * SUB
+    ty = cols // 2
+    span = range(n)
+    side, left, (hw, qw), mask_w = halo(True, flag_ref, got_ref, wide, rows, n)
+    flags = [scalings([flag_ref[k, j] for j in span]) for k in range(2)]
+
+    def mask(c, kind):
+        return flags[0 if c < DEEP + ty else 1][kind]
+
+    h = {DEEP + c: [heat_in[c, j] for j in span] for c in range(cols)}
+    q = {DEEP + c: [pore_in[c, j] for j in span] for c in range(cols)}
+
+    def pick(low, high):
+        return [jnp.where(left, a, b) for a, b in zip(low, high)]
+
+    def at(state, c):
+        return pick(state[c], state[width - 1 - c])
+
+    kept = ({}, {})
+    for p in range(EARLY):
+        for keep, save, out in zip(kept, (heat_save, pore_save), (heat_kept, pore_kept)):
+            keep[p] = [save[p, side, j] for j in span]
+            for j in span:
+                out[p, j] = save[p, 1 - side, j]
+
+    def keep_now(field, state, p, c):
+        low, high = state[c], state[width - 1 - c]
+        kept[field][p] = pick(low, high)
+        for j, v in enumerate(pick(high, low)):
+            (heat_kept, pore_kept)[field][p, j] = v
+
+    waiting = []
+
+    def block_half(step):
+        p, k = EARLY + step // 4, step % 4
+        pore = k >= 2
+        lo = DEEP + 2 * p + (2 if pore else 1)
+        if k % 2 == 0:
+            keep_now(int(pore), q if pore else h, p, lo)
+        half = (lo, width // 2) if k % 2 == 0 else (width // 2, width - lo)
+        return (pore, h, q, *half, mask)
+
+    for p in range(PAIRS):
+        for pore in (False, True):
+            step = 2 * p + pore
+            lo = 2 * p + 1 + pore
+            end = block_half(step)
+            if pore:
+                hw[lo + DEEP - 1], hw[lo + DEEP] = at(h, lo + DEEP - 1), at(h, lo + DEEP)
+                then = dict(qw)
+                then[lo + DEEP] = kept[1][p]
+                part = (True, hw, then, lo, lo + DEEP, mask_w)
+            else:
+                c = lo + DEEP - 1
+                hw[c] = at(h, c)
+                qw[c], qw[c + 1] = at(q, c), at(q, c + 1)
+                then = dict(hw)
+                then[c + 1] = kept[0][p]
+                part = (False, then, qw, lo, lo + DEEP, mask_w)
+            new, ours = advance(part, end)
+            (qw if pore else hw).update(new)
+            waiting.append(ours)
+            if step % 2 == 1:
+                for result in waiting:
+                    (q if end[0] else h).update(result)
+                waiting = []
+
+    strips(hw, qw, left, wide, turn, rows, n)
+    for field, out in ((0, heat_strip), (1, pore_strip)):
+        for r in range(rows):
+            out[r] = turn[field, pl.ds(r, DEEP, stride=rows), :]
+    for field, state, edge, mid in ((0, h, heat_edge, heat_mid), (1, q, pore_edge, pore_mid)):
         for c in range(DEEP + 1):
-            state[DEEP + c] = [edge[0, c, j] for j in range(n)]
-            state[width - DEEP - 1 - c] = [edge[1, c, j] for j in range(n)]
-
+            for j, v in enumerate(pick(state[width - 1 - DEEP - c], state[DEEP + c])):
+                edge[c, j] = v
+        back(
+            [state[c] for c in range(2 * DEEP, width - 2 * DEEP)], wide_mid.at[field],
+            turn_mid.at[field], rows, total, field == 0,
+        )
+        for r in range(rows):
+            for g in range(0, cols - 2 * DEEP, SUB):
+                mid[r, g : g + SUB] = turn_mid[field, pl.ds(g * rows + r, SUB, stride=rows), :]
+
+
+def far_edge(
+    mask_ref, heat_edge, pore_edge, heat_kept, pore_kept, heat_mid, pore_mid, flag_ref, got_ref,
+    heat_near, pore_near, heat_out, pore_out, send_ref, later_ref, wide, turn, block,
+):
+    rows, cols = heat_mid.shape[0], heat_mid.shape[1] + 2 * DEEP
+    n = heat_edge.shape[1]
+    tx, ty = rows // 2, cols // 2
+    span = range(n)
+    side, left, (h, q), mask = halo(False, flag_ref, got_ref, wide, rows, n)
+    for state, edge in ((h, heat_edge), (q, pore_edge)):
+        for c in range(DEEP + 1):
+            state[DEEP + c] = [edge[c, j] for j in span]
     for p in range(PAIRS):
         lo = 2 * p + 1
-        hi = width - lo
-        parts = []
-        for side, a, b, c in ((0, lo, lo + DEEP, lo + DEEP), (1, hi - DEEP, hi, hi - DEEP - 1)):
-            then = dict(h)
-            then[c] = [heat_save[p, side, j] for j in range(n)]
-            parts.append((then, q, a, b))
-        h.update(conduct(parts, mask))
-        lo, hi = lo + 1, hi - 1
-        parts = []
-        for side, a, b, c in ((0, lo, lo + DEEP, lo + DEEP), (1, hi - DEEP, hi, hi - DEEP - 1)):
-            then = dict(q)
-            then[c] = [pore_save[p, side, j] for j in range(n)]
-            parts.append((h, then, a, b))
-        q.update(consolidate(parts, mask))
-
-    for field, state, mid, out in ((0, h, heat_mid, heat_out), (1, q, pore_mid, pore_out)):
-        ends = [*range(DEEP, pair), *range(width - pair, width - DEEP)]
-        back([state[c] for c in ends], wide.at[field], turn.at[field], rows, total, field == 0)
+        then = dict(h)
+        then[lo + DEEP] = [heat_kept[p, j] for j in span]
+        h.update(*advance((False, then, q, lo, lo + DEEP, mask), twice=False))
+        lo = lo + 1
+        then = dict(q)
+        then[lo + DEEP] = [pore_kept[p, j] for j in span]
+        q.update(*advance((True, h, then, lo, lo + DEEP, mask), twice=False))
+    strips(h, q, left, wide, turn, rows, n)
+    end = cols - DEEP
+    far_at = pl.ds(pl.multiple_of(end * side, SUB), DEEP)
+    near_at = pl.ds(pl.multiple_of(end - end * side, SUB), DEEP)
+    for field, mid, near, out in (
+        (0, heat_mid, heat_near, heat_out),
+        (1, pore_mid, pore_near, pore_out),
+    ):
         for r in range(rows):
-            block[field, r, 0:DEEP] = turn[field, pl.ds(r, DEEP, stride=rows), :]
-            block[field, r, DEEP : cols - DEEP] = mid[r]
-            block[field, r, cols - DEEP :] = turn[
-                field, pl.ds(DEEP * rows + r, DEEP, stride=rows), :
-            ]
+            block[field, r, DEEP:end] = mid[r]
+            block[field, r, near_at] = near[r]
+            block[field, r, far_at] = turn[field, pl.ds(r, DEEP, stride=rows), :]
         for i in range(2):
             for k in range(2):
                 out[2 * i + k] = block[field, i * tx : (i + 1) * tx, k * ty : (k + 1) * ty, :]
@@ -529,25 +619,33 @@
     n = total // SUB
     tiles = ((4, tx, ty, depth), f32)
     parcel = ((ranks, 2, tx, ty, depth), i16)
-    edge = ((2, DEEP + 1, n, SUB, depth), f32)
-    save = ((PAIRS, 2, n, SUB, depth), f32)
+    column = (n, SUB, depth)
+    whole = ((cols, *column), f32)
+    save = ((EARLY, 2, *column), f32)
+    edge = ((DEEP + 1, *column), f32)
+    kept = ((PAIRS, *column), f32)
     mid = ((rows, cols - 2 * DEEP, depth), f32)
-    flag = ((2, n, SUB, depth), f32)
+    strip = ((rows, DEEP, depth), f32)
     state = call(
-        inner, "VVVVV", [edge, edge, save, save, mid, mid, flag],
-        [
-            pltpu.VMEM((2, total * cols, depth), f32),
+        inner, "VVVVV", [whole, whole, save, save, ((2, *column), f32)],
+        [pltpu.VMEM((2, total * cols, depth), f32)],
+    )(own, enthalpy, porosity, x_near, x_far)
+    scratch = [
+        pltpu.VMEM((2, total * DEEP, depth), f32),
+        pltpu.VMEM((2, rows * DEEP, depth), f32),
+    ]
+    heat_near, pore_near, heat_mid, pore_mid, *ends = call(
+        middle, "V" * 6, [strip, strip, mid, mid, edge, edge, kept, kept],
+        scratch
+        + [
+            pltpu.VMEM((2, total * (cols - 2 * DEEP), depth), f32),
             pltpu.VMEM((2, rows * (cols - 2 * DEEP), depth), f32),
         ],
-    )(own, enthalpy, porosity, x_near, x_far)
+    )(*state, y_near)
     heat, pore, first, later = call(
-        edges, "V" * 10, [tiles, tiles, parcel, parcel],
-        [
-            pltpu.VMEM((2, total * 2 * DEEP, depth), f32),
-            pltpu.VMEM((2, rows * 2 * DEEP, depth), f32),
-            pltpu.VMEM((2, rows, cols, depth), f32),
-        ],
-    )(masks, *state, y_near, y_far)
+        far_edge, "V" * 11, [tiles, tiles, parcel, parcel],
+        scratch + [pltpu.VMEM((2, rows, cols, depth), f32)],
+    )(masks, *ends, heat_mid, pore_mid, state[4], y_far, heat_near, pore_near)
     first = swap(first, "gx")
     (second,) = call(resend, "VVV", [parcel])(masks, first, later)
     second = swap(second, "gy")

time: 28.3 us -> 28.1 us (level)
  waiting for transfers between devices: 11.3 us -> 10.1 us
  starting transfers between devices: 9.65 us -> 10.5 us
    ppermute x2, waiting for transfers between devices: 7.43 us -> 6.56 us  [swap(): return lax.ppermute(value, axis, [(i, (i + n // 2) % n) for i in range(n)])]
    ppermute x2, starting transfers between devices: 3.54 us -> 4.4 us  [swap(): return lax.ppermute(value, axis, [(i, (i + n // 2) % n) for i in range(n)])]
    pallas_call x6 -> x7, Pallas kernels: 6.56 us -> 6.62 us  [run(): pl.pallas_call(body, in_specs=[pl.BlockSpec(memory_space=space[c]) for c...]
  transfers between devices with their start and end apart: 6 -> 6, of which waited for: 5 -> 4; matrix products, arithmetic and copies ran while one was open for 0% -> 0% of each run, Pallas kernels for 9% -> 13%
where the time goes in v10:
time: 28.1 us; the launch traced here: 28 us
  starting transfers between devices  10.5 us (37%)
  waiting for transfers between devices  10.1 us (36%)
  Pallas kernels  6.62 us (24%)
  between operations  0.69 us (2%)
    pallas_call x7, Pallas kernels, run(): pl.pallas_call(body, in_specs=[pl.BlockSpec(memory_space=space[c]) for c...  6.62 us
    ppermute x2, waiting for transfers between devices, swap(): return lax.ppermute(value, axis, [(i, (i + n // 2) % n) for i in range(n)])  6.56 us
    ppermute x4, starting transfers between devices, permute(): return lax.ppermute(value, ('gx', 'gy'), pairs)  6.11 us
    ppermute x2, starting transfers between devices, swap(): return lax.ppermute(value, axis, [(i, (i + n // 2) % n) for i in range(n)])  4.4 us
    ppermute x4, waiting for transfers between devices, permute(): return lax.ppermute(value, ('gx', 'gy'), pairs)  3.57 us
  transfers between devices with their start and end apart: 6, of which 4 were waited for; matrix products, arithmetic and copies ran while one was open for 0% of the time, Pallas kernels for 13%

profile of v10, /device:TPU:0, one launch (start us, length us, event | category | flops | bytes accessed | tf_op | source)
XLA Modules:
  0.0 28.0 jit_solution(15432118908937810545)
XLA Ops:
  0.6 1.0 %shard_map.68 = (bf16[17,32,128]{2,1,0:T(8,128)(2,1)S(1)}, f32[8,32,128]{2,1,0:T(8,128)S(1)}, f32[8,32,128]{2,1,0:T(8,128)S(1)}, f32[36,8,128]{2,1,0:T(8,128)S(1)}) custom-call(s32[2,2]{1,0:T(2,128)} %active_ref.1, s32[2]{0:T(128)} %bitcast.5, s32[2,2]{1,0:T(2,128)} %bitcast.4, f32[8,32,128]{2,1,0:T(8,128)} %heat_ref.1, f32[8,32,128]{2,1,0:T(8,128)} %pore_ref.1), custom_call_target="tpu_custom_call" | custom-call | tf_op jit(solution)/shard_map/pallas_call | solution.py:546
  1.7 3.1 %collective-permute-start = (bf16[17,32,128]{2,1,0:T(8,128)(2,1)S(1)}, bf16[17,32,128]{2,1,0:T(8,128)(2,1)S(1)}, u32[]{:S(2)}, u32[]{:S(2)}) collective-permute-start(bf16[17,32,128]{2,1,0:T(8,128)(2,1)S(1)} %get-tuple-element.28.own_ref), channel_id=1, source_target_pairs={{0,8},{1,3},{2,10},{3,1},{4,12},{5,7},{6,14},{7,5},{8,0},{9,17},{1... | collective-permute-start | bytes 417800 | tf_op jit(solution)/shard_map/ppermute | solution.py:565
  4.8 1.5 %collective-permute-start.1 = (bf16[17,32,128]{2,1,0:T(8,128)(2,1)S(1)}, bf16[17,32,128]{2,1,0:T(8,128)(2,1)S(1)}, u32[]{:S(2)}, u32[]{:S(2)}) collective-permute-start(bf16[17,32,128]{2,1,0:T(8,128)(2,1)S(1)} %get-tuple-element.28.own_ref), channel_id=1, source_target_pairs={{0,2},{1,9},{2,0},{3,11},{4,6},{5,13},{6,4},{7,15},{8,16},{9,1},{1... | collective-permute-start | bytes 417800 | tf_op jit(solution)/shard_map/ppermute | solution.py:565
  6.3 2.5 %collective-permute-done.xa_ref.first_ref = bf16[17,32,128]{2,1,0:T(8,128)(2,1)S(1)} collective-permute-done((bf16[17,32,128]{2,1,0:T(8,128)(2,1)S(1)}, bf16[17,32,128]{2,1,0:T(8,128)(2,1)S(1)}, u32[]{:S(2)}, u32[]{:S(2)}) %collective-permute-start) | collective-permute-done | bytes 139296 | tf_op jit(solution)/shard_map/ppermute | solution.py:565
  8.8 1.0 %collective-permute-done.1.xb_ref.second_ref = bf16[17,32,128]{2,1,0:T(8,128)(2,1)S(1)} collective-permute-done((bf16[17,32,128]{2,1,0:T(8,128)(2,1)S(1)}, bf16[17,32,128]{2,1,0:T(8,128)(2,1)S(1)}, u32[]{:S(2)}, u32[]{:S(2)}) %collective-permute-start.1) | collective-permute-done | bytes 139296 | tf_op jit(solution)/shard_map/ppermute | solution.py:565
  9.8 0.1 shard_map.70
  9.9 0.1 collective-permute-start.2
  10.0 1.4 %collective-permute-start.3 = (bf16[33,8,128]{2,1,0:T(8,128)(2,1)S(1)}, bf16[33,8,128]{2,1,0:T(8,128)(2,1)S(1)}, u32[]{:S(2)}, u32[]{:S(2)}) collective-permute-start(bf16[33,8,128]{2,1,0:T(8,128)(2,1)S(1)} %get-tuple-element.43), channel_id=1, source_target_pairs={{0,8},{1,2},{2,1},{3,4},{4,3},{5,6},{6,5},{7,15},{8,0},{9,10},{10,... | collective-permute-start | bytes 202760 | tf_op jit(solution)/shard_map/ppermute | solution.py:565
  11.4 1.6 %shard_map.69 = (f32[32,3,8,128]{3,2,1,0:T(8,128)S(1)}, f32[32,3,8,128]{3,2,1,0:T(8,128)S(1)}, f32[2,2,3,8,128]{4,3,2,1,0:T(8,128)S(1)}, f32[2,2,3,8,128]{4,3,2,1,0:T(8,128)S(1)}, f32[2,3,8,128]{3,2,1,0:T(8,128)S(1)}) custom-call(bf16[17,32,128]{2,1,0:T(8,128)(2,1)S(1)} %get-tuple-element.28.own_ref, f32[8,32,128]{2,1,0:T(8,128)S(1)} %get-tuple-element.29.heat_ref, ...), custom_call_target="tpu_custom_call" | custom-call | tf_op jit(solution)/shard_map/pallas_call | solution.py:546
  13.0 0.0 collective-permute-done.2.got_ref
  13.0 2.0 %shard_map.71 = (f32[8,8,128]{2,1,0:T(8,128)S(1)}, f32[8,8,128]{2,1,0:T(8,128)S(1)}, f32[8,16,128]{2,1,0:T(8,128)S(1)}, f32[8,16,128]{2,1,0:T(8,128)S(1)}, f32[9...) custom-call(f32[32,3,8,128]{3,2,1,0:T(8,128)S(1)} %get-tuple-element, ...), custom_call_target="tpu_custom_call" | custom-call | tf_op jit(solution)/shard_map/pallas_call | solution.py:546
  15.1 0.0 collective-permute-done.3.got_ref
  15.1 1.1 %shard_map.72 = (f32[4,4,16,128]{3,2,1,0:T(8,128)S(1)}, f32[4,4,16,128]{3,2,1,0:T(8,128)S(1)}, s16[2,2,4,16,128]{4,3,2,1,0:T(8,128)(2,1)S(1)}, s16[2,2,4,16,128]{4,3,2,1,0:T(8,128)(2,1)S(1)}) custom-call(f32[36,8,128]{2,1,0:T(8,128)S(1)} %get-tuple-element.27.mask_ref, f32[9,3,8,128]{3,2,1,0:T(8,128)S(1)} %get-tuple-element.37.heat_edge, ...), custom_call_target="tpu_custom_call" | custom-call | tf_op jit(solution)/shard_map/pallas_call | solution.py:546
  16.2 2.7 %collective-permute-start.4 = (s16[2,2,4,16,128]{4,3,2,1,0:T(8,128)(2,1)S(1)}, s16[2,2,4,16,128]{4,3,2,1,0:T(8,128)(2,1)S(1)}, u32[]{:S(2)}, u32[]{:S(2)}) collective-permute-start(s16[2,2,4,16,128]{4,3,2,1,0:T(8,128)(2,1)S(1)} %get-tuple-element.48), channel_id=1, source_target_pairs={{0,16},{8,24},{16,0},{24,8},{1,17},{9,25},{17,1},{25,9},{2,18},{10... | collective-permute-start | bytes 196616 | tf_op jit(solution)/shard_map/ppermute | solution.py:598
  19.0 3.9 %collective-permute-done.4.got_ref.first_ref = s16[2,2,4,16,128]{4,3,2,1,0:T(8,128)(2,1)S(1)} collective-permute-done((s16[2,2,4,16,128]{4,3,2,1,0:T(8,128)(2,1)S(1)}, s16[2,2,4,16,128]{4,3,2,1,0:T(8,128)(2,1)S(1)}, u32[]{:S(2)}, u32[]{:S(2)}) %collective-permute-start.4) | collective-permute-done | bytes 65568 | tf_op jit(solution)/shard_map/ppermute | solution.py:598
  22.9 1.7 %collective-permute-start.5 = (s16[2,2,4,16,128]{4,3,2,1,0:T(8,128)(2,1)S(1)}, s16[2,2,4,16,128]{4,3,2,1,0:T(8,128)(2,1)S(1)}, u32[]{:S(2)}, u32[]{:S(2)}) collective-permute-start(s16[2,2,4,16,128]{4,3,2,1,0:T(8,128)(2,1)S(1)} %shard_map.73), channel_id=1, source_target_pairs={{0,4},{1,5},{2,6},{3,7},{4,0},{5,1},{6,2},{7,3},{8,12},{9,13},{10,... | collective-permute-start | bytes 196616 | tf_op jit(solution)/shard_map/ppermute | solution.py:598
  24.5 2.7 %collective-permute-done.5.second_ref = s16[2,2,4,16,128]{4,3,2,1,0:T(8,128)(2,1)S(1)} collective-permute-done((s16[2,2,4,16,128]{4,3,2,1,0:T(8,128)(2,1)S(1)}, s16[2,2,4,16,128]{4,3,2,1,0:T(8,128)(2,1)S(1)}, u32[]{:S(2)}, u32[]{:S(2)}) %collective-permute-start.5) | collective-permute-done | bytes 65568 | tf_op jit(solution)/shard_map/ppermute | solution.py:598
  27.2 0.7 %shard_map.74 = (f32[4,4,16,128]{3,2,1,0:T(8,128)}, f32[4,4,16,128]{3,2,1,0:T(8,128)}) custom-call(f32[36,8,128]{2,1,0:T(8,128)S(1)} %get-tuple-element.27.mask_ref, f32[4,4,16,128]{3,2,1,0:T(8,128)S(1)} %get-tuple-element.46.heat_ref, f32[4,4,16,128]{3,2,1,0:T(8,128)S(1)} %get-tuple-element.47.pore_ref, ...), custom_call_target="tpu_custom_call" | custom-call | tf_op jit(solution)/shard_map/pallas_call | solution.py:546
  (1 shorter events, 0.0 us)
Async XLA Ops:
  1.7 7.1 %collective-permute-start = (bf16[17,32,128]{2,1,0:T(8,128)(2,1)S(1)}, bf16[17,32,128]{2,1,0:T(8,128)(2,1)S(1)}, u32[]{:S(2)}, u32[]{:S(2)}) collective-permute-start(bf16[17,32,128]{2,1,0:T(8,128)(2,1)S(1)} %get-tuple-element.28.own_ref), channel_id=1, source_target_pairs={{0,8},{1,3},{2,10},{3,1},{4,12},{5,7},{6,14},{7,5},{8,0},{9,17},{1... | collective-permute-start | bytes 417800 | tf_op jit(solution)/shard_map/ppermute | solution.py:565
  4.8 5.1 %collective-permute-start.1 = (bf16[17,32,128]{2,1,0:T(8,128)(2,1)S(1)}, bf16[17,32,128]{2,1,0:T(8,128)(2,1)S(1)}, u32[]{:S(2)}, u32[]{:S(2)}) collective-permute-start(bf16[17,32,128]{2,1,0:T(8,128)(2,1)S(1)} %get-tuple-element.28.own_ref), channel_id=1, source_target_pairs={{0,2},{1,9},{2,0},{3,11},{4,6},{5,13},{6,4},{7,15},{8,16},{9,1},{1... | collective-permute-start | bytes 417800 | tf_op jit(solution)/shard_map/ppermute | solution.py:565
  9.9 3.1 %collective-permute-start.2 = (bf16[33,8,128]{2,1,0:T(8,128)(2,1)S(1)}, bf16[33,8,128]{2,1,0:T(8,128)(2,1)S(1)}, u32[]{:S(2)}, u32[]{:S(2)}) collective-permute-start(bf16[33,8,128]{2,1,0:T(8,128)(2,1)S(1)} %get-tuple-element.36), channel_id=1, source_target_pairs={{0,1},{1,0},{2,3},{3,2},{4,5},{5,4},{6,7},{7,6},{8,9},{9,8},{10,11... | collective-permute-start | bytes 202760 | tf_op jit(solution)/shard_map/ppermute | solution.py:565
  10.0 5.1 %collective-permute-start.3 = (bf16[33,8,128]{2,1,0:T(8,128)(2,1)S(1)}, bf16[33,8,128]{2,1,0:T(8,128)(2,1)S(1)}, u32[]{:S(2)}, u32[]{:S(2)}) collective-permute-start(bf16[33,8,128]{2,1,0:T(8,128)(2,1)S(1)} %get-tuple-element.43), channel_id=1, source_target_pairs={{0,8},{1,2},{2,1},{3,4},{4,3},{5,6},{6,5},{7,15},{8,0},{9,10},{10,... | collective-permute-start | bytes 202760 | tf_op jit(solution)/shard_map/ppermute | solution.py:565
  16.2 6.6 %collective-permute-start.4 = (s16[2,2,4,16,128]{4,3,2,1,0:T(8,128)(2,1)S(1)}, s16[2,2,4,16,128]{4,3,2,1,0:T(8,128)(2,1)S(1)}, u32[]{:S(2)}, u32[]{:S(2)}) collective-permute-start(s16[2,2,4,16,128]{4,3,2,1,0:T(8,128)(2,1)S(1)} %get-tuple-element.48), channel_id=1, source_target_pairs={{0,16},{8,24},{16,0},{24,8},{1,17},{9,25},{17,1},{25,9},{2,18},{10... | collective-permute-start | bytes 196616 | tf_op jit(solution)/shard_map/ppermute | solution.py:598
  22.9 4.3 %collective-permute-start.5 = (s16[2,2,4,16,128]{4,3,2,1,0:T(8,128)(2,1)S(1)}, s16[2,2,4,16,128]{4,3,2,1,0:T(8,128)(2,1)S(1)}, u32[]{:S(2)}, u32[]{:S(2)}) collective-permute-start(s16[2,2,4,16,128]{4,3,2,1,0:T(8,128)(2,1)S(1)} %shard_map.73), channel_id=1, source_target_pairs={{0,4},{1,5},{2,6},{3,7},{4,0},{5,1},{6,2},{7,3},{8,12},{9,13},{10,... | collective-permute-start | bytes 196616 | tf_op jit(solution)/shard_map/ppermute | solution.py:598
